TPU v7x, 32 devices: a whole 2x2x4 slice. The times are simulated.
32 devices in a mesh: lat: 8 (over z, x), lon: 4 (over y, core).
Axes of the slice: x: 2, y: 2, z: 4, core: 2. Of those that a mesh axis runs over, the one named last changes fastest.
Arguments:
- field: bfloat16 [69, 256, 2048], P(None, 'lat', 'lon'), may hold values from -6 to 6
- stem_weight: bfloat16 [1104, 512], replicated, may hold values from -0.1875 to 0.1875
- stem_bias: float32 [512], replicated, may hold values from -3 to 3
- token_gain: float32 [512], replicated, may hold values from 0.1 to 1.9
- kv_weight: bfloat16 [512, 1024], replicated, may hold values from -0.25 to 0.25
- latents: float32 [512, 512], replicated, may hold values from -6 to 6
- latent_gain: float32 [512], replicated, may hold values from 0.1 to 1.9
- query_weight: bfloat16 [512, 512], replicated, may hold values from -0.25 to 0.25
- head_gain: float32 [8], replicated, may hold values from 2 to 40
- out_weight: bfloat16 [512, 512], replicated, may hold values from -0.25 to 0.25
- out_gain: float32 [512], replicated, may hold values from 0.1 to 1.9
Outputs:
- tokens: bfloat16 [128, 1024, 512], P('lat', 'lon')
- latent_out: float32 [512, 512], replicated
All inputs are finite; a program needn't handle non-finite values.
Results may differ from a plain program's by a relative error of at most 0.015.
The roundings to bfloat16 on the way count: a program that leaves them out, or rounds other values in their place, can miss the bound.
Values may be sent and summed in bfloat16 or wider, within the bound.
No kernel may reach another device: no remote copies, remote signals or barrier semaphores. Data moves between devices by JAX's collectives and lax.ppermute only.
A program may use at most 512 MiB of HBM per device.

v0:
```python
import jax
import jax.numpy as jnp
from jax import lax
from jax.sharding import PartitionSpec as P

HEADS = 8
HD = 64
LAT = 512
BLK = 1024


def padded(block, sides, width, periodic):
    for axis, dim in sides:
        count = lax.axis_size(axis)
        forward = [(i, i + 1) for i in range(count - 1)]
        if periodic:
            forward.append((count - 1, 0))
        backward = [(target, source) for source, target in forward]
        low = lax.ppermute(
            lax.slice_in_dim(block, block.shape[dim] - width, None, axis=dim), axis, forward
        )
        high = lax.ppermute(lax.slice_in_dim(block, 0, width, axis=dim), axis, backward)
        block = jnp.concatenate([low, block, high], axis=dim)
    return block


def normalize(values):
    mean = jnp.mean(values, axis=-1, keepdims=True)
    centred = values - mean
    spread = jnp.mean(centred * centred, axis=-1, keepdims=True)
    return centred / jnp.sqrt(spread + 1e-05)


def rescale(accum, fold):
    rows = accum.shape[0]
    return (accum.reshape(rows, HEADS, HD) * jnp.transpose(fold)[:, :, None]).reshape(
        rows, HEADS * HD
    )


def shards(
    field,
    stem_weight,
    stem_bias,
    token_gain,
    kv_weight,
    latents,
    latent_gain,
    query_weight,
    head_gain,
    out_weight,
    out_gain,
):
    widened = padded(field, (("lon", 2),), 1, True)
    widened = padded(widened, (("lat", 1),), 1, False)
    width = stem_weight.shape[1]
    kernel = stem_weight.reshape(4, 4, field.shape[0], width)
    stem = lax.conv_general_dilated(
        widened[None],
        kernel,
        (2, 2),
        "VALID",
        dimension_numbers=("NCHW", "HWIO", "NHWC"),
        preferred_element_type=jnp.float32,
    )[0]
    tokens = (normalize(stem + stem_bias) * token_gain).astype(jnp.bfloat16)
    normed = (normalize(latents) * latent_gain).astype(jnp.bfloat16)
    query = jnp.dot(normed, query_weight, preferred_element_type=jnp.float32).astype(jnp.bfloat16)
    query_heads = query.reshape(LAT, HEADS, HD)
    factor = head_gain / jnp.sqrt(jnp.float32(HD))
    count = tokens.shape[0] * tokens.shape[1]
    blocks = tokens.reshape(count // BLK, BLK, width)

    def attend(carry, block):
        peak, total, accum = carry
        kv = jnp.dot(block, kv_weight, preferred_element_type=jnp.float32).astype(jnp.bfloat16)
        keys = kv[:, :width].reshape(BLK, HEADS, HD)
        values = kv[:, width:].reshape(BLK, HEADS, HD)
        scores = (
            jnp.einsum("ihd,thd->hit", query_heads, keys, preferred_element_type=jnp.float32)
            * factor[:, None, None]
        )
        newpeak = jnp.maximum(peak, jnp.max(scores, axis=-1))
        fold = jnp.exp(peak - newpeak)
        expo = jnp.exp(scores - newpeak[:, :, None])
        total = total * fold + jnp.sum(expo, axis=-1)
        part = jnp.einsum(
            "hit,thd->ihd", expo.astype(jnp.bfloat16), values, preferred_element_type=jnp.float32
        )
        accum = rescale(accum, fold) + part.reshape(LAT, width)
        return ((newpeak, total, accum), None)

    start = (
        jnp.full((HEADS, LAT), -1e30, jnp.float32),
        jnp.zeros((HEADS, LAT), jnp.float32),
        jnp.zeros((LAT, width), jnp.float32),
    )
    (peak, total, accum), unused = lax.scan(attend, start, blocks)
    overall = lax.pmax(peak, ("lat", "lon"))
    fold = jnp.exp(peak - overall)
    total, accum = lax.psum((total * fold, rescale(accum, fold)), ("lat", "lon"))
    attended = rescale(accum, 1.0 / total).astype(jnp.bfloat16)
    mixed = jnp.dot(attended, out_weight, preferred_element_type=jnp.float32)
    latent_out = normalize(mixed) * out_gain
    return (tokens, latent_out)


def solution(mesh):
    return jax.shard_map(
        shards,
        mesh=mesh,
        in_specs=(P(None, "lat", "lon"), P(), P(), P(), P(), P(), P(), P(), P(), P(), P()),
        out_specs=(P("lat", "lon", None), P()),
        check_vma=False,
    )
```

profile of v0, /device:TPU:0, one launch (start us, length us, event | category | flops | bytes accessed | tf_op | source)
XLA Modules:
  0.0 374.0 jit_solution(1993222412906148977)
XLA Ops:
  7.2 1.5 fusion.33
  8.7 0.7 copy.64
  9.5 2.5 collective-permute-start.1
  11.9 0.7 copy.63
  12.7 1.4 reduce_sum.65
  14.0 1.5 multiply_reduce_fusion.2
  15.5 2.0 convolution_convert_fusion.1
  17.6 4.3 %copy.50 = bf16[69,32,512]{2,0,1:T(8,128)(2,1)} copy(bf16[69,32,512]{2,1,0:T(8,128)(2,1)} %param.13) | data formatting | bytes 4521984 | tf_op args[0]
  21.9 0.4 copy.49
  22.2 0.4 copy.51
  22.6 1.7 pad_maximum_fusion.2
  24.3 3.4 collective-permute-start.2
  27.7 1.6 collective-permute-start.3
  29.4 2.2 reshape.88
  31.6 3.0 collective-permute-done.3
  34.7 4.3 %maximum_bitcast_fusion = bf16[69,34,1,514]{3,0,1,2:T(8,128)(2,1)S(1)} fusion(bf16[69,1,514]{2,0,1:T(8,128)(2,1)} %collective-permute-done.3, bf16[69,32,1]{2,0,1:T(8,128)(2,1)S(1)} %copy.51, bf16[69,32,512]{2,0,1:T(8,128)(2,1)} %copy.50, bf16[69,32,1]{2,0,1:T(8,128)(2,1)S(1)} %copy.49, bf16[69,1,514]{2,0,1:T(8,128)(2,1)S(1)} %collective-permute-done.2), kind=kLoop, calls=%fused_computation.32 | loop fusion | flops 12058440 | bytes 4823376 | tf_op jit(solution)/shard_map/broadcast_in_dim | solution.py:59
  39.0 2.0 pad
  40.9 8.9 %reshape.92 = bf16[69,34,1,8,66]{4,3,0,1,2:T(8,128)(2,1)} reshape(bf16[69,34,1,528]{3,0,1,2:T(8,128)(2,1)} %pad) | data formatting | bytes 4954752 | tf_op jit(solution)/shard_map/conv_general_dilated | solution.py:58
  49.8 8.3 %copy.53 = bf16[69,34,1,8,66]{0,3,4,1,2:T(8,128)(2,1)} copy(bf16[69,34,1,8,66]{4,3,0,1,2:T(8,128)(2,1)} %reshape.92) | data formatting | bytes 4954752 | tf_op jit(solution)/shard_map/conv_general_dilated | solution.py:58
  58.1 1.0 slice.28
  59.1 9.1 %broadcast_select_fusion = f32[16,8,33,512]{3,1,2,0:T(8,128)S(1)} fusion(pred[8,33]{0,1:T(8,128)(4,1)S(1)} %copy-done.8, bf16[4,4,69,512]{3,2,1,0:T(8,128)(2,1)S(1)} %copy-done.3, bf16[69,34,1,7,3]{0,3,4,1,2:T(8,128)(2,1)S(1)} %slice.28, bf16[69,34,1,8,66]{0,3,4,1,2:T(8,128)(2,1)} %copy.53), kind=kOutput, calls=%fused_computation.31 | convolution fusion | flops 4785147904 | bytes 12357420 | tf_op jit(solution)/shard_map/conv_general_dilated | solution.py:58
  68.3 5.0 %copy.54 = f32[16,8,33,512]{3,0,2,1:T(8,128)S(1)} copy(f32[16,8,33,512]{3,1,2,0:T(8,128)S(1)} %broadcast_select_fusion) | data formatting | bytes 17301504 | tf_op jit(solution)/shard_map/conv_general_dilated | solution.py:58
  73.3 3.3 copy-done.2
  76.6 0.7 fusion.12
  77.5 4.6 %multiply_reduce_fusion = f32[16,256]{0,1:T(8,128)S(1)} fusion(f32[16,256]{0,1:T(8,128)S(1)} %copy.56, f32[512]{0:T(512)S(1)} %copy-done.4, f32[16,1,264,512]{3,0,2,1:T(8,128)} %bitcast.92), kind=kLoop, calls=%fused_computation.22 | loop fusion | flops 8384512 | bytes 8423424 | tf_op jit(solution)/shard_map/reduce_sum | solution.py:30
  82.3 4.4 %slice.29 = f32[16,1,256,512]{3,0,2,1:T(8,128)S(1)} slice(f32[16,1,264,512]{3,0,2,1:T(8,128)} %bitcast.93), slice={[0:16], [0:1], [0:256], [0:512]} | slice | bytes 16777216 | tf_op jit(solution)/shard_map/conv_general_dilated | solution.py:58
  86.7 4.9 %copy.59 = f32[16,1,256,512]{3,2,0,1:T(8,128)S(1)} copy(f32[16,1,256,512]{3,0,2,1:T(8,128)S(1)} %slice.29) | data formatting | bytes 16777216 | tf_op jit(solution)/shard_map/conv_general_dilated | solution.py:58
  91.6 3.3 multiply_convert_fusion
  94.9 94.9 %while.15 = (s32[]{:T(128)}, f32[8,512]{1,0:T(8,128)S(1)}, f32[8,512]{1,0:T(8,128)S(1)}, f32[512,512]{0,1:T(8,128)S(1)}, bf16[4,1024,512]{2,1,0:T(8,128)(2,1)}, ...) while((s32[]{:T(128)}, f32[8,512]{1,0:T(8,128)S(1)}, ...), condition=%wide.region_7.8_spmd.clone, body=%wide.region_4.7_spmd.clone.sunk | while | flops 2182897664 | bytes 132907248 | solution.py:98
  95.1 2.8 convolution_convert_fusion.3
  97.9 0.2 fusion.60
  98.1 3.0 bitcast_reduce_fusion.2
  101.1 5.7 %copy-done.1 = f32[8,1024,512]{2,1,0:T(8,128)} copy-done((f32[8,1024,512]{2,1,0:T(8,128)}, f32[8,1024,512]{2,1,0:T(8,128)S(1)}, u32[]{:S(2)}) %copy-start.1) | copy-done | bytes 16777240 | tf_op jit(solution)/shard_map/while
  106.8 3.0 fusion.64
  109.8 8.6 %fusion.62 = f32[8,512]{1,0:T(8,128)S(1)} fusion(f32[8,1024,512]{2,1,0:T(8,128)} %copy-done.1, f32[8,512]{1,0:T(8,128)S(1)} %get-tuple-element.198, f32[8]{0:T(128)S(1)} %get-tuple-element.204), kind=kLoop, calls=%fused_computation.4.clone.1 | loop fusion | flops 12578816 | bytes 16810016 | tf_op jit(solution)/shard_map/while/body/eval_jaxpr/reduce_sum | solution.py:86
  118.4 0.3 bitcast_add_fusion.3
  118.8 2.8 convolution_convert_fusion.3
  121.8 3.0 bitcast_reduce_fusion.2
  124.8 5.7 %copy-done.1 = f32[8,1024,512]{2,1,0:T(8,128)} copy-done((f32[8,1024,512]{2,1,0:T(8,128)}, f32[8,1024,512]{2,1,0:T(8,128)S(1)}, u32[]{:S(2)}) %copy-start.1) | copy-done | bytes 16777240 | tf_op jit(solution)/shard_map/while
  130.5 3.0 fusion.64
  133.5 8.6 %fusion.62 = f32[8,512]{1,0:T(8,128)S(1)} fusion(f32[8,1024,512]{2,1,0:T(8,128)} %copy-done.1, f32[8,512]{1,0:T(8,128)S(1)} %get-tuple-element.198, f32[8]{0:T(128)S(1)} %get-tuple-element.204), kind=kLoop, calls=%fused_computation.4.clone.1 | loop fusion | flops 12578816 | bytes 16810016 | tf_op jit(solution)/shard_map/while/body/eval_jaxpr/reduce_sum | solution.py:86
  142.0 0.3 bitcast_add_fusion.3
  142.4 2.8 convolution_convert_fusion.3
  145.5 3.0 bitcast_reduce_fusion.2
  148.5 5.7 %copy-done.1 = f32[8,1024,512]{2,1,0:T(8,128)} copy-done((f32[8,1024,512]{2,1,0:T(8,128)}, f32[8,1024,512]{2,1,0:T(8,128)S(1)}, u32[]{:S(2)}) %copy-start.1) | copy-done | bytes 16777240 | tf_op jit(solution)/shard_map/while
  154.2 3.0 fusion.64
  157.2 8.6 %fusion.62 = f32[8,512]{1,0:T(8,128)S(1)} fusion(f32[8,1024,512]{2,1,0:T(8,128)} %copy-done.1, f32[8,512]{1,0:T(8,128)S(1)} %get-tuple-element.198, f32[8]{0:T(128)S(1)} %get-tuple-element.204), kind=kLoop, calls=%fused_computation.4.clone.1 | loop fusion | flops 12578816 | bytes 16810016 | tf_op jit(solution)/shard_map/while/body/eval_jaxpr/reduce_sum | solution.py:86
  165.7 0.3 bitcast_add_fusion.3
  166.1 2.8 convolution_convert_fusion.3
  169.1 3.0 bitcast_reduce_fusion.2
  172.2 5.7 %copy-done.1 = f32[8,1024,512]{2,1,0:T(8,128)} copy-done((f32[8,1024,512]{2,1,0:T(8,128)}, f32[8,1024,512]{2,1,0:T(8,128)S(1)}, u32[]{:S(2)}) %copy-start.1) | copy-done | bytes 16777240 | tf_op jit(solution)/shard_map/while
  177.8 3.0 fusion.64
  180.8 8.6 %fusion.62 = f32[8,512]{1,0:T(8,128)S(1)} fusion(f32[8,1024,512]{2,1,0:T(8,128)} %copy-done.1, f32[8,512]{1,0:T(8,128)S(1)} %get-tuple-element.198, f32[8]{0:T(128)S(1)} %get-tuple-element.204), kind=kLoop, calls=%fused_computation.4.clone.1 | loop fusion | flops 12578816 | bytes 16810016 | tf_op jit(solution)/shard_map/while/body/eval_jaxpr/reduce_sum | solution.py:86
  189.4 0.3 bitcast_add_fusion.3
  189.8 41.7 %pmax.7 = f32[8,512]{1,0:T(8,128)S(1)} all-reduce(f32[8,512]{1,0:T(8,128)S(1)} %get-tuple-element.47), channel_id=1, replica_groups=mesh['lat'=8,'lon'=4] {'lat','lon'}, use_global_device_ids=true, to_apply=%region_8.9 | all-reduce | flops 4096 | bytes 32768 | tf_op jit(solution)/shard_map/pmax | solution.py:99
  231.5 1.1 bitcast_multiply_fusion.2
  232.6 5.5 %multiply_convert_fusion.1 = bf16[16,256,512]{2,0,1:T(8,128)(2,1)S(1)} fusion(f32[512]{0:T(512)S(1)} %copy-done.5, f32[16,256]{0,1:T(8,128)S(1)} %copy.58, f32[16,256]{0,1:T(8,128)S(1)} %copy.56, f32[512]{0:T(512)S(1)} %copy-done.4, f32[16,1,264,512]{3,0,2,1:T(8,128)} %bitcast.94), kind=kLoop, calls=%fused_computation.21 | loop fusion | flops 10485760 | bytes 12619776 | tf_op jit(solution)/shard_map/convert_element_type | solution.py:66
  238.2 4.4 %copy.60 = bf16[16,256,512]{2,1,0:T(8,128)(2,1)} copy(bf16[16,256,512]{2,0,1:T(8,128)(2,1)S(1)} %multiply_convert_fusion.1) | data formatting | bytes 8388608
  242.6 39.1 %psum.15 = f32[8,512]{1,0:T(8,128)S(1)} all-reduce(f32[8,512]{1,0:T(8,128)S(1)} %get-tuple-element.112), channel_id=1, replica_groups=mesh['lat'=8,'lon'=4] {'lat','lon'}, use_global_device_ids=true, to_apply=%region_10.11 | all-reduce | flops 4096 | bytes 32768 | tf_op jit(solution)/shard_map/psum | solution.py:101
  281.7 81.6 %all-reduce.2.cloned.1.call-done = f32[512,512]{0,1:T(8,128)} async-done(((f32[512,512]{0,1:T(8,128)}), f32[512,512]{0,1:T(8,128)}) %all-reduce.2.cloned.1.call-update) | async-done | bytes 1048592 | tf_op jit(solution)/shard_map/psum | solution.py:101
  363.3 1.4 fusion.23
  364.7 0.5 fusion.34
  365.2 0.2 multiply_reduce_fusion.1
  365.5 1.3 copy.61
  (59 shorter events, 1.4 us)
Async XLA Ops:
  7.2 357.5 %copy-start = (bf16[512,512]{1,0:T(8,128)(2,1)S(1)}, bf16[512,512]{1,0:T(8,128)(2,1)}, u32[]{:S(2)}) copy-start(bf16[512,512]{1,0:T(8,128)(2,1)} %param.22) | copy-start | bytes 1572868
  7.2 356.1 %all-reduce.2.cloned.1.call-start = ((), (), s32[]{:S(2)}) async-start(), calls=%async_computation | async-start | bytes 2097152 | tf_op jit(solution)/shard_map/psum | solution.py:101
  9.5 12.8 %collective-permute-start.1 = (bf16[69,32,1]{0,1,2:T(8,128)(2,1)S(1)}, bf16[69,32,1]{0,1,2:T(8,128)(2,1)S(1)}, u32[]{:S(2)}, u32[]{:S(2)}) collective-permute-start(bf16[69,32,1]{0,1,2:T(8,128)(2,1)S(1)} %copy.64), channel_id=1, source_target_pairs={{1,0},{2,1},{3,2},{0,3},{5,4},{6,5},{7,6},{4,7},{9,8},{10,9},{11,1... | collective-permute-start | bytes 13256 | tf_op jit(solution)/shard_map/ppermute | solution.py:22
  12.6 16.7 %copy-start.7 = (f32[8]{0:T(128)S(1)}, f32[8]{0:T(128)}, u32[]{:S(2)}) copy-start(f32[8]{0:T(128)} %param.21) | copy-start | bytes 100
  12.6 9.2 %collective-permute-start = (bf16[69,32,1]{0,1,2:T(8,128)(2,1)S(1)}, bf16[69,32,1]{0,1,2:T(8,128)(2,1)S(1)}, u32[]{:S(2)}, u32[]{:S(2)}) collective-permute-start(bf16[69,32,1]{0,1,2:T(8,128)(2,1)S(1)} %copy.63), channel_id=1, source_target_pairs={{0,1},{1,2},{2,3},{3,0},{4,5},{5,6},{6,7},{7,4},{8,9},{9,10},{10,1... | collective-permute-start | bytes 13256 | tf_op jit(solution)/shard_map/ppermute | solution.py:19
  24.3 7.3 %collective-permute-start.2 = (bf16[69,1,514]{2,0,1:T(8,128)(2,1)}, bf16[69,1,514]{2,0,1:T(8,128)(2,1)S(1)}, u32[]{:S(2)}, u32[]{:S(2)}) collective-permute-start(bf16[69,1,514]{2,0,1:T(8,128)(2,1)} %get-tuple-element.108), channel_id=1, source_target_pairs={{0,4},{4,8},{8,12},{12,16},{16,20},{20,24},{24,28},{1,5},{5,9},{9,... | collective-permute-start | bytes 212804 | tf_op jit(solution)/shard_map/ppermute | solution.py:19
  27.7 7.0 %collective-permute-start.3 = (bf16[69,1,514]{2,0,1:T(8,128)(2,1)S(1)}, bf16[69,1,514]{2,0,1:T(8,128)(2,1)}, u32[]{:S(2)}, u32[]{:S(2)}) collective-permute-start(bf16[69,1,514]{2,0,1:T(8,128)(2,1)S(1)} %get-tuple-element.109), channel_id=1, source_target_pairs={{4,0},{8,4},{12,8},{16,12},{20,16},{24,20},{28,24},{5,1},{9,5},{13... | collective-permute-start | bytes 212804 | tf_op jit(solution)/shard_map/ppermute | solution.py:22
  40.9 18.2 %copy-start.3 = (bf16[4,4,69,512]{3,2,1,0:T(8,128)(2,1)S(1)}, bf16[4,4,69,512]{3,2,1,0:T(8,128)(2,1)}, u32[]{:S(2)}) copy-start(bf16[4,4,69,512]{3,2,1,0:T(8,128)(2,1)} %reshape.88) | copy-start | bytes 3391492
  40.9 18.2 %copy-start.8 = (pred[8,33]{0,1:T(8,128)(4,1)S(1)}, pred[8,33]{0,1:T(8,128)(4,1)}, u32[]{:S(2)}) copy-start(pred[8,33]{0,1:T(8,128)(4,1)} %constant.40) | copy-start | bytes 796
  68.3 8.3 %copy-start.4 = (f32[512]{0:T(512)S(1)}, f32[512]{0:T(512)}, u32[]{:S(2)}) copy-start(f32[512]{0:T(512)} %param.15) | copy-start | bytes 6148
  73.3 3.3 copy-start.2
  86.7 4.9 %copy-start.5 = (f32[512]{0:T(512)S(1)}, f32[512]{0:T(512)}, u32[]{:S(2)}) copy-start(f32[512]{0:T(512)} %param.16) | copy-start | bytes 6148
  101.1 5.7 %copy-start.1 = (f32[8,1024,512]{2,1,0:T(8,128)}, f32[8,1024,512]{2,1,0:T(8,128)S(1)}, u32[]{:S(2)}) copy-start(f32[8,1024,512]{2,1,0:T(8,128)S(1)} %get-tuple-element.174) | copy-start | bytes 50331652 | tf_op jit(solution)/shard_map/while
  124.8 5.7 %copy-start.1 = (f32[8,1024,512]{2,1,0:T(8,128)}, f32[8,1024,512]{2,1,0:T(8,128)S(1)}, u32[]{:S(2)}) copy-start(f32[8,1024,512]{2,1,0:T(8,128)S(1)} %get-tuple-element.174) | copy-start | bytes 50331652 | tf_op jit(solution)/shard_map/while
  148.4 5.7 %copy-start.1 = (f32[8,1024,512]{2,1,0:T(8,128)}, f32[8,1024,512]{2,1,0:T(8,128)S(1)}, u32[]{:S(2)}) copy-start(f32[8,1024,512]{2,1,0:T(8,128)S(1)} %get-tuple-element.174) | copy-start | bytes 50331652 | tf_op jit(solution)/shard_map/while
  172.1 5.7 %copy-start.1 = (f32[8,1024,512]{2,1,0:T(8,128)}, f32[8,1024,512]{2,1,0:T(8,128)S(1)}, u32[]{:S(2)}) copy-start(f32[8,1024,512]{2,1,0:T(8,128)S(1)} %get-tuple-element.174) | copy-start | bytes 50331652 | tf_op jit(solution)/shard_map/while
  238.1 127.2 %copy-start.6 = (f32[512]{0:T(512)S(1)}, f32[512]{0:T(512)}, u32[]{:S(2)}) copy-start(f32[512]{0:T(512)} %param.23) | copy-start | bytes 6148
Sparse Core Ops, SparseCore 0:
  232.8 130.4 all-reduce.1
where the time goes:
time: 379 us; the launch traced here: 374 us
  waiting for transfers between devices  84.7 us (22%)
  blocking collectives  80.9 us (21%)
  local copies, waits for them, and re-layouts  77.5 us (20%)
  other arithmetic  61.5 us (16%)
  matrix products  46.8 us (12%)
  between operations  14.6 us (4%)
  starting transfers between devices  7.54 us (2%)
    psum x1, waiting for transfers between devices, shards(): lax.psum((total * fold, rescale(accum, fold)), ('lat', 'lon'))  81.6 us
    pmax x1, blocking collectives, shards(): overall = lax.pmax(peak, ('lat', 'lon'))  41.7 us
    psum x1, blocking collectives, shards(): lax.psum((total * fold, rescale(accum, fold)), ('lat', 'lon'))  39.1 us
    reduce_sum x4, other arithmetic, attend(): total = total * fold + jnp.sum(expo, axis=-1)  34.3 us
    conv_general_dilated x6, local copies, waits for them, and re-layouts, shards(): lax.conv_general_dilated(widened[None], kernel, (2, 2), 'VALID', dimensio...  32.5 us
    while x12, local copies, waits for them, and re-layouts  22.8 us
    unnamed x21, local copies, waits for them, and re-layouts  14.8 us
    dot_general x4, matrix products, attend(): jnp.einsum('hit,thd->ihd', expo.astype(jnp.bfloat16), values, preferred_e...  12 us
  transfers between devices with their start and end apart: 5, of which 2 were waited for; matrix products, arithmetic and copies ran while one was open for 6% of the time, Pallas kernels for 0%

commit v1 on v0

v1 whole, which is shorter than its diff:
```python
import functools

import jax
import jax.numpy as jnp
from jax import lax
from jax.experimental import pallas as pl
from jax.experimental.pallas import tpu as pltpu
from jax.sharding import PartitionSpec as P

HEADS = 8
HD = 64
CP = 80
HR = 80
CT = 1024
VMEM = pltpu.VMEM
bf16 = jnp.bfloat16
f32 = jnp.float32
LOG2E = 1.4426950408889634


def call(kernel, out, n_in, scratch=(), smem=0, out_spaces=None):
    outs = out if isinstance(out, (list, tuple)) else [out]
    spaces = out_spaces or [VMEM] * len(outs)
    specs = [pl.BlockSpec(memory_space=s) for s in spaces]
    return pl.pallas_call(
        kernel,
        out_shape=out,
        in_specs=[pl.BlockSpec(memory_space=pltpu.SMEM)] * smem
        + [pl.BlockSpec(memory_space=VMEM)] * n_in,
        out_specs=specs if isinstance(out, (list, tuple)) else specs[0],
        scratch_shapes=list(scratch),
        compiler_params=pltpu.CompilerParams(vmem_limit_bytes=60 << 20),
    )


def shape(dims, dtype):
    return jax.ShapeDtypeStruct(tuple(dims), dtype)


def rows_norm(x, axis):
    mean = jnp.mean(x, axis=axis, keepdims=True)
    centred = x - mean
    spread = jnp.mean(centred * centred, axis=axis, keepdims=True)
    return centred * lax.rsqrt(spread + 1e-05)


def split3(x):
    hi = x.astype(bf16)
    rest = x - hi.astype(f32)
    mid = rest.astype(bf16)
    lo = (rest - mid.astype(f32)).astype(bf16)
    return hi, mid, lo


def query_kernel(gain_ref, latents_ref, lgain_ref, qw_ref, qz_ref):
    normed = (rows_norm(latents_ref[...], 1) * lgain_ref[...]).astype(bf16)
    query = jnp.dot(normed, qw_ref[...], preferred_element_type=f32).astype(bf16)
    qt = jnp.transpose(query.astype(f32))
    zero = jnp.zeros((HD, qt.shape[1]), bf16)
    for h in range(HEADS):
        scaled = qt[h * HD : (h + 1) * HD] * (gain_ref[h] * (LOG2E / HD**0.5))
        hi = scaled.astype(bf16)
        lo = (scaled - hi.astype(f32)).astype(bf16)
        parts = [hi, zero, lo, zero] if h % 2 == 0 else [zero, hi, zero, lo]
        for j, part in enumerate(parts):
            qz_ref[h, j * HD : (j + 1) * HD, :] = part


def encode_kernel(
    place_ref,
    x_ref, hl_ref, hr_ref, top_ref, bot_ref, wt_ref, bias_ref, gain_ref, wk_ref, wvt_ref, qz_ref,
    tok_out, keep_ref, send_ref,
    y_ref, xs_ref, st_ref, tok_ref, k_ref, vt_ref, s_ref, sems,
):
    chan, rows, cols = x_ref.shape
    half = cols // 2
    trows = rows // 2
    width = wk_ref.shape[0]
    tokens = trows * half
    lat = qz_ref.shape[2]

    i = lax.broadcasted_iota(jnp.int32, (256, 256), 0)
    j = lax.broadcasted_iota(jnp.int32, (256, 256), 1)
    perm = jnp.where(((i >> 4) == (j & 15)) & ((i & 15) == (j >> 4)), 1.0, 0.0).astype(bf16)
    for g in range(CP // 16):
        n = min(16, chan - 16 * g)
        for b in range(rows // 16):
            x = x_ref[16 * g : 16 * g + n, 16 * b : 16 * b + 16, :].reshape(n * 16, cols)
            y = jnp.dot(perm[:, : n * 16], x, preferred_element_type=f32).astype(bf16)
            y_ref[1 + 16 * b : 17 + 16 * b, 16 * g : 16 * g + 16, :] = y.reshape(16, 16, cols)
    y_ref[0] = top_ref[:, :cols]
    y_ref[rows + 1] = bot_ref[:, :cols]

    ci = lax.broadcasted_iota(jnp.int32, (cols, cols), 0)
    cj = lax.broadcasted_iota(jnp.int32, (cols, cols), 1)
    want = jnp.where(cj < half, 2 * cj, 2 * (cj - half) + 1)
    select = jnp.where(ci == want, 1.0, 0.0).astype(bf16)
    lane = lax.broadcasted_iota(jnp.int32, (CP, half), 1)
    left_all = hl_ref[...].astype(f32)
    right_all = hr_ref[...].astype(f32)
    edges = [top_ref[:, cols:].astype(f32), bot_ref[:, cols:].astype(f32)]
    for p in range((rows + 2) // 2):
        pair = y_ref[2 * p : 2 * p + 2].reshape(2 * CP, cols)
        sel = jnp.dot(pair, select, preferred_element_type=f32)
        for q in range(2):
            r = 2 * p + q
            if r == 0 or r == rows + 1:
                e = edges[0 if r == 0 else 1]
                left, right = e[:, 0:1], e[:, 1:2]
            else:
                left, right = left_all[:, r - 1 : r], right_all[:, r - 1 : r]
            even = sel[q * CP : (q + 1) * CP, :half]
            odd = sel[q * CP : (q + 1) * CP, half:]
            first = jnp.where(lane == 0, left, pltpu.roll(odd, 1, 1))
            last = jnp.where(lane == half - 1, right, pltpu.roll(even, half - 1, 1))
            for kx, v in enumerate((first, even, odd, last)):
                xs_ref[r, kx * CP : (kx + 1) * CP, :] = v.astype(bf16)

    for h in range(HEADS):
        vt_ref[h * HR + HD : (h + 1) * HR, :] = jnp.ones((HR - HD, tokens), bf16)

    def stem(r, slot):
        patch = xs_ref[pl.ds(2 * r, 4)].reshape(16 * CP, half)
        st_ref[slot] = jnp.dot(wt_ref[...], patch, preferred_element_type=f32)

    def finish(r, slot):
        value = rows_norm(st_ref[slot] + bias_ref[...], 0) * gain_ref[...]
        tt = value.astype(bf16)
        tok = jnp.transpose(tt)
        tok_ref[r] = tok
        pltpu.make_async_copy(tok_ref.at[r], tok_out.at[r], sems.at[r]).start()
        at = pl.ds(pl.multiple_of(r * half, half), half)
        k_ref[at, :] = jnp.dot(tok, wk_ref[...], preferred_element_type=f32).astype(bf16)
        vt = jnp.dot(wvt_ref[...], tt, preferred_element_type=f32).astype(bf16)
        for h in range(HEADS):
            vt_ref[h * HR : h * HR + HD, at] = vt[h * HD : (h + 1) * HD]

    stem(0, 0)

    def band(n, carry):
        r = 2 * n
        stem(r + 1, 1)
        finish(r, 0)
        stem(jnp.minimum(r + 2, trows - 1), 0)
        finish(r + 1, 1)
        return carry

    lax.fori_loop(0, trows // 2, band, 0)

    def produce(h, c, slot):
        pair = pl.ds(pl.multiple_of((h >> 1) * (2 * HD), 2 * HD), 2 * HD)
        keys = k_ref[c * CT : (c + 1) * CT, pair]
        keys = jnp.concatenate([keys, keys], axis=1)
        s = jnp.dot(keys, qz_ref[h], preferred_element_type=f32)
        s_ref[slot] = s
        return jnp.max(s, axis=0, keepdims=True)

    chunks = tokens // CT

    def head_of(t):
        return (t & (HEADS // 2 - 1)) ^ place_ref[t >> (HEADS.bit_length() - 2)]

    def head(t, most):
        h = head_of(t)
        after = head_of(jnp.minimum(t + 1, HEADS - 1))
        peak = jnp.full((1, lat), -1e30, f32)
        state = jnp.zeros((HR, lat), f32)
        for c in range(chunks):
            if c + 1 < chunks:
                following = produce(h, c + 1, (c + 1) % 2)
            else:
                following = produce(after, 0, (c + 1) % 2)
            newpeak = jnp.maximum(peak, jnp.ceil(most))
            fold = jnp.exp2(peak - newpeak)
            weights = jnp.exp2(s_ref[c % 2] - newpeak).astype(bf16)
            values = vt_ref[pl.ds(pl.multiple_of(h * HR, 16), HR), c * CT : (c + 1) * CT]
            state = state * fold + jnp.dot(values, weights, preferred_element_type=f32)
            peak, most = newpeak, following
        total = state[HD : HD + 1]
        packed = pack(state[:HD], total, peak)

        @pl.when(t < HEADS // 2)
        def _():
            keep_ref[jnp.minimum(t, HEADS // 2 - 1)] = packed

        @pl.when(t >= HEADS // 2)
        def _():
            send_ref[jnp.maximum(t - HEADS // 2, 0)] = packed

        return most

    lax.fori_loop(0, HEADS, head, produce(head_of(0), 0, 0))
    for r in range(trows):
        pltpu.make_async_copy(tok_ref.at[r], tok_out.at[r], sems.at[r]).wait()


def pack(sums, total, peak):
    lat = sums.shape[1]
    row = lax.broadcasted_iota(jnp.int32, (16, lat), 0)
    tail = jnp.zeros((16, lat), f32)
    for n, part in enumerate(split3(total) + split3(peak)):
        tail = jnp.where(row == n, part.astype(f32), tail)
    return jnp.concatenate([sums.astype(bf16), tail.astype(bf16)], axis=0)


def unpack(state):
    tail = state[HD:].astype(f32)
    total = (tail[0:1] + tail[1:2]) + tail[2:3]
    peak = (tail[3:4] + tail[4:5]) + tail[5:6]
    return state[:HD].astype(f32), total, peak


def combined(a, b):
    sums_a, total_a, peak_a = unpack(a)
    sums_b, total_b, peak_b = unpack(b)
    peak = jnp.maximum(peak_a, peak_b)
    fold_a = jnp.exp2(peak_a - peak)
    fold_b = jnp.exp2(peak_b - peak)
    return sums_a * fold_a + sums_b * fold_b, total_a * fold_a + total_b * fold_b, peak


def fold_kernel(a_ref, b_ref, *outs):
    per = a_ref.shape[0] // len(outs)
    for n in range(a_ref.shape[0]):
        outs[n // per][n % per] = pack(*combined(a_ref[n], b_ref[n]))


def attended_kernel(a_ref, b_ref, out_ref):
    sums, total, peak = combined(a_ref[0], b_ref[0])
    out_ref[0] = (sums / total).astype(bf16)


def out_kernel(place_ref, a_ref, b_ref, wo_ref, gain_ref, out_ref, all_ref):
    half = HEADS // 2
    for t in range(HEADS):
        value = a_ref[t] if t < half else b_ref[t - half]
        h = (t % half) ^ place_ref[t // half]
        all_ref[pl.ds(pl.multiple_of(h * HD, HD), HD), :] = value.astype(f32)
    attended = jnp.transpose(all_ref[...]).astype(bf16)
    mixed = jnp.dot(attended, wo_ref[...], preferred_element_type=f32)
    out_ref[...] = rows_norm(mixed, 1) * gain_ref[...]


def shards(
    field, stem_weight, stem_bias, token_gain, kv_weight, latents,
    latent_gain, query_weight, head_gain, out_weight, out_gain,
):
    chan, rows, cols = field.shape
    width = stem_weight.shape[1]
    lat = latents.shape[0]
    nlat = lax.axis_size("lat")
    nlon = lax.axis_size("lon")
    half = cols // 2
    trows = rows // 2

    extra = ((0, CP - chan), (0, 0))
    ahead = [(i, (i + 1) % nlon) for i in range(nlon)]
    back = [(t, s) for s, t in ahead]
    hl = lax.ppermute(jnp.pad(field[:, :, cols - 1], extra), "lon", ahead)
    hr = lax.ppermute(jnp.pad(field[:, :, 0], extra), "lon", back)

    def edge(r):
        return jnp.concatenate([jnp.pad(field[:, r, :], extra), hl[:, r : r + 1], hr[:, r : r + 1]], 1)

    up = [(i, i + 1) for i in range(nlat - 1)]
    down = [(t, s) for s, t in up]
    top = lax.ppermute(edge(rows - 1), "lat", up)
    bot = lax.ppermute(edge(0), "lat", down)

    wt = stem_weight.reshape(16, chan, width)
    wt = jnp.pad(wt, ((0, 0), (0, CP - chan), (0, 0))).reshape(16 * CP, width).T
    wk = kv_weight[:, :width]
    wvt = kv_weight[:, width:].T
    qz = call(query_kernel, shape((HEADS, 4 * HD, lat), bf16), 3, smem=1)(
        head_gain, latents, latent_gain[None, :], query_weight
    )

    core = lax.axis_index("lon") & 1
    by = (lax.axis_index("lon") >> 1) & 1
    bx = lax.axis_index("lat") & 1
    yx, xy = 2 * by + bx, 2 * bx + by
    mine = 4 * core + jnp.where(core == 0, yx, xy)
    other = 4 * (1 - core) + jnp.where(core == 0, xy, yx)
    place = jnp.stack([mine, other]).astype(jnp.int32)

    tokens = trows * half
    state = shape((HEADS // 2, HR, lat), bf16)
    tok, keep, send = call(
        encode_kernel,
        [shape((trows, half, width), bf16), state, state],
        11,
        smem=1,
        out_spaces=[pl.ANY, VMEM, VMEM],
        scratch=[
            VMEM((rows + 2, CP, cols), bf16),
            VMEM((rows + 2, 4 * CP, half), bf16),
            VMEM((2, width, half), f32),
            VMEM((trows, half, width), bf16),
            VMEM((tokens, width), bf16),
            VMEM((HEADS * HR, tokens), bf16),
            VMEM((2, CT, lat), f32),
            pltpu.SemaphoreType.DMA((trows,)),
        ],
    )(place, field, hl, hr, top, bot, wt, stem_bias[:, None], token_gain[:, None], wk, wvt, qz)

    def swap(x, flip0, flip1):
        pairs = []
        for a in range(nlat):
            for b in range(nlon):
                axis, bit = flip1 if b & 1 else flip0
                to = (a ^ bit, b) if axis == "lat" else (a, b ^ bit)
                pairs.append((a * nlon + b, to[0] * nlon + to[1]))
        return lax.ppermute(x, ("lat", "lon"), pairs)

    cores = ("lon", 1)
    first, second = ("lon", 2), ("lat", 1)
    rest = [("lat", 1 << n) for n in range(1, nlat.bit_length() - 1)]
    rest += [("lon", 1 << n) for n in range(2, nlon.bit_length() - 1)]

    two = shape((HEADS // 4, HR, lat), bf16)
    one = shape((HEADS // 8, HR, lat), bf16)
    keep, send = call(fold_kernel, [two, two], 2)(keep, swap(send, cores, cores))
    keep, send = call(fold_kernel, [one, one], 2)(keep, swap(send, first, second))
    (mine,) = call(fold_kernel, [one], 2)(keep, swap(send, second, first))
    for n in range(len(rest) - 1):
        (mine,) = call(fold_kernel, [one], 2)(mine, swap(mine, rest[n], rest[(n + 1) % len(rest)]))
    part = call(attended_kernel, shape((1, HD, lat), bf16), 2)(mine, swap(mine, rest[-1], rest[0]))
    part = jnp.concatenate([part, swap(part, second, first)])
    part = jnp.concatenate([part, swap(part, first, second)])
    latent_out = call(
        out_kernel, shape((lat, width), f32), 4, smem=1, scratch=[VMEM((width, lat), f32)]
    )(place, part, swap(part, cores, cores), out_weight, out_gain[None, :])
    return (tok, latent_out)


def solution(mesh):
    return jax.shard_map(
        shards,
        mesh=mesh,
        in_specs=(P(None, "lat", "lon"), P(), P(), P(), P(), P(), P(), P(), P(), P(), P()),
        out_specs=(P("lat", "lon", None), P()),
        check_vma=False,
    )
```

time: 379 us -> 120 us (0.32); the launches traced: 374 us -> 119 us
  blocking collectives: 80.9 us -> 0 us
  local copies, waits for them, and re-layouts: 77.5 us -> 15.5 us
  other arithmetic: 61.5 us -> 2.55 us
  waiting for transfers between devices: 84.7 us -> 26.9 us
  Pallas kernels: 0 us -> 53.5 us
  matrix products: 46.8 us -> 0 us
  between operations: 14.6 us -> 0.82 us
  starting transfers between devices: 7.54 us -> 20 us
    psum x1 -> x0, waiting for transfers between devices: 81.6 us -> none  [shards(): lax.psum((total * fold, rescale(accum, fold)), ('lat', 'lon'))]
    pallas_call x0 -> x8, Pallas kernels: none -> 53.5 us  [the longest x1 38.4 us: shards(): call(encode_kernel, [shape((trows, half, width), bf16), state, state], 11...]
    reduce_sum x9 -> x0, other arithmetic: 42.6 us -> none  [the longest x4 34.3 us: attend(): total = total * fold + jnp.sum(expo, axis=-1)]
    pmax x1 -> x0, blocking collectives: 41.7 us -> none  [shards(): overall = lax.pmax(peak, ('lat', 'lon'))]
    psum x1 -> x0, blocking collectives: 39.1 us -> none  [shards(): lax.psum((total * fold, rescale(accum, fold)), ('lat', 'lon'))]
    dot_general x14 -> x0, matrix products: 37.7 us -> none  [the longest x4 12 us: attend(): jnp.einsum('hit,thd->ihd', expo.astype(jnp.bfloat16), values, preferred_e...]
    conv_general_dilated x6 -> x0, local copies, waits for them, and re-layouts: 32.5 us -> none  [shards(): lax.conv_general_dilated(widened[None], kernel, (2, 2), 'VALID', dimensio...]
    ppermute x4 -> x12, waiting for transfers between devices: 3.04 us -> 26.9 us  [the longest x8 22.5 us: swap(): return lax.ppermute(x, ('lat', 'lon'), pairs)]
  transfers between devices with their start and end apart: 5 -> 12, of which waited for: 2 -> 9; matrix products, arithmetic and copies ran while one was open for 6% -> 8% of each run, Pallas kernels for 0% -> 3%
where the time goes in v1:
time: 120 us; the launch traced here: 119 us
  Pallas kernels  53.5 us (45%)
  waiting for transfers between devices  26.9 us (22%)
  starting transfers between devices  20 us (17%)
  local copies, waits for them, and re-layouts  15.5 us (13%)
  other arithmetic  2.55 us (2%)
    pallas_call x1, Pallas kernels, shards(): call(encode_kernel, [shape((trows, half, width), bf16), state, state], 11...  38.4 us
    ppermute x8, waiting for transfers between devices, swap(): return lax.ppermute(x, ('lat', 'lon'), pairs)  22.5 us
    ppermute x8, starting transfers between devices, swap(): return lax.ppermute(x, ('lat', 'lon'), pairs)  11.9 us
    unnamed x33, local copies, waits for them, and re-layouts  6.71 us
    ppermute x1, waiting for transfers between devices, shards(): bot = lax.ppermute(edge(0), 'lat', down)  4.4 us
    ppermute x1, starting transfers between devices, shards(): top = lax.ppermute(edge(rows - 1), 'lat', up)  4.16 us
    pallas_call x1, Pallas kernels, shards(): call(query_kernel, shape((HEADS, 4 * HD, lat), bf16), 3, smem=1)  3.68 us
    pallas_call x1, Pallas kernels, shards(): call(out_kernel, shape((lat, width), f32), 4, smem=1, scratch=[VMEM((widt...  2.95 us
  transfers between devices with their start and end apart: 12, of which 9 were waited for; matrix products, arithmetic and copies ran while one was open for 8% of the time, Pallas kernels for 3%

profile of v1, /device:TPU:0, one launch (start us, length us, event | category | flops | bytes accessed | tf_op | source)
XLA Modules:
  0.0 119.3 jit_solution(4137637625631736490)
XLA Ops:
  0.6 0.0 copy-start
  0.6 1.6 %fusion.7 = (bf16[69,32,1]{2,1,0:T(8,128)(2,1)S(1)}, bf16[69,32,1]{2,1,0:T(8,128)(2,1)S(1)}) fusion(bf16[69,32,512]{2,1,0:T(8,128)(2,1)} %x_ref.1), kind=kLoop, calls=%fused_computation.13 | loop fusion | bytes 17664 | tf_op jit(solution)/shard_map/slice | solution.py:260
  2.2 0.0 copy-start.12
  2.2 0.0 copy-start.13
  2.2 0.5 copy.27
  2.8 0.5 collective-permute-start
  3.3 0.5 copy.28
  3.8 2.0 %collective-permute-start.1 = (bf16[80,32]{1,0:T(8,128)(2,1)S(1)}, bf16[80,32]{1,0:T(8,128)(2,1)S(1)}, u32[]{:S(2)}, u32[]{:S(2)}) collective-permute-start(bf16[80,32]{1,0:T(8,128)(2,1)S(1)} %pad.19), channel_id=1, source_target_pairs={{1,0},{2,1},{3,2},{0,3},{5,4},{6,5},{7,6},{4,7},{9,8},{10,9},{11,1... | collective-permute-start | bytes 15368 | tf_op jit(solution)/shard_map/ppermute | solution.py:260
  5.8 0.0 copy-done
  5.8 0.9 fusion.8
  6.7 1.5 %fusion.6 = (bf16[69,1,512]{2,1,0:T(2,128)(2,1)S(1)}, bf16[69,1,512]{2,1,0:T(2,128)(2,1)S(1)}) fusion(bf16[69,32,512]{2,1,0:T(8,128)(2,1)} %x_ref.1), kind=kLoop, calls=%fused_computation.12 | loop fusion | bytes 282624 | tf_op jit(solution)/shard_map/slice | solution.py:263
  8.2 0.0 copy-done.12
  8.2 0.8 copy.25.bias_ref
  9.0 0.0 copy-done.13
  9.0 0.9 copy.26.gain_ref
  10.0 1.0 copy.31
  11.0 1.4 %reshape.10 = bf16[16,69,512]{2,1,0:T(8,128)(2,1)S(1)} reshape(bf16[1104,512]{1,0:T(8,128)(2,1)} %param.12) | data formatting | bytes 2260992 | tf_op jit(solution)/shard_map/reshape | solution.py:270
  12.4 0.1 pad.22
  12.6 1.4 %copy.23 = bf16[1280,512]{0,1:T(8,128)(2,1)} copy(bf16[1280,512]{1,0:T(8,128)(2,1)S(1)} %bitcast.17) | data formatting | bytes 2621440 | tf_op jit(solution)/shard_map/reshape | solution.py:271
  14.0 3.7 %shard_map.122.qz_ref = bf16[8,256,512]{2,1,0:T(8,128)(2,1)} custom-call(f32[8]{0:T(128)} %gain_ref.1, f32[512,512]{1,0:T(8,128)} %latents_ref.1, f32[1,512]{1,0:T(1,128)} %bitcast.24, bf16[512,512]{1,0:T(8,128)(2,1)} %qw_ref.1), custom_call_target="tpu_custom_call" | custom-call | tf_op jit(solution)/shard_map/pallas_call | solution.py:274
  17.7 0.0 collective-permute-done.1.hr_ref
  17.7 0.1 fusion.10
  17.8 0.0 collective-permute-done.hl_ref
  17.8 0.1 fusion.9
  17.8 0.1 fusion.3
  17.9 4.2 %collective-permute-start.2 = (bf16[80,514]{1,0:T(8,128)(2,1)S(1)}, bf16[80,514]{1,0:T(8,128)(2,1)S(1)}, u32[]{:S(2)}, u32[]{:S(2)}) collective-permute-start(bf16[80,514]{1,0:T(8,128)(2,1)S(1)} %fusion.3), channel_id=1, source_target_pairs={{0,4},{4,8},{8,12},{12,16},{16,20},{20,24},{24,28},{1,5},{5,9},{9,... | collective-permute-start | bytes 246728 | tf_op jit(solution)/shard_map/ppermute | solution.py:267
  22.1 0.1 fusion.5
  22.2 1.5 %collective-permute-start.3 = (bf16[80,514]{1,0:T(8,128)(2,1)S(1)}, bf16[80,514]{1,0:T(8,128)(2,1)S(1)}, u32[]{:S(2)}, u32[]{:S(2)}) collective-permute-start(bf16[80,514]{1,0:T(8,128)(2,1)S(1)} %fusion.5), channel_id=1, source_target_pairs={{4,0},{8,4},{12,8},{16,12},{20,16},{24,20},{28,24},{5,1},{9,5},{13... | collective-permute-start | bytes 246728 | tf_op jit(solution)/shard_map/ppermute | solution.py:268
  23.7 0.7 pad_add_fusion.place_ref
  24.3 0.0 collective-permute-done.2.top_ref
  24.3 4.4 %collective-permute-done.3.bot_ref = bf16[80,514]{1,0:T(8,128)(2,1)S(1)} collective-permute-done((bf16[80,514]{1,0:T(8,128)(2,1)S(1)}, bf16[80,514]{1,0:T(8,128)(2,1)S(1)}, u32[]{:S(2)}, u32[]{:S(2)}) %collective-permute-start.3) | collective-permute-done | bytes 82272 | tf_op jit(solution)/shard_map/ppermute | solution.py:268
  28.7 0.6 copy-done.8
  29.4 38.4 %shard_map.123 = (bf16[16,256,512]{2,1,0:T(8,128)(2,1)}, bf16[4,80,512]{2,1,0:T(8,128)(2,1)}, bf16[4,80,512]{2,1,0:T(8,128)(2,1)}) custom-call(s32[2]{0:T(128)} %pad_add_fusion.place_ref, bf16[69,32,512]{2,1,0:T(8,128)(2,1)} %x_ref.1, bf16[80,32]{1,0:T(8,128)(2,1)} %copy-done.4, bf16[80,32]{1,0:T(8,128)(2,1)} %copy-done.5, bf16[80,514]{1,0:T(8,128)(2,1)} %copy-done.7, ...), custom_call_target="tpu_custom_call" | custom-call | tf_op jit(solution)/shard_map/pallas_call | solution.py:288
  67.7 0.1 collective-permute-start.4
  67.8 1.8 %collective-permute-done.4.b_ref = bf16[4,80,512]{2,1,0:T(8,128)(2,1)S(1)} collective-permute-done((bf16[4,80,512]{2,1,0:T(8,128)(2,1)}, bf16[4,80,512]{2,1,0:T(8,128)(2,1)S(1)}, u32[]{:S(2)}, u32[]{:S(2)}) %collective-permute-start.4) | collective-permute-done | bytes 327712 | tf_op jit(solution)/shard_map/ppermute | solution.py:313
  69.7 0.7 copy-done.2
  70.4 1.9 %shard_map.124 = (bf16[2,80,512]{2,1,0:T(8,128)(2,1)}, bf16[2,80,512]{2,1,0:T(8,128)(2,1)}) custom-call(bf16[4,80,512]{2,1,0:T(8,128)(2,1)} %get-tuple-element.10.a_ref, bf16[4,80,512]{2,1,0:T(8,128)(2,1)} %copy-done.2), custom_call_target="tpu_custom_call" | custom-call | tf_op jit(solution)/shard_map/pallas_call | solution.py:322
  72.3 1.5 %collective-permute-start.5 = (bf16[2,80,512]{2,1,0:T(8,128)(2,1)}, bf16[2,80,512]{2,1,0:T(8,128)(2,1)S(1)}, u32[]{:S(2)}, u32[]{:S(2)}) collective-permute-start(bf16[2,80,512]{2,1,0:T(8,128)(2,1)} %get-tuple-element.13), channel_id=1, source_target_pairs={{0,2},{1,5},{2,0},{3,7},{4,6},{5,1},{6,4},{7,3},{8,10},{9,13},{10,... | collective-permute-start | bytes 491528 | tf_op jit(solution)/shard_map/ppermute | solution.py:313
  73.8 4.0 %collective-permute-done.5.b_ref = bf16[2,80,512]{2,1,0:T(8,128)(2,1)S(1)} collective-permute-done((bf16[2,80,512]{2,1,0:T(8,128)(2,1)}, bf16[2,80,512]{2,1,0:T(8,128)(2,1)S(1)}, u32[]{:S(2)}, u32[]{:S(2)}) %collective-permute-start.5) | collective-permute-done | bytes 163872 | tf_op jit(solution)/shard_map/ppermute | solution.py:313
  77.8 0.7 copy-done.6
  78.5 1.7 %shard_map.125 = (bf16[1,80,512]{2,1,0:T(8,128)(2,1)}, bf16[1,80,512]{2,1,0:T(8,128)(2,1)}) custom-call(bf16[2,80,512]{2,1,0:T(8,128)(2,1)} %get-tuple-element.12.a_ref, bf16[2,80,512]{2,1,0:T(8,128)(2,1)} %copy-done.6), custom_call_target="tpu_custom_call" | custom-call | tf_op jit(solution)/shard_map/pallas_call | solution.py:323
  80.2 2.4 %collective-permute-start.6 = (bf16[1,80,512]{2,1,0:T(8,128)(2,1)}, bf16[1,80,512]{2,1,0:T(8,128)(2,1)S(1)}, u32[]{:S(2)}, u32[]{:S(2)}) collective-permute-start(bf16[1,80,512]{2,1,0:T(8,128)(2,1)} %get-tuple-element.15), channel_id=1, source_target_pairs={{0,4},{1,3},{2,6},{3,1},{4,0},{5,7},{6,2},{7,5},{8,12},{9,11},{10,... | collective-permute-start | bytes 245768 | tf_op jit(solution)/shard_map/ppermute | solution.py:313
  82.7 2.6 %collective-permute-done.6.b_ref = bf16[1,80,512]{2,1,0:T(8,128)(2,1)S(1)} collective-permute-done((bf16[1,80,512]{2,1,0:T(8,128)(2,1)}, bf16[1,80,512]{2,1,0:T(8,128)(2,1)S(1)}, u32[]{:S(2)}, u32[]{:S(2)}) %collective-permute-start.6) | collective-permute-done | bytes 81952 | tf_op jit(solution)/shard_map/ppermute | solution.py:313
  85.3 0.6 copy-done.10
  85.9 1.6 %shard_map.126.a_ref = bf16[1,80,512]{2,1,0:T(8,128)(2,1)} custom-call(bf16[1,80,512]{2,1,0:T(8,128)(2,1)} %get-tuple-element.14.a_ref, bf16[1,80,512]{2,1,0:T(8,128)(2,1)} %copy-done.10), custom_call_target="tpu_custom_call" | custom-call | tf_op jit(solution)/shard_map/pallas_call | solution.py:324
  87.6 1.6 %collective-permute-start.7 = (bf16[1,80,512]{2,1,0:T(8,128)(2,1)}, bf16[1,80,512]{2,1,0:T(8,128)(2,1)S(1)}, u32[]{:S(2)}, u32[]{:S(2)}) collective-permute-start(bf16[1,80,512]{2,1,0:T(8,128)(2,1)} %shard_map.126.a_ref), channel_id=1, source_target_pairs={{0,8},{1,17},{2,10},{3,19},{4,12},{5,21},{6,14},{7,23},{8,0},{9,25... | collective-permute-start | bytes 245768 | tf_op jit(solution)/shard_map/ppermute | solution.py:313
  89.1 3.1 %collective-permute-done.7.b_ref = bf16[1,80,512]{2,1,0:T(8,128)(2,1)S(1)} collective-permute-done((bf16[1,80,512]{2,1,0:T(8,128)(2,1)}, bf16[1,80,512]{2,1,0:T(8,128)(2,1)S(1)}, u32[]{:S(2)}, u32[]{:S(2)}) %collective-permute-start.7) | collective-permute-done | bytes 81952 | tf_op jit(solution)/shard_map/ppermute | solution.py:313
  92.2 0.6 copy-done.11
  92.8 1.6 %shard_map.127.a_ref = bf16[1,80,512]{2,1,0:T(8,128)(2,1)} custom-call(bf16[1,80,512]{2,1,0:T(8,128)(2,1)} %shard_map.126.a_ref, bf16[1,80,512]{2,1,0:T(8,128)(2,1)} %copy-done.11), custom_call_target="tpu_custom_call" | custom-call | tf_op jit(solution)/shard_map/pallas_call | solution.py:326
  94.5 2.6 %collective-permute-start.8 = (bf16[1,80,512]{2,1,0:T(8,128)(2,1)}, bf16[1,80,512]{2,1,0:T(8,128)(2,1)S(1)}, u32[]{:S(2)}, u32[]{:S(2)}) collective-permute-start(bf16[1,80,512]{2,1,0:T(8,128)(2,1)} %shard_map.127.a_ref), channel_id=1, source_target_pairs={{0,16},{1,9},{2,18},{3,11},{4,20},{5,13},{6,22},{7,15},{8,24},{9,1... | collective-permute-start | bytes 245768 | tf_op jit(solution)/shard_map/ppermute | solution.py:313
  97.0 3.0 %collective-permute-done.8.b_ref = bf16[1,80,512]{2,1,0:T(8,128)(2,1)S(1)} collective-permute-done((bf16[1,80,512]{2,1,0:T(8,128)(2,1)}, bf16[1,80,512]{2,1,0:T(8,128)(2,1)S(1)}, u32[]{:S(2)}, u32[]{:S(2)}) %collective-permute-start.8) | collective-permute-done | bytes 81952 | tf_op jit(solution)/shard_map/ppermute | solution.py:313
  100.0 0.6 copy-done.9
  100.6 1.6 %shard_map.128 = bf16[1,64,512]{2,1,0:T(8,128)(2,1)} custom-call(bf16[1,80,512]{2,1,0:T(8,128)(2,1)} %shard_map.127.a_ref, bf16[1,80,512]{2,1,0:T(8,128)(2,1)} %copy-done.9), custom_call_target="tpu_custom_call" | custom-call | tf_op jit(solution)/shard_map/pallas_call | solution.py:327
  102.2 2.0 %collective-permute-start.9 = (bf16[1,64,512]{2,1,0:T(8,128)(2,1)}, bf16[1,64,512]{2,1,0:T(8,128)(2,1)S(1)}, u32[]{:S(2)}, u32[]{:S(2)}) collective-permute-start(bf16[1,64,512]{2,1,0:T(8,128)(2,1)} %shard_map.128), channel_id=1, source_target_pairs={{0,4},{1,3},{2,6},{3,1},{4,0},{5,7},{6,2},{7,5},{8,12},{9,11},{10,... | collective-permute-start | bytes 196616 | tf_op jit(solution)/shard_map/ppermute | solution.py:313
  104.3 3.0 %collective-permute-done.9 = bf16[1,64,512]{2,1,0:T(8,128)(2,1)S(1)} collective-permute-done((bf16[1,64,512]{2,1,0:T(8,128)(2,1)}, bf16[1,64,512]{2,1,0:T(8,128)(2,1)S(1)}, u32[]{:S(2)}, u32[]{:S(2)}) %collective-permute-start.9) | collective-permute-done | bytes 65568 | tf_op jit(solution)/shard_map/ppermute | solution.py:313
  107.3 0.9 pad_maximum_fusion.1
  108.2 1.6 %collective-permute-start.10 = (bf16[2,64,512]{2,1,0:T(8,128)(2,1)S(1)}, bf16[2,64,512]{2,1,0:T(8,128)(2,1)S(1)}, u32[]{:S(2)}, u32[]{:S(2)}) collective-permute-start(bf16[2,64,512]{2,1,0:T(8,128)(2,1)S(1)} %pad_maximum_fusion.1), channel_id=1, source_target_pairs={{0,2},{1,5},{2,0},{3,7},{4,6},{5,1},{6,4},{7,3},{8,10},{9,13},{10,... | collective-permute-start | bytes 393224 | tf_op jit(solution)/shard_map/ppermute | solution.py:313
  109.7 3.4 %collective-permute-done.10 = bf16[2,64,512]{2,1,0:T(8,128)(2,1)S(1)} collective-permute-done((bf16[2,64,512]{2,1,0:T(8,128)(2,1)S(1)}, bf16[2,64,512]{2,1,0:T(8,128)(2,1)S(1)}, u32[]{:S(2)}, u32[]{:S(2)}) %collective-permute-start.10) | collective-permute-done | bytes 131104 | tf_op jit(solution)/shard_map/ppermute | solution.py:313
  113.2 0.9 pad_maximum_fusion.a_ref
  114.1 0.0 copy-start.1
  114.1 0.1 collective-permute-start.11
  114.1 1.5 %collective-permute-done.11.b_ref = bf16[4,64,512]{2,1,0:T(8,128)(2,1)S(1)} collective-permute-done((bf16[4,64,512]{2,1,0:T(8,128)(2,1)S(1)}, bf16[4,64,512]{2,1,0:T(8,128)(2,1)S(1)}, u32[]{:S(2)}, u32[]{:S(2)}) %collective-permute-start.11) | collective-permute-done | bytes 262176 | tf_op jit(solution)/shard_map/ppermute | solution.py:313
  115.7 0.7 copy-done.3
  116.4 3.0 %shard_map.129 = f32[512,512]{1,0:T(8,128)} custom-call(s32[2]{0:T(128)} %pad_add_fusion.place_ref, bf16[4,64,512]{2,1,0:T(8,128)(2,1)} %copy-done.1, bf16[4,64,512]{2,1,0:T(8,128)(2,1)} %copy-done.3, bf16[512,512]{1,0:T(8,128)(2,1)} %wo_ref.1, f32[1,512]{1,0:T(1,128)} %bitcast.27), custom_call_target="tpu_custom_call" | custom-call | tf_op jit(solution)/shard_map/pallas_call | solution.py:330
  (18 shorter events, 0.1 us)
Async XLA Ops:
  0.6 5.2 %copy-start = (bf16[512,1024]{1,0:T(8,128)(2,1)S(1)}, bf16[512,1024]{1,0:T(8,128)(2,1)}, u32[]{:S(2)}) copy-start(bf16[512,1024]{1,0:T(8,128)(2,1)} %param.15) | copy-start | bytes 3145732
  2.2 6.0 %copy-start.12 = (f32[512]{0:T(512)S(1)}, f32[512]{0:T(512)}, u32[]{:S(2)}) copy-start(f32[512]{0:T(512)} %param.13) | copy-start | bytes 6148
  2.2 6.8 %copy-start.13 = (f32[512]{0:T(512)S(1)}, f32[512]{0:T(512)}, u32[]{:S(2)}) copy-start(f32[512]{0:T(512)} %param.14) | copy-start | bytes 6148
  2.8 15.0 %collective-permute-start = (bf16[80,32]{1,0:T(8,128)(2,1)S(1)}, bf16[80,32]{1,0:T(8,128)(2,1)S(1)}, u32[]{:S(2)}, u32[]{:S(2)}) collective-permute-start(bf16[80,32]{1,0:T(8,128)(2,1)S(1)} %pad.18), channel_id=1, source_target_pairs={{0,1},{1,2},{2,3},{3,0},{4,5},{5,6},{6,7},{7,4},{8,9},{9,10},{10,1... | collective-permute-start | bytes 15368 | tf_op jit(solution)/shard_map/ppermute | solution.py:259
  3.8 13.9 %collective-permute-start.1 = (bf16[80,32]{1,0:T(8,128)(2,1)S(1)}, bf16[80,32]{1,0:T(8,128)(2,1)S(1)}, u32[]{:S(2)}, u32[]{:S(2)}) collective-permute-start(bf16[80,32]{1,0:T(8,128)(2,1)S(1)} %pad.19), channel_id=1, source_target_pairs={{1,0},{2,1},{3,2},{0,3},{5,4},{6,5},{7,6},{4,7},{9,8},{10,9},{11,1... | collective-permute-start | bytes 15368 | tf_op jit(solution)/shard_map/ppermute | solution.py:260
  17.7 11.1 %copy-start.5 = (bf16[80,32]{1,0:T(8,128)(2,1)}, bf16[80,32]{1,0:T(8,128)(2,1)S(1)}, u32[]{:S(2)}) copy-start(bf16[80,32]{1,0:T(8,128)(2,1)S(1)} %collective-permute-done.1.hr_ref) | copy-start | bytes 15364
  17.8 11.0 %copy-start.4 = (bf16[80,32]{1,0:T(8,128)(2,1)}, bf16[80,32]{1,0:T(8,128)(2,1)S(1)}, u32[]{:S(2)}) copy-start(bf16[80,32]{1,0:T(8,128)(2,1)S(1)} %collective-permute-done.hl_ref) | copy-start | bytes 15364
  17.9 6.4 %collective-permute-start.2 = (bf16[80,514]{1,0:T(8,128)(2,1)S(1)}, bf16[80,514]{1,0:T(8,128)(2,1)S(1)}, u32[]{:S(2)}, u32[]{:S(2)}) collective-permute-start(bf16[80,514]{1,0:T(8,128)(2,1)S(1)} %fusion.3), channel_id=1, source_target_pairs={{0,4},{4,8},{8,12},{12,16},{16,20},{20,24},{24,28},{1,5},{5,9},{9,... | collective-permute-start | bytes 246728 | tf_op jit(solution)/shard_map/ppermute | solution.py:267
  22.2 6.5 %collective-permute-start.3 = (bf16[80,514]{1,0:T(8,128)(2,1)S(1)}, bf16[80,514]{1,0:T(8,128)(2,1)S(1)}, u32[]{:S(2)}, u32[]{:S(2)}) collective-permute-start(bf16[80,514]{1,0:T(8,128)(2,1)S(1)} %fusion.5), channel_id=1, source_target_pairs={{4,0},{8,4},{12,8},{16,12},{20,16},{24,20},{28,24},{5,1},{9,5},{13... | collective-permute-start | bytes 246728 | tf_op jit(solution)/shard_map/ppermute | solution.py:268
  24.3 4.4 %copy-start.7 = (bf16[80,514]{1,0:T(8,128)(2,1)}, bf16[80,514]{1,0:T(8,128)(2,1)S(1)}, u32[]{:S(2)}) copy-start(bf16[80,514]{1,0:T(8,128)(2,1)S(1)} %collective-permute-done.2.top_ref) | copy-start | bytes 246724
  28.7 0.7 copy-start.8
  67.7 1.9 %collective-permute-start.4 = (bf16[4,80,512]{2,1,0:T(8,128)(2,1)}, bf16[4,80,512]{2,1,0:T(8,128)(2,1)S(1)}, u32[]{:S(2)}, u32[]{:S(2)}) collective-permute-start(bf16[4,80,512]{2,1,0:T(8,128)(2,1)} %get-tuple-element.11), channel_id=1, source_target_pairs={{0,1},{1,0},{2,3},{3,2},{4,5},{5,4},{6,7},{7,6},{8,9},{9,8},{10,11... | collective-permute-start | bytes 983048 | tf_op jit(solution)/shard_map/ppermute | solution.py:313
  69.6 0.7 copy-start.2
  72.3 5.5 %collective-permute-start.5 = (bf16[2,80,512]{2,1,0:T(8,128)(2,1)}, bf16[2,80,512]{2,1,0:T(8,128)(2,1)S(1)}, u32[]{:S(2)}, u32[]{:S(2)}) collective-permute-start(bf16[2,80,512]{2,1,0:T(8,128)(2,1)} %get-tuple-element.13), channel_id=1, source_target_pairs={{0,2},{1,5},{2,0},{3,7},{4,6},{5,1},{6,4},{7,3},{8,10},{9,13},{10,... | collective-permute-start | bytes 491528 | tf_op jit(solution)/shard_map/ppermute | solution.py:313
  77.8 0.7 copy-start.6
  80.2 5.1 %collective-permute-start.6 = (bf16[1,80,512]{2,1,0:T(8,128)(2,1)}, bf16[1,80,512]{2,1,0:T(8,128)(2,1)S(1)}, u32[]{:S(2)}, u32[]{:S(2)}) collective-permute-start(bf16[1,80,512]{2,1,0:T(8,128)(2,1)} %get-tuple-element.15), channel_id=1, source_target_pairs={{0,4},{1,3},{2,6},{3,1},{4,0},{5,7},{6,2},{7,5},{8,12},{9,11},{10,... | collective-permute-start | bytes 245768 | tf_op jit(solution)/shard_map/ppermute | solution.py:313
  85.3 0.6 copy-start.10
  87.6 4.7 %collective-permute-start.7 = (bf16[1,80,512]{2,1,0:T(8,128)(2,1)}, bf16[1,80,512]{2,1,0:T(8,128)(2,1)S(1)}, u32[]{:S(2)}, u32[]{:S(2)}) collective-permute-start(bf16[1,80,512]{2,1,0:T(8,128)(2,1)} %shard_map.126.a_ref), channel_id=1, source_target_pairs={{0,8},{1,17},{2,10},{3,19},{4,12},{5,21},{6,14},{7,23},{8,0},{9,25... | collective-permute-start | bytes 245768 | tf_op jit(solution)/shard_map/ppermute | solution.py:313
  92.2 0.6 copy-start.11
  94.5 5.6 %collective-permute-start.8 = (bf16[1,80,512]{2,1,0:T(8,128)(2,1)}, bf16[1,80,512]{2,1,0:T(8,128)(2,1)S(1)}, u32[]{:S(2)}, u32[]{:S(2)}) collective-permute-start(bf16[1,80,512]{2,1,0:T(8,128)(2,1)} %shard_map.127.a_ref), channel_id=1, source_target_pairs={{0,16},{1,9},{2,18},{3,11},{4,20},{5,13},{6,22},{7,15},{8,24},{9,1... | collective-permute-start | bytes 245768 | tf_op jit(solution)/shard_map/ppermute | solution.py:313
  100.0 0.6 copy-start.9
  102.2 5.1 %collective-permute-start.9 = (bf16[1,64,512]{2,1,0:T(8,128)(2,1)}, bf16[1,64,512]{2,1,0:T(8,128)(2,1)S(1)}, u32[]{:S(2)}, u32[]{:S(2)}) collective-permute-start(bf16[1,64,512]{2,1,0:T(8,128)(2,1)} %shard_map.128), channel_id=1, source_target_pairs={{0,4},{1,3},{2,6},{3,1},{4,0},{5,7},{6,2},{7,5},{8,12},{9,11},{10,... | collective-permute-start | bytes 196616 | tf_op jit(solution)/shard_map/ppermute | solution.py:313
  108.2 5.0 %collective-permute-start.10 = (bf16[2,64,512]{2,1,0:T(8,128)(2,1)S(1)}, bf16[2,64,512]{2,1,0:T(8,128)(2,1)S(1)}, u32[]{:S(2)}, u32[]{:S(2)}) collective-permute-start(bf16[2,64,512]{2,1,0:T(8,128)(2,1)S(1)} %pad_maximum_fusion.1), channel_id=1, source_target_pairs={{0,2},{1,5},{2,0},{3,7},{4,6},{5,1},{6,4},{7,3},{8,10},{9,13},{10,... | collective-permute-start | bytes 393224 | tf_op jit(solution)/shard_map/ppermute | solution.py:313
  114.1 1.6 %copy-start.1 = (bf16[4,64,512]{2,1,0:T(8,128)(2,1)}, bf16[4,64,512]{2,1,0:T(8,128)(2,1)S(1)}, u32[]{:S(2)}) copy-start(bf16[4,64,512]{2,1,0:T(8,128)(2,1)S(1)} %pad_maximum_fusion.a_ref) | copy-start | bytes 786436
  114.1 1.6 %collective-permute-start.11 = (bf16[4,64,512]{2,1,0:T(8,128)(2,1)S(1)}, bf16[4,64,512]{2,1,0:T(8,128)(2,1)S(1)}, u32[]{:S(2)}, u32[]{:S(2)}) collective-permute-start(bf16[4,64,512]{2,1,0:T(8,128)(2,1)S(1)} %pad_maximum_fusion.a_ref), channel_id=1, source_target_pairs={{0,1},{1,0},{2,3},{3,2},{4,5},{5,4},{6,7},{7,6},{8,9},{9,8},{10,11... | collective-permute-start | bytes 786440 | tf_op jit(solution)/shard_map/ppermute | solution.py:313
  115.7 0.7 copy-start.3

commit v2 on v1

--- a/solution.py
+++ b/solution.py
@@ -70,7 +70,7 @@
     place_ref,
     x_ref, hl_ref, hr_ref, top_ref, bot_ref, wt_ref, bias_ref, gain_ref, wk_ref, wvt_ref, qz_ref,
     tok_out, keep_ref, send_ref,
-    y_ref, xs_ref, st_ref, tok_ref, k_ref, vt_ref, s_ref, sems,
+    y_ref, xs_ref, st_ref, tok_ref, k_ref, vt_ref, s_ref, col_ref, sems,
 ):
     chan, rows, cols = x_ref.shape
     half = cols // 2
@@ -119,12 +119,18 @@
     for h in range(HEADS):
         vt_ref[h * HR + HD : (h + 1) * HR, :] = jnp.ones((HR - HD, tokens), bf16)
 
+    for n, row in enumerate((bias_ref, gain_ref)):
+        col_ref[n] = jnp.transpose(jnp.broadcast_to(row[...], (128, width)))
+
+    def column(n):
+        return jnp.concatenate([col_ref[n]] * (half // 128), axis=1)
+
     def stem(r, slot):
         patch = xs_ref[pl.ds(2 * r, 4)].reshape(16 * CP, half)
         st_ref[slot] = jnp.dot(wt_ref[...], patch, preferred_element_type=f32)
 
     def finish(r, slot):
-        value = rows_norm(st_ref[slot] + bias_ref[...], 0) * gain_ref[...]
+        value = rows_norm(st_ref[slot] + column(0), 0) * column(1)
         tt = value.astype(bf16)
         tok = jnp.transpose(tt)
         tok_ref[r] = tok
@@ -211,8 +217,8 @@
 
 
 def combined(a, b):
-    sums_a, total_a, peak_a = unpack(a)
-    sums_b, total_b, peak_b = unpack(b)
+    sums_a, total_a, peak_a = a
+    sums_b, total_b, peak_b = b
     peak = jnp.maximum(peak_a, peak_b)
     fold_a = jnp.exp2(peak_a - peak)
     fold_b = jnp.exp2(peak_b - peak)
@@ -220,20 +226,23 @@
 
 
 def fold_kernel(a_ref, b_ref, *outs):
-    per = a_ref.shape[0] // len(outs)
-    for n in range(a_ref.shape[0]):
-        outs[n // per][n % per] = pack(*combined(a_ref[n], b_ref[n]))
-
-
-def attended_kernel(a_ref, b_ref, out_ref):
-    sums, total, peak = combined(a_ref[0], b_ref[0])
-    out_ref[0] = (sums / total).astype(bf16)
-
-
-def out_kernel(place_ref, a_ref, b_ref, wo_ref, gain_ref, out_ref, all_ref):
+    for n, out in enumerate(outs):
+        out[0] = pack(*combined(unpack(a_ref[n]), unpack(b_ref[n])))
+
+
+def group_kernel(*refs, last):
+    states = [unpack(ref[0]) for ref in refs[:-1]]
+    while len(states) > 1:
+        states = [combined(*states[n : n + 2]) for n in range(0, len(states), 2)]
+    sums, total, peak = states[0]
+    refs[-1][0] = (sums / total).astype(bf16) if last else pack(sums, total, peak)
+
+
+def out_kernel(place_ref, *refs):
+    parts, (wo_ref, gain_ref, out_ref, all_ref) = refs[:HEADS], refs[HEADS:]
     half = HEADS // 2
     for t in range(HEADS):
-        value = a_ref[t] if t < half else b_ref[t - half]
+        value = parts[t][0]
         h = (t % half) ^ place_ref[t // half]
         all_ref[pl.ds(pl.multiple_of(h * HD, HD), HD), :] = value.astype(f32)
     attended = jnp.transpose(all_ref[...]).astype(bf16)
@@ -259,18 +268,21 @@
     hl = lax.ppermute(jnp.pad(field[:, :, cols - 1], extra), "lon", ahead)
     hr = lax.ppermute(jnp.pad(field[:, :, 0], extra), "lon", back)
 
-    def edge(r):
-        return jnp.concatenate([jnp.pad(field[:, r, :], extra), hl[:, r : r + 1], hr[:, r : r + 1]], 1)
-
-    up = [(i, i + 1) for i in range(nlat - 1)]
-    down = [(t, s) for s, t in up]
-    top = lax.ppermute(edge(rows - 1), "lat", up)
-    bot = lax.ppermute(edge(0), "lat", down)
-
     wt = stem_weight.reshape(16, chan, width)
     wt = jnp.pad(wt, ((0, 0), (0, CP - chan), (0, 0))).reshape(16 * CP, width).T
     wk = kv_weight[:, :width]
     wvt = kv_weight[:, width:].T
+    hl, hr, wt, wvt = lax.optimization_barrier((hl, hr, wt, wvt))
+
+    def edge(r):
+        return jnp.concatenate([jnp.pad(field[:, r, :], extra), hl[:, r : r + 1], hr[:, r : r + 1]], 1)
+
+    low, high = edge(rows - 1), edge(0)
+    low, high, latents = lax.optimization_barrier((low, high, latents))
+    up = [(i, i + 1) for i in range(nlat - 1)]
+    down = [(t, s) for s, t in up]
+    top = lax.ppermute(low, "lat", up)
+    bot = lax.ppermute(high, "lat", down)
     qz = call(query_kernel, shape((HEADS, 4 * HD, lat), bf16), 3, smem=1)(
         head_gain, latents, latent_gain[None, :], query_weight
     )
@@ -299,37 +311,45 @@
             VMEM((tokens, width), bf16),
             VMEM((HEADS * HR, tokens), bf16),
             VMEM((2, CT, lat), f32),
+            VMEM((2, width, 128), f32),
             pltpu.SemaphoreType.DMA((trows,)),
         ],
-    )(place, field, hl, hr, top, bot, wt, stem_bias[:, None], token_gain[:, None], wk, wvt, qz)
-
-    def swap(x, flip0, flip1):
+    )(place, field, hl, hr, top, bot, wt, stem_bias[None, :], token_gain[None, :], wk, wvt, qz)
+
+    def swap(x, flips0, flips1):
         pairs = []
         for a in range(nlat):
             for b in range(nlon):
-                axis, bit = flip1 if b & 1 else flip0
-                to = (a ^ bit, b) if axis == "lat" else (a, b ^ bit)
-                pairs.append((a * nlon + b, to[0] * nlon + to[1]))
+                to = {"lat": a, "lon": b}
+                for axis, bit in flips1 if b & 1 else flips0:
+                    to[axis] ^= bit
+                pairs.append((a * nlon + b, to["lat"] * nlon + to["lon"]))
         return lax.ppermute(x, ("lat", "lon"), pairs)
 
-    cores = ("lon", 1)
+    def subsets(bits):
+        return [[bit for n, bit in enumerate(bits) if m >> n & 1] for m in range(1, 1 << len(bits))]
+
+    cores = [("lon", 1)]
     first, second = ("lon", 2), ("lat", 1)
-    rest = [("lat", 1 << n) for n in range(1, nlat.bit_length() - 1)]
-    rest += [("lon", 1 << n) for n in range(2, nlon.bit_length() - 1)]
-
-    two = shape((HEADS // 4, HR, lat), bf16)
-    one = shape((HEADS // 8, HR, lat), bf16)
-    keep, send = call(fold_kernel, [two, two], 2)(keep, swap(send, cores, cores))
-    keep, send = call(fold_kernel, [one, one], 2)(keep, swap(send, first, second))
-    (mine,) = call(fold_kernel, [one], 2)(keep, swap(send, second, first))
-    for n in range(len(rest) - 1):
-        (mine,) = call(fold_kernel, [one], 2)(mine, swap(mine, rest[n], rest[(n + 1) % len(rest)]))
-    part = call(attended_kernel, shape((1, HD, lat), bf16), 2)(mine, swap(mine, rest[-1], rest[0]))
-    part = jnp.concatenate([part, swap(part, second, first)])
-    part = jnp.concatenate([part, swap(part, first, second)])
+    near = list(zip(subsets([second, first]), subsets([first, second])))
+    far = [("lat", 1 << n) for n in range(1, nlat.bit_length() - 1)]
+    far += [("lon", 1 << n) for n in range(2, nlon.bit_length() - 1)]
+    groups = [far[n : n + 2] for n in range(0, len(far), 2)]
+
+    one = shape((1, HR, lat), bf16)
+    own, *others = call(fold_kernel, [one] * (HEADS // 2), 2)(keep, swap(send, cores, cores))
+    states = [own] + [swap(x, *flips) for x, flips in zip(others, near)]
+    own = call(functools.partial(group_kernel, last=False), one, 4)(*states)
+    for n, bits in enumerate(groups):
+        last = n == len(groups) - 1
+        states = [own] + [swap(own, flips, flips) for flips in subsets(bits)]
+        out = shape((1, HD, lat), bf16) if last else one
+        own = call(functools.partial(group_kernel, last=last), out, len(states))(*states)
+    parts = [own] + [swap(own, *flips) for flips in near]
+    parts += [swap(x, cores, cores) for x in parts]
     latent_out = call(
-        out_kernel, shape((lat, width), f32), 4, smem=1, scratch=[VMEM((width, lat), f32)]
-    )(place, part, swap(part, cores, cores), out_weight, out_gain[None, :])
+        out_kernel, shape((lat, width), f32), HEADS + 2, smem=1, scratch=[VMEM((width, lat), f32)]
+    )(place, *parts, out_weight, out_gain[None, :])
     return (tok, latent_out)
 
 

time: 120 us -> 104 us (0.87)
  waiting for transfers between devices: 26.9 us -> 18.2 us
  Pallas kernels: 53.5 us -> 50.6 us
  local copies, waits for them, and re-layouts: 15.5 us -> 12.9 us
  other arithmetic: 2.55 us -> 0.81 us
    ppermute x8 -> x14, waiting for transfers between devices: 22.5 us -> 17.4 us  [swap(): return lax.ppermute(x, ('lat', 'lon'), pairs)]
    ppermute x2, waiting for transfers between devices: 4.41 us -> 0.73 us  [the longest x1 0.73 us: shards(): bot = lax.ppermute(high, 'lat', down)]
    pallas_call x6 -> x4, Pallas kernels: 11.4 us -> 8.47 us  [the longest x1 3.06 us: shards(): call(out_kernel, shape((lat, width), f32), HEADS + 2, smem=1, scratch=[VM...]
    broadcast_in_dim x2 -> x0, local copies, waits for them, and re-layouts: 1.73 us -> none  [the longest x1 0.88 us: shards(): token_gain[:, None]]
    concatenate x2 -> x0, other arithmetic: 1.72 us -> none  [the longest x1 0.87 us: shards(): part = jnp.concatenate([part, swap(part, first, second)])]
    unnamed x33 -> x41, local copies, waits for them, and re-layouts: 6.71 us -> 5.89 us
    ppermute x8 -> x14, starting transfers between devices: 11.9 us -> 12 us  [swap(): return lax.ppermute(x, ('lat', 'lon'), pairs)]
  transfers between devices with their start and end apart: 12 -> 18, of which waited for: 9 -> 12; matrix products, arithmetic and copies ran while one was open for 8% -> 7% of each run, Pallas kernels for 3% -> 4%
where the time goes in v2:
time: 104 us
  Pallas kernels  50.6 us (49%)
  starting transfers between devices  20.2 us (19%)
  waiting for transfers between devices  18.2 us (18%)
  local copies, waits for them, and re-layouts  12.9 us (12%)
    pallas_call x1, Pallas kernels, shards(): call(encode_kernel, [shape((trows, half, width), bf16), state, state], 11...  38.5 us
    ppermute x14, waiting for transfers between devices, swap(): return lax.ppermute(x, ('lat', 'lon'), pairs)  17.4 us
    ppermute x14, starting transfers between devices, swap(): return lax.ppermute(x, ('lat', 'lon'), pairs)  12 us
    unnamed x41, local copies, waits for them, and re-layouts  5.89 us
    ppermute x1, starting transfers between devices, shards(): top = lax.ppermute(low, 'lat', up)  4.16 us
    pallas_call x1, Pallas kernels, shards(): call(query_kernel, shape((HEADS, 4 * HD, lat), bf16), 3, smem=1)  3.68 us
    pallas_call x1, Pallas kernels, shards(): call(out_kernel, shape((lat, width), f32), HEADS + 2, smem=1, scratch=[VM...  3.06 us
  transfers between devices with their start and end apart: 18, of which 12 were waited for; matrix products, arithmetic and copies ran while one was open for 7% of the time, Pallas kernels for 4%

profile of v2, /device:TPU:0, one launch (start us, length us, event | category | flops | bytes accessed | tf_op | source)
XLA Modules:
  0.0 103.6 jit_solution(4048923167777931125)
XLA Ops:
  0.6 1.6 %fusion.7 = (bf16[69,32,1]{2,1,0:T(8,128)(2,1)S(1)}, bf16[69,32,1]{2,1,0:T(8,128)(2,1)S(1)}) fusion(bf16[69,32,512]{2,1,0:T(8,128)(2,1)} %x_ref.1), kind=kLoop, calls=%fused_computation.11 | loop fusion | bytes 17664 | tf_op jit(solution)/shard_map/slice | solution.py:269
  2.2 0.5 copy.25
  2.7 0.5 collective-permute-start
  3.3 0.5 copy.26
  3.8 2.0 %collective-permute-start.1 = (bf16[80,32]{1,0:T(8,128)(2,1)S(1)}, bf16[80,32]{1,0:T(8,128)(2,1)S(1)}, u32[]{:S(2)}, u32[]{:S(2)}) collective-permute-start(bf16[80,32]{1,0:T(8,128)(2,1)S(1)} %pad.19), channel_id=1, source_target_pairs={{1,0},{2,1},{3,2},{0,3},{5,4},{6,5},{7,6},{4,7},{9,8},{10,9},{11,1... | collective-permute-start | bytes 15368 | tf_op jit(solution)/shard_map/ppermute | solution.py:269
  5.8 1.5 %fusion.6 = (bf16[69,1,512]{2,1,0:T(2,128)(2,1)S(1)}, bf16[69,1,512]{2,1,0:T(2,128)(2,1)S(1)}) fusion(bf16[69,32,512]{2,1,0:T(8,128)(2,1)} %x_ref.1), kind=kLoop, calls=%fused_computation.10 | loop fusion | bytes 282624 | tf_op jit(solution)/shard_map/slice | solution.py:278
  7.3 0.9 fusion.8
  8.2 1.0 copy.27
  9.2 1.4 %reshape.10 = bf16[16,69,512]{2,1,0:T(8,128)(2,1)S(1)} reshape(bf16[1104,512]{1,0:T(8,128)(2,1)} %param.12) | data formatting | bytes 2260992 | tf_op jit(solution)/shard_map/reshape | solution.py:271
  10.6 0.1 pad.20
  10.8 1.5 %copy.21 = bf16[1280,512]{0,1:T(8,128)(2,1)} copy(bf16[1280,512]{1,0:T(8,128)(2,1)S(1)} %bitcast.15) | data formatting | bytes 2621440 | tf_op jit(solution)/shard_map/reshape | solution.py:272
  12.2 0.0 collective-permute-done.hl_ref
  12.2 0.0 collective-permute-done.1.hr_ref
  12.2 0.0 copy-start.3
  12.2 0.1 fusion.9
  12.3 0.1 fusion.5
  12.4 0.1 fusion.3
  12.5 4.2 %collective-permute-start.2 = (bf16[80,514]{1,0:T(8,128)(2,1)S(1)}, bf16[80,514]{1,0:T(8,128)(2,1)S(1)}, u32[]{:S(2)}, u32[]{:S(2)}) collective-permute-start(bf16[80,514]{1,0:T(8,128)(2,1)S(1)} %fusion.3), channel_id=1, source_target_pairs={{0,4},{4,8},{8,12},{12,16},{16,20},{20,24},{24,28},{1,5},{5,9},{9,... | collective-permute-start | bytes 246728 | tf_op jit(solution)/shard_map/ppermute | solution.py:284
  16.7 1.5 %collective-permute-start.3 = (bf16[80,514]{1,0:T(8,128)(2,1)S(1)}, bf16[80,514]{1,0:T(8,128)(2,1)S(1)}, u32[]{:S(2)}, u32[]{:S(2)}) collective-permute-start(bf16[80,514]{1,0:T(8,128)(2,1)S(1)} %fusion.5), channel_id=1, source_target_pairs={{4,0},{8,4},{12,8},{16,12},{20,16},{24,20},{28,24},{5,1},{9,5},{13... | collective-permute-start | bytes 246728 | tf_op jit(solution)/shard_map/ppermute | solution.py:285
  18.1 0.6 pad_add_fusion.place_ref
  18.8 3.7 %shard_map.122.qz_ref = bf16[8,256,512]{2,1,0:T(8,128)(2,1)} custom-call(f32[8]{0:T(128)} %gain_ref.1, f32[512,512]{1,0:T(8,128)} %latents_ref, f32[1,512]{1,0:T(1,128)} %bitcast.20, bf16[512,512]{1,0:T(8,128)(2,1)} %qw_ref.1), custom_call_target="tpu_custom_call" | custom-call | tf_op jit(solution)/shard_map/pallas_call | solution.py:286
  22.5 0.0 copy-done.2
  22.5 0.0 collective-permute-done.2.top_ref
  22.5 0.7 collective-permute-done.3.bot_ref
  23.2 0.6 copy-done.5
  23.9 38.5 %shard_map.123 = (bf16[16,256,512]{2,1,0:T(8,128)(2,1)}, bf16[4,80,512]{2,1,0:T(8,128)(2,1)}, bf16[4,80,512]{2,1,0:T(8,128)(2,1)}) custom-call(s32[2]{0:T(128)} %pad_add_fusion.place_ref, bf16[69,32,512]{2,1,0:T(8,128)(2,1)} %x_ref.1, bf16[80,32]{1,0:T(8,128)(2,1)} %copy-done.2, bf16[80,32]{1,0:T(8,128)(2,1)} %copy-done.3, bf16[80,514]{1,0:T(8,128)(2,1)} %copy-done.4, ...), custom_call_target="tpu_custom_call" | custom-call | tf_op jit(solution)/shard_map/pallas_call | solution.py:300
  62.4 0.1 collective-permute-start.4
  62.5 1.8 %collective-permute-done.4.b_ref = bf16[4,80,512]{2,1,0:T(8,128)(2,1)S(1)} collective-permute-done((bf16[4,80,512]{2,1,0:T(8,128)(2,1)}, bf16[4,80,512]{2,1,0:T(8,128)(2,1)S(1)}, u32[]{:S(2)}, u32[]{:S(2)}) %collective-permute-start.4) | collective-permute-done | bytes 327712 | tf_op jit(solution)/shard_map/ppermute | solution.py:327
  64.3 0.7 copy-done.1
  65.0 1.9 %shard_map.124 = (bf16[1,80,512]{2,1,0:T(8,128)(2,1)}, bf16[1,80,512]{2,1,0:T(8,128)(2,1)}, bf16[1,80,512]{2,1,0:T(8,128)(2,1)}, bf16[1,80,512]{2,1,0:T(8,128)(2,1)}) custom-call(bf16[4,80,512]{2,1,0:T(8,128)(2,1)} %get-tuple-element.24.a_ref, bf16[4,80,512]{2,1,0:T(8,128)(2,1)} %copy-done.1), custom_call_target="tpu_custom_call" | custom-call | tf_op jit(solution)/shard_map/pallas_call | solution.py:340
  66.9 2.5 %collective-permute-start.5 = (bf16[1,80,512]{2,1,0:T(8,128)(2,1)}, bf16[1,80,512]{2,1,0:T(8,128)(2,1)S(1)}, u32[]{:S(2)}, u32[]{:S(2)}) collective-permute-start(bf16[1,80,512]{2,1,0:T(8,128)(2,1)} %get-tuple-element.27), channel_id=1, source_target_pairs={{0,4},{1,3},{2,6},{3,1},{4,0},{5,7},{6,2},{7,5},{8,12},{9,11},{10,... | collective-permute-start | bytes 245768 | tf_op jit(solution)/shard_map/ppermute | solution.py:327
  69.4 1.5 %collective-permute-start.6 = (bf16[1,80,512]{2,1,0:T(8,128)(2,1)}, bf16[1,80,512]{2,1,0:T(8,128)(2,1)S(1)}, u32[]{:S(2)}, u32[]{:S(2)}) collective-permute-start(bf16[1,80,512]{2,1,0:T(8,128)(2,1)} %get-tuple-element.28), channel_id=1, source_target_pairs={{0,2},{1,5},{2,0},{3,7},{4,6},{5,1},{6,4},{7,3},{8,10},{9,13},{10,... | collective-permute-start | bytes 245768 | tf_op jit(solution)/shard_map/ppermute | solution.py:327
  70.9 0.0 collective-permute-start.7
  70.9 1.3 %collective-permute-done.5.refs_1_ = bf16[1,80,512]{2,1,0:T(8,128)(2,1)S(1)} collective-permute-done((bf16[1,80,512]{2,1,0:T(8,128)(2,1)}, bf16[1,80,512]{2,1,0:T(8,128)(2,1)S(1)}, u32[]{:S(2)}, u32[]{:S(2)}) %collective-permute-start.5) | collective-permute-done | bytes 81952 | tf_op jit(solution)/shard_map/ppermute | solution.py:327
  72.2 2.7 %collective-permute-done.6.refs_2_ = bf16[1,80,512]{2,1,0:T(8,128)(2,1)S(1)} collective-permute-done((bf16[1,80,512]{2,1,0:T(8,128)(2,1)}, bf16[1,80,512]{2,1,0:T(8,128)(2,1)S(1)}, u32[]{:S(2)}, u32[]{:S(2)}) %collective-permute-start.6) | collective-permute-done | bytes 81952 | tf_op jit(solution)/shard_map/ppermute | solution.py:327
  75.0 1.5 %collective-permute-done.7.refs_3_ = bf16[1,80,512]{2,1,0:T(8,128)(2,1)S(1)} collective-permute-done((bf16[1,80,512]{2,1,0:T(8,128)(2,1)}, bf16[1,80,512]{2,1,0:T(8,128)(2,1)S(1)}, u32[]{:S(2)}, u32[]{:S(2)}) %collective-permute-start.7) | collective-permute-done | bytes 81952 | tf_op jit(solution)/shard_map/ppermute | solution.py:327
  76.4 0.6 copy-done.9
  77.1 1.7 %shard_map.125.refs_0_ = bf16[1,80,512]{2,1,0:T(8,128)(2,1)} custom-call(bf16[1,80,512]{2,1,0:T(8,128)(2,1)} %get-tuple-element.26.refs_0_, bf16[1,80,512]{2,1,0:T(8,128)(2,1)} %copy-done.6, bf16[1,80,512]{2,1,0:T(8,128)(2,1)} %copy-done.7, bf16[1,80,512]{2,1,0:T(8,128)(2,1)} %copy-done.9), custom_call_target="tpu_custom_call" | custom-call | tf_op jit(solution)/shard_map/pallas_call | solution.py:342
  78.8 3.1 %collective-permute-start.10 = (bf16[1,80,512]{2,1,0:T(8,128)(2,1)}, bf16[1,80,512]{2,1,0:T(8,128)(2,1)S(1)}, u32[]{:S(2)}, u32[]{:S(2)}) collective-permute-start(bf16[1,80,512]{2,1,0:T(8,128)(2,1)} %shard_map.125.refs_0_), channel_id=1, source_target_pairs={{0,24},{1,25},{2,26},{3,27},{4,28},{5,29},{6,30},{7,31},{8,16},{9,... | collective-permute-start | bytes 245768 | tf_op jit(solution)/shard_map/ppermute | solution.py:327
  81.9 0.0 collective-permute-start.9
  82.0 1.3 %collective-permute-start.8 = (bf16[1,80,512]{2,1,0:T(8,128)(2,1)}, bf16[1,80,512]{2,1,0:T(8,128)(2,1)S(1)}, u32[]{:S(2)}, u32[]{:S(2)}) collective-permute-start(bf16[1,80,512]{2,1,0:T(8,128)(2,1)} %shard_map.125.refs_0_), channel_id=1, source_target_pairs={{0,8},{1,9},{2,10},{3,11},{4,12},{5,13},{6,14},{7,15},{8,0},{9,1},... | collective-permute-start | bytes 245768 | tf_op jit(solution)/shard_map/ppermute | solution.py:327
  83.2 2.1 %collective-permute-done.10.refs_3_ = bf16[1,80,512]{2,1,0:T(8,128)(2,1)S(1)} collective-permute-done((bf16[1,80,512]{2,1,0:T(8,128)(2,1)}, bf16[1,80,512]{2,1,0:T(8,128)(2,1)S(1)}, u32[]{:S(2)}, u32[]{:S(2)}) %collective-permute-start.10) | collective-permute-done | bytes 81952 | tf_op jit(solution)/shard_map/ppermute | solution.py:327
  85.3 3.3 %collective-permute-done.9.refs_2_ = bf16[1,80,512]{2,1,0:T(8,128)(2,1)S(1)} collective-permute-done((bf16[1,80,512]{2,1,0:T(8,128)(2,1)}, bf16[1,80,512]{2,1,0:T(8,128)(2,1)S(1)}, u32[]{:S(2)}, u32[]{:S(2)}) %collective-permute-start.9) | collective-permute-done | bytes 81952 | tf_op jit(solution)/shard_map/ppermute | solution.py:327
  88.5 0.0 collective-permute-done.8.refs_1_
  88.6 0.6 copy-done.10
  89.2 0.6 copy-done.11
  89.8 1.7 %shard_map.126.refs_0_ = bf16[1,64,512]{2,1,0:T(8,128)(2,1)} custom-call(bf16[1,80,512]{2,1,0:T(8,128)(2,1)} %shard_map.125.refs_0_, bf16[1,80,512]{2,1,0:T(8,128)(2,1)} %copy-done.11, bf16[1,80,512]{2,1,0:T(8,128)(2,1)} %copy-done.10, bf16[1,80,512]{2,1,0:T(8,128)(2,1)} %copy-done.8), custom_call_target="tpu_custom_call" | custom-call | tf_op jit(solution)/shard_map/pallas_call | solution.py:347
  91.5 2.0 %collective-permute-start.13 = (bf16[1,64,512]{2,1,0:T(8,128)(2,1)}, bf16[1,64,512]{2,1,0:T(8,128)(2,1)S(1)}, u32[]{:S(2)}, u32[]{:S(2)}) collective-permute-start(bf16[1,64,512]{2,1,0:T(8,128)(2,1)} %shard_map.126.refs_0_), channel_id=1, source_target_pairs={{0,6},{1,7},{2,4},{3,5},{4,2},{5,3},{6,0},{7,1},{8,14},{9,15},{10,... | collective-permute-start | bytes 196616 | tf_op jit(solution)/shard_map/ppermute | solution.py:327
  93.6 0.6 collective-permute-start.12
  94.1 0.9 collective-permute-start.11
  95.0 0.0 collective-permute-start.14
  95.0 2.0 %collective-permute-done.13.refs_3_ = bf16[1,64,512]{2,1,0:T(8,128)(2,1)S(1)} collective-permute-done((bf16[1,64,512]{2,1,0:T(8,128)(2,1)}, bf16[1,64,512]{2,1,0:T(8,128)(2,1)S(1)}, u32[]{:S(2)}, u32[]{:S(2)}) %collective-permute-start.13) | collective-permute-done | bytes 65568 | tf_op jit(solution)/shard_map/ppermute | solution.py:327
  97.0 0.0 collective-permute-start.17
  97.0 1.2 %collective-permute-done.12.refs_2_ = bf16[1,64,512]{2,1,0:T(8,128)(2,1)S(1)} collective-permute-done((bf16[1,64,512]{2,1,0:T(8,128)(2,1)}, bf16[1,64,512]{2,1,0:T(8,128)(2,1)S(1)}, u32[]{:S(2)}, u32[]{:S(2)}) %collective-permute-start.12) | collective-permute-done | bytes 65568 | tf_op jit(solution)/shard_map/ppermute | solution.py:327
  98.2 0.0 collective-permute-start.16
  98.2 0.4 collective-permute-done.11.refs_1_
  98.6 0.1 collective-permute-start.15
  98.7 0.0 collective-permute-done.14.refs_4_
  98.7 0.0 collective-permute-done.17.refs_7_
  98.7 0.7 collective-permute-done.16.refs_6_
  99.4 0.4 collective-permute-done.15.refs_5_
  99.9 0.1 copy-done.17
  100.1 0.4 copy-done.18
  100.5 3.1 %shard_map.127 = f32[512,512]{1,0:T(8,128)} custom-call(s32[2]{0:T(128)} %pad_add_fusion.place_ref, bf16[1,64,512]{2,1,0:T(8,128)(2,1)} %shard_map.126.refs_0_, bf16[1,64,512]{2,1,0:T(8,128)(2,1)} %copy-done.14, bf16[1,64,512]{2,1,0:T(8,128)(2,1)} %copy-done.13, bf16[1,64,512]{2,1,0:T(8,128)(2,1)} %copy-done.12, bf16[1,64,512]{2,1,0:T(8,128)(2,1)} %copy-done.15, ...), custom_call_target="tpu_custom_call" | custom-call | tf_op jit(solution)/shard_map/pallas_call | solution.py:350
  (32 shorter events, 0.1 us)
Async XLA Ops:
  0.6 6.6 %copy-start = (bf16[512,1024]{1,0:T(8,128)(2,1)S(1)}, bf16[512,1024]{1,0:T(8,128)(2,1)}, u32[]{:S(2)}) copy-start(bf16[512,1024]{1,0:T(8,128)(2,1)} %param.15) | copy-start | bytes 3145732
  2.7 9.5 %collective-permute-start = (bf16[80,32]{1,0:T(8,128)(2,1)S(1)}, bf16[80,32]{1,0:T(8,128)(2,1)S(1)}, u32[]{:S(2)}, u32[]{:S(2)}) collective-permute-start(bf16[80,32]{1,0:T(8,128)(2,1)S(1)} %pad.18), channel_id=1, source_target_pairs={{0,1},{1,2},{2,3},{3,0},{4,5},{5,6},{6,7},{7,4},{8,9},{9,10},{10,1... | collective-permute-start | bytes 15368 | tf_op jit(solution)/shard_map/ppermute | solution.py:268
  3.8 8.4 %collective-permute-start.1 = (bf16[80,32]{1,0:T(8,128)(2,1)S(1)}, bf16[80,32]{1,0:T(8,128)(2,1)S(1)}, u32[]{:S(2)}, u32[]{:S(2)}) collective-permute-start(bf16[80,32]{1,0:T(8,128)(2,1)S(1)} %pad.19), channel_id=1, source_target_pairs={{1,0},{2,1},{3,2},{0,3},{5,4},{6,5},{7,6},{4,7},{9,8},{10,9},{11,1... | collective-permute-start | bytes 15368 | tf_op jit(solution)/shard_map/ppermute | solution.py:269
  12.2 10.3 %copy-start.2 = (bf16[80,32]{1,0:T(8,128)(2,1)}, bf16[80,32]{1,0:T(8,128)(2,1)S(1)}, u32[]{:S(2)}) copy-start(bf16[80,32]{1,0:T(8,128)(2,1)S(1)} %collective-permute-done.hl_ref) | copy-start | bytes 15364
  12.2 10.2 %copy-start.3 = (bf16[80,32]{1,0:T(8,128)(2,1)}, bf16[80,32]{1,0:T(8,128)(2,1)S(1)}, u32[]{:S(2)}) copy-start(bf16[80,32]{1,0:T(8,128)(2,1)S(1)} %collective-permute-done.1.hr_ref) | copy-start | bytes 15364
  12.5 10.0 %collective-permute-start.2 = (bf16[80,514]{1,0:T(8,128)(2,1)S(1)}, bf16[80,514]{1,0:T(8,128)(2,1)S(1)}, u32[]{:S(2)}, u32[]{:S(2)}) collective-permute-start(bf16[80,514]{1,0:T(8,128)(2,1)S(1)} %fusion.3), channel_id=1, source_target_pairs={{0,4},{4,8},{8,12},{12,16},{16,20},{20,24},{24,28},{1,5},{5,9},{9,... | collective-permute-start | bytes 246728 | tf_op jit(solution)/shard_map/ppermute | solution.py:284
  16.7 6.6 %collective-permute-start.3 = (bf16[80,514]{1,0:T(8,128)(2,1)S(1)}, bf16[80,514]{1,0:T(8,128)(2,1)S(1)}, u32[]{:S(2)}, u32[]{:S(2)}) collective-permute-start(bf16[80,514]{1,0:T(8,128)(2,1)S(1)} %fusion.5), channel_id=1, source_target_pairs={{4,0},{8,4},{12,8},{16,12},{20,16},{24,20},{28,24},{5,1},{9,5},{13... | collective-permute-start | bytes 246728 | tf_op jit(solution)/shard_map/ppermute | solution.py:285
  22.5 0.7 copy-start.4
  23.2 0.6 copy-start.5
  62.4 1.9 %collective-permute-start.4 = (bf16[4,80,512]{2,1,0:T(8,128)(2,1)}, bf16[4,80,512]{2,1,0:T(8,128)(2,1)S(1)}, u32[]{:S(2)}, u32[]{:S(2)}) collective-permute-start(bf16[4,80,512]{2,1,0:T(8,128)(2,1)} %get-tuple-element.25), channel_id=1, source_target_pairs={{0,1},{1,0},{2,3},{3,2},{4,5},{5,4},{6,7},{7,6},{8,9},{9,8},{10,11... | collective-permute-start | bytes 983048 | tf_op jit(solution)/shard_map/ppermute | solution.py:327
  64.3 0.7 copy-start.1
  66.9 5.3 %collective-permute-start.5 = (bf16[1,80,512]{2,1,0:T(8,128)(2,1)}, bf16[1,80,512]{2,1,0:T(8,128)(2,1)S(1)}, u32[]{:S(2)}, u32[]{:S(2)}) collective-permute-start(bf16[1,80,512]{2,1,0:T(8,128)(2,1)} %get-tuple-element.27), channel_id=1, source_target_pairs={{0,4},{1,3},{2,6},{3,1},{4,0},{5,7},{6,2},{7,5},{8,12},{9,11},{10,... | collective-permute-start | bytes 245768 | tf_op jit(solution)/shard_map/ppermute | solution.py:327
  69.4 5.6 %collective-permute-start.6 = (bf16[1,80,512]{2,1,0:T(8,128)(2,1)}, bf16[1,80,512]{2,1,0:T(8,128)(2,1)S(1)}, u32[]{:S(2)}, u32[]{:S(2)}) collective-permute-start(bf16[1,80,512]{2,1,0:T(8,128)(2,1)} %get-tuple-element.28), channel_id=1, source_target_pairs={{0,2},{1,5},{2,0},{3,7},{4,6},{5,1},{6,4},{7,3},{8,10},{9,13},{10,... | collective-permute-start | bytes 245768 | tf_op jit(solution)/shard_map/ppermute | solution.py:327
  70.9 5.6 %collective-permute-start.7 = (bf16[1,80,512]{2,1,0:T(8,128)(2,1)}, bf16[1,80,512]{2,1,0:T(8,128)(2,1)S(1)}, u32[]{:S(2)}, u32[]{:S(2)}) collective-permute-start(bf16[1,80,512]{2,1,0:T(8,128)(2,1)} %get-tuple-element.29), channel_id=1, source_target_pairs={{0,6},{1,7},{2,4},{3,5},{4,2},{5,3},{6,0},{7,1},{8,14},{9,15},{10,... | collective-permute-start | bytes 245768 | tf_op jit(solution)/shard_map/ppermute | solution.py:327
  72.2 4.2 %copy-start.6 = (bf16[1,80,512]{2,1,0:T(8,128)(2,1)}, bf16[1,80,512]{2,1,0:T(8,128)(2,1)S(1)}, u32[]{:S(2)}) copy-start(bf16[1,80,512]{2,1,0:T(8,128)(2,1)S(1)} %collective-permute-done.5.refs_1_) | copy-start | bytes 245764
  75.0 1.5 %copy-start.7 = (bf16[1,80,512]{2,1,0:T(8,128)(2,1)}, bf16[1,80,512]{2,1,0:T(8,128)(2,1)S(1)}, u32[]{:S(2)}) copy-start(bf16[1,80,512]{2,1,0:T(8,128)(2,1)S(1)} %collective-permute-done.6.refs_2_) | copy-start | bytes 245764
  76.4 0.7 copy-start.9
  78.8 6.5 %collective-permute-start.10 = (bf16[1,80,512]{2,1,0:T(8,128)(2,1)}, bf16[1,80,512]{2,1,0:T(8,128)(2,1)S(1)}, u32[]{:S(2)}, u32[]{:S(2)}) collective-permute-start(bf16[1,80,512]{2,1,0:T(8,128)(2,1)} %shard_map.125.refs_0_), channel_id=1, source_target_pairs={{0,24},{1,25},{2,26},{3,27},{4,28},{5,29},{6,30},{7,31},{8,16},{9,... | collective-permute-start | bytes 245768 | tf_op jit(solution)/shard_map/ppermute | solution.py:327
  81.9 6.6 %collective-permute-start.9 = (bf16[1,80,512]{2,1,0:T(8,128)(2,1)}, bf16[1,80,512]{2,1,0:T(8,128)(2,1)S(1)}, u32[]{:S(2)}, u32[]{:S(2)}) collective-permute-start(bf16[1,80,512]{2,1,0:T(8,128)(2,1)} %shard_map.125.refs_0_), channel_id=1, source_target_pairs={{0,16},{1,17},{2,18},{3,19},{4,20},{5,21},{6,22},{7,23},{8,24},{9,... | collective-permute-start | bytes 245768 | tf_op jit(solution)/shard_map/ppermute | solution.py:327
  82.0 6.6 %collective-permute-start.8 = (bf16[1,80,512]{2,1,0:T(8,128)(2,1)}, bf16[1,80,512]{2,1,0:T(8,128)(2,1)S(1)}, u32[]{:S(2)}, u32[]{:S(2)}) collective-permute-start(bf16[1,80,512]{2,1,0:T(8,128)(2,1)} %shard_map.125.refs_0_), channel_id=1, source_target_pairs={{0,8},{1,9},{2,10},{3,11},{4,12},{5,13},{6,14},{7,15},{8,0},{9,1},... | collective-permute-start | bytes 245768 | tf_op jit(solution)/shard_map/ppermute | solution.py:327
  85.3 3.3 %copy-start.8 = (bf16[1,80,512]{2,1,0:T(8,128)(2,1)}, bf16[1,80,512]{2,1,0:T(8,128)(2,1)S(1)}, u32[]{:S(2)}) copy-start(bf16[1,80,512]{2,1,0:T(8,128)(2,1)S(1)} %collective-permute-done.10.refs_3_) | copy-start | bytes 245764
  88.5 0.6 copy-start.10
  89.2 0.6 copy-start.11
  91.5 5.5 %collective-permute-start.13 = (bf16[1,64,512]{2,1,0:T(8,128)(2,1)}, bf16[1,64,512]{2,1,0:T(8,128)(2,1)S(1)}, u32[]{:S(2)}, u32[]{:S(2)}) collective-permute-start(bf16[1,64,512]{2,1,0:T(8,128)(2,1)} %shard_map.126.refs_0_), channel_id=1, source_target_pairs={{0,6},{1,7},{2,4},{3,5},{4,2},{5,3},{6,0},{7,1},{8,14},{9,15},{10,... | collective-permute-start | bytes 196616 | tf_op jit(solution)/shard_map/ppermute | solution.py:327
  93.6 4.6 %collective-permute-start.12 = (bf16[1,64,512]{2,1,0:T(8,128)(2,1)}, bf16[1,64,512]{2,1,0:T(8,128)(2,1)S(1)}, u32[]{:S(2)}, u32[]{:S(2)}) collective-permute-start(bf16[1,64,512]{2,1,0:T(8,128)(2,1)} %shard_map.126.refs_0_), channel_id=1, source_target_pairs={{0,2},{1,5},{2,0},{3,7},{4,6},{5,1},{6,4},{7,3},{8,10},{9,13},{10,... | collective-permute-start | bytes 196616 | tf_op jit(solution)/shard_map/ppermute | solution.py:327
  94.1 4.5 %collective-permute-start.11 = (bf16[1,64,512]{2,1,0:T(8,128)(2,1)}, bf16[1,64,512]{2,1,0:T(8,128)(2,1)S(1)}, u32[]{:S(2)}, u32[]{:S(2)}) collective-permute-start(bf16[1,64,512]{2,1,0:T(8,128)(2,1)} %shard_map.126.refs_0_), channel_id=1, source_target_pairs={{0,4},{1,3},{2,6},{3,1},{4,0},{5,7},{6,2},{7,5},{8,12},{9,11},{10,... | collective-permute-start | bytes 196616 | tf_op jit(solution)/shard_map/ppermute | solution.py:327
  95.0 3.7 %collective-permute-start.14 = (bf16[1,64,512]{2,1,0:T(8,128)(2,1)}, bf16[1,64,512]{2,1,0:T(8,128)(2,1)S(1)}, u32[]{:S(2)}, u32[]{:S(2)}) collective-permute-start(bf16[1,64,512]{2,1,0:T(8,128)(2,1)} %shard_map.126.refs_0_), channel_id=1, source_target_pairs={{0,1},{1,0},{2,3},{3,2},{4,5},{5,4},{6,7},{7,6},{8,9},{9,8},{10,11... | collective-permute-start | bytes 196616 | tf_op jit(solution)/shard_map/ppermute | solution.py:327
  97.0 2.9 %copy-start.12 = (bf16[1,64,512]{2,1,0:T(8,128)(2,1)}, bf16[1,64,512]{2,1,0:T(8,128)(2,1)S(1)}, u32[]{:S(2)}) copy-start(bf16[1,64,512]{2,1,0:T(8,128)(2,1)S(1)} %collective-permute-done.13.refs_3_) | copy-start | bytes 196612
  97.0 1.7 %collective-permute-start.17 = (bf16[1,64,512]{2,1,0:T(8,128)(2,1)S(1)}, bf16[1,64,512]{2,1,0:T(8,128)(2,1)S(1)}, u32[]{:S(2)}, u32[]{:S(2)}) collective-permute-start(bf16[1,64,512]{2,1,0:T(8,128)(2,1)S(1)} %collective-permute-done.13.refs_3_), channel_id=1, source_target_pairs={{0,1},{1,0},{2,3},{3,2},{4,5},{5,4},{6,7},{7,6},{8,9},{9,8},{10,11... | collective-permute-start | bytes 196616 | tf_op jit(solution)/shard_map/ppermute | solution.py:327
  98.2 1.7 %copy-start.13 = (bf16[1,64,512]{2,1,0:T(8,128)(2,1)}, bf16[1,64,512]{2,1,0:T(8,128)(2,1)S(1)}, u32[]{:S(2)}) copy-start(bf16[1,64,512]{2,1,0:T(8,128)(2,1)S(1)} %collective-permute-done.12.refs_2_) | copy-start | bytes 196612
  98.2 1.3 %collective-permute-start.16 = (bf16[1,64,512]{2,1,0:T(8,128)(2,1)S(1)}, bf16[1,64,512]{2,1,0:T(8,128)(2,1)S(1)}, u32[]{:S(2)}, u32[]{:S(2)}) collective-permute-start(bf16[1,64,512]{2,1,0:T(8,128)(2,1)S(1)} %collective-permute-done.12.refs_2_), channel_id=1, source_target_pairs={{0,1},{1,0},{2,3},{3,2},{4,5},{5,4},{6,7},{7,6},{8,9},{9,8},{10,11... | collective-permute-start | bytes 196616 | tf_op jit(solution)/shard_map/ppermute | solution.py:327
  98.6 1.3 %copy-start.14 = (bf16[1,64,512]{2,1,0:T(8,128)(2,1)}, bf16[1,64,512]{2,1,0:T(8,128)(2,1)S(1)}, u32[]{:S(2)}) copy-start(bf16[1,64,512]{2,1,0:T(8,128)(2,1)S(1)} %collective-permute-done.11.refs_1_) | copy-start | bytes 196612
  98.6 1.3 %collective-permute-start.15 = (bf16[1,64,512]{2,1,0:T(8,128)(2,1)S(1)}, bf16[1,64,512]{2,1,0:T(8,128)(2,1)S(1)}, u32[]{:S(2)}, u32[]{:S(2)}) collective-permute-start(bf16[1,64,512]{2,1,0:T(8,128)(2,1)S(1)} %collective-permute-done.11.refs_1_), channel_id=1, source_target_pairs={{0,1},{1,0},{2,3},{3,2},{4,5},{5,4},{6,7},{7,6},{8,9},{9,8},{10,11... | collective-permute-start | bytes 196616 | tf_op jit(solution)/shard_map/ppermute | solution.py:327
  98.7 1.2 %copy-start.15 = (bf16[1,64,512]{2,1,0:T(8,128)(2,1)}, bf16[1,64,512]{2,1,0:T(8,128)(2,1)S(1)}, u32[]{:S(2)}) copy-start(bf16[1,64,512]{2,1,0:T(8,128)(2,1)S(1)} %collective-permute-done.14.refs_4_) | copy-start | bytes 196612
  98.7 1.2 %copy-start.16 = (bf16[1,64,512]{2,1,0:T(8,128)(2,1)}, bf16[1,64,512]{2,1,0:T(8,128)(2,1)S(1)}, u32[]{:S(2)}) copy-start(bf16[1,64,512]{2,1,0:T(8,128)(2,1)S(1)} %collective-permute-done.17.refs_7_) | copy-start | bytes 196612
  99.4 0.6 copy-start.17
  99.9 0.6 copy-start.18

commit v3 on v2

--- a/solution.py
+++ b/solution.py
@@ -52,6 +52,17 @@
     return hi, mid, lo
 
 
+def weights_kernel(w_ref, kv_ref, wt_ref, wvt_ref, pad_ref):
+    chan = w_ref.shape[0] // 16
+    width = w_ref.shape[1]
+    for k in range(16):
+        pad_ref[(k + 1) * CP - 16 : (k + 1) * CP] = jnp.zeros((16, width), f32)
+        pad_ref[k * CP : k * CP + chan] = w_ref[k * chan : (k + 1) * chan].astype(f32)
+    for k in range(0, 16 * CP, 256):
+        wt_ref[:, k : k + 256] = jnp.transpose(pad_ref[k : k + 256].astype(bf16))
+    wvt_ref[...] = jnp.transpose(kv_ref[:, width:])
+
+
 def query_kernel(gain_ref, latents_ref, lgain_ref, qw_ref, qz_ref):
     normed = (rows_norm(latents_ref[...], 1) * lgain_ref[...]).astype(bf16)
     query = jnp.dot(normed, qw_ref[...], preferred_element_type=f32).astype(bf16)
@@ -66,16 +77,22 @@
             qz_ref[h, j * HD : (j + 1) * HD, :] = part
 
 
+def places():
+    lon, lat = lax.axis_index("lon"), lax.axis_index("lat")
+    core, by, bx = lon & 1, (lon >> 1) & 1, lat & 1
+    yx, xy = 2 * by + bx, 2 * bx + by
+    return 4 * core + yx + core * (xy - yx), 4 * (1 - core) + xy + core * (yx - xy)
+
+
 def encode_kernel(
-    place_ref,
-    x_ref, hl_ref, hr_ref, top_ref, bot_ref, wt_ref, bias_ref, gain_ref, wk_ref, wvt_ref, qz_ref,
+    x_ref, hl_ref, hr_ref, top_ref, bot_ref, wt_ref, bias_ref, gain_ref, kv_ref, wvt_ref, qz_ref,
     tok_out, keep_ref, send_ref,
-    y_ref, xs_ref, st_ref, tok_ref, k_ref, vt_ref, s_ref, col_ref, sems,
+    y_ref, xs_ref, st_ref, tok_ref, k_ref, vt_ref, s_ref, col_ref, state_ref, peak_ref, side_ref, sems,
 ):
     chan, rows, cols = x_ref.shape
     half = cols // 2
     trows = rows // 2
-    width = wk_ref.shape[0]
+    width = kv_ref.shape[0]
     tokens = trows * half
     lat = qz_ref.shape[2]
 
@@ -88,27 +105,26 @@
             x = x_ref[16 * g : 16 * g + n, 16 * b : 16 * b + 16, :].reshape(n * 16, cols)
             y = jnp.dot(perm[:, : n * 16], x, preferred_element_type=f32).astype(bf16)
             y_ref[1 + 16 * b : 17 + 16 * b, 16 * g : 16 * g + 16, :] = y.reshape(16, 16, cols)
-    y_ref[0] = top_ref[:, :cols]
-    y_ref[rows + 1] = bot_ref[:, :cols]
+    y_ref[0] = top_ref[:CP]
+    y_ref[rows + 1] = bot_ref[:CP]
 
     ci = lax.broadcasted_iota(jnp.int32, (cols, cols), 0)
     cj = lax.broadcasted_iota(jnp.int32, (cols, cols), 1)
     want = jnp.where(cj < half, 2 * cj, 2 * (cj - half) + 1)
     select = jnp.where(ci == want, 1.0, 0.0).astype(bf16)
     lane = lax.broadcasted_iota(jnp.int32, (CP, half), 1)
-    left_all = hl_ref[...].astype(f32)
-    right_all = hr_ref[...].astype(f32)
-    edges = [top_ref[:, cols:].astype(f32), bot_ref[:, cols:].astype(f32)]
+    side_ref[...] = jnp.zeros(side_ref.shape, f32)
+    for n, ref in enumerate((hl_ref, hr_ref)):
+        side_ref[n, 1 : rows + 1] = ref[...].astype(f32)
+        for r, row in ((0, top_ref), (rows + 1, bot_ref)):
+            side_ref[n, r : r + 1] = row[CP + 16 * n : CP + 16 * n + 16, :128].astype(f32)[:1]
+    left_all, right_all = (jnp.transpose(side_ref[n])[:CP] for n in range(2))
     for p in range((rows + 2) // 2):
         pair = y_ref[2 * p : 2 * p + 2].reshape(2 * CP, cols)
         sel = jnp.dot(pair, select, preferred_element_type=f32)
         for q in range(2):
             r = 2 * p + q
-            if r == 0 or r == rows + 1:
-                e = edges[0 if r == 0 else 1]
-                left, right = e[:, 0:1], e[:, 1:2]
-            else:
-                left, right = left_all[:, r - 1 : r], right_all[:, r - 1 : r]
+            left, right = left_all[:, r : r + 1], right_all[:, r : r + 1]
             even = sel[q * CP : (q + 1) * CP, :half]
             odd = sel[q * CP : (q + 1) * CP, half:]
             first = jnp.where(lane == 0, left, pltpu.roll(odd, 1, 1))
@@ -136,7 +152,7 @@
         tok_ref[r] = tok
         pltpu.make_async_copy(tok_ref.at[r], tok_out.at[r], sems.at[r]).start()
         at = pl.ds(pl.multiple_of(r * half, half), half)
-        k_ref[at, :] = jnp.dot(tok, wk_ref[...], preferred_element_type=f32).astype(bf16)
+        k_ref[at, :] = jnp.dot(tok, kv_ref[:, :width], preferred_element_type=f32).astype(bf16)
         vt = jnp.dot(wvt_ref[...], tt, preferred_element_type=f32).astype(bf16)
         for h in range(HEADS):
             vt_ref[h * HR : h * HR + HD, at] = vt[h * HD : (h + 1) * HD]
@@ -162,9 +178,11 @@
         return jnp.max(s, axis=0, keepdims=True)
 
     chunks = tokens // CT
+    mine, other = places()
 
     def head_of(t):
-        return (t & (HEADS // 2 - 1)) ^ place_ref[t >> (HEADS.bit_length() - 2)]
+        late = t >> (HEADS.bit_length() - 2)
+        return (t & (HEADS // 2 - 1)) ^ (mine + late * (other - mine))
 
     def head(t, most):
         h = head_of(t)
@@ -182,22 +200,36 @@
             values = vt_ref[pl.ds(pl.multiple_of(h * HR, 16), HR), c * CT : (c + 1) * CT]
             state = state * fold + jnp.dot(values, weights, preferred_element_type=f32)
             peak, most = newpeak, following
-        total = state[HD : HD + 1]
-        packed = pack(state[:HD], total, peak)
-
-        @pl.when(t < HEADS // 2)
-        def _():
-            keep_ref[jnp.minimum(t, HEADS // 2 - 1)] = packed
-
-        @pl.when(t >= HEADS // 2)
-        def _():
-            send_ref[jnp.maximum(t - HEADS // 2, 0)] = packed
-
+        state_ref[t] = state
+        peak_ref[t] = peak
         return most
 
     lax.fori_loop(0, HEADS, head, produce(head_of(0), 0, 0))
+    for t in range(HEADS):
+        state = state_ref[t]
+        packed = pack(state[:HD], state[HD : HD + 1], peak_ref[t])
+        (keep_ref if t < HEADS // 2 else send_ref)[t % (HEADS // 2)] = packed
     for r in range(trows):
         pltpu.make_async_copy(tok_ref.at[r], tok_out.at[r], sems.at[r]).wait()
+
+
+def encode_scratch(rows, cols, width, lat):
+    half, trows = cols // 2, rows // 2
+    tokens = trows * half
+    return [
+        VMEM((rows + 2, CP, cols), bf16),
+        VMEM((rows + 2, 4 * CP, half), bf16),
+        VMEM((2, width, half), f32),
+        VMEM((trows, half, width), bf16),
+        VMEM((tokens, width), bf16),
+        VMEM((HEADS * HR, tokens), bf16),
+        VMEM((2, CT, lat), f32),
+        VMEM((2, width, 128), f32),
+        VMEM((HEADS, HR, lat), f32),
+        VMEM((HEADS, 1, lat), f32),
+        VMEM((2, 128, 128), f32),
+        pltpu.SemaphoreType.DMA((trows,)),
+    ]
 
 
 def pack(sums, total, peak):
@@ -225,25 +257,40 @@
     return sums_a * fold_a + sums_b * fold_b, total_a * fold_a + total_b * fold_b, peak
 
 
-def fold_kernel(a_ref, b_ref, *outs):
-    for n, out in enumerate(outs):
-        out[0] = pack(*combined(unpack(a_ref[n]), unpack(b_ref[n])))
-
-
-def group_kernel(*refs, last):
-    states = [unpack(ref[0]) for ref in refs[:-1]]
+def open_state(state):
+    tail = state[:, HD:].astype(f32)
+    total = (tail[:, 0:1] + tail[:, 1:2]) + tail[:, 2:3]
+    peak = (tail[:, 3:4] + tail[:, 4:5]) + tail[:, 5:6]
+    return state[:, :HD].astype(f32), total, peak
+
+
+def rounded(x):
+    return lax.reduce_precision(x, 8, 7)
+
+
+def closed_state(sums, total, peak):
+    parts = [sums]
+    for x in (total, peak):
+        hi = rounded(x)
+        mid = rounded(x - hi)
+        parts += [hi, mid, rounded((x - hi) - mid)]
+    parts.append(jnp.zeros((sums.shape[0], HR - HD - 6, sums.shape[2]), f32))
+    return jnp.concatenate(parts, 1).astype(bf16)
+
+
+def merged(states):
+    states = [open_state(x) for x in states]
     while len(states) > 1:
         states = [combined(*states[n : n + 2]) for n in range(0, len(states), 2)]
-    sums, total, peak = states[0]
-    refs[-1][0] = (sums / total).astype(bf16) if last else pack(sums, total, peak)
-
-
-def out_kernel(place_ref, *refs):
+    return states[0]
+
+
+def out_kernel(*refs):
     parts, (wo_ref, gain_ref, out_ref, all_ref) = refs[:HEADS], refs[HEADS:]
-    half = HEADS // 2
+    half, place = HEADS // 2, places()
     for t in range(HEADS):
         value = parts[t][0]
-        h = (t % half) ^ place_ref[t // half]
+        h = (t % half) ^ place[t // half]
         all_ref[pl.ds(pl.multiple_of(h * HD, HD), HD), :] = value.astype(f32)
     attended = jnp.transpose(all_ref[...]).astype(bf16)
     mixed = jnp.dot(attended, wo_ref[...], preferred_element_type=f32)
@@ -262,20 +309,25 @@
     half = cols // 2
     trows = rows // 2
 
-    extra = ((0, CP - chan), (0, 0))
     ahead = [(i, (i + 1) % nlon) for i in range(nlon)]
     back = [(t, s) for s, t in ahead]
-    hl = lax.ppermute(jnp.pad(field[:, :, cols - 1], extra), "lon", ahead)
-    hr = lax.ppermute(jnp.pad(field[:, :, 0], extra), "lon", back)
-
-    wt = stem_weight.reshape(16, chan, width)
-    wt = jnp.pad(wt, ((0, 0), (0, CP - chan), (0, 0))).reshape(16 * CP, width).T
-    wk = kv_weight[:, :width]
-    wvt = kv_weight[:, width:].T
+
+    def side(c):
+        return jnp.pad(field[:, :, c].T, ((0, 0), (0, 128 - chan)))
+
+    hl = lax.ppermute(side(cols - 1), "lon", ahead)
+    hr = lax.ppermute(side(0), "lon", back)
+    wt, wvt = call(
+        weights_kernel,
+        [shape((width, 16 * CP), bf16), shape((width, width), bf16)],
+        2,
+        scratch=[VMEM((16 * CP, width), f32)],
+    )(stem_weight, kv_weight)
     hl, hr, wt, wvt = lax.optimization_barrier((hl, hr, wt, wvt))
 
     def edge(r):
-        return jnp.concatenate([jnp.pad(field[:, r, :], extra), hl[:, r : r + 1], hr[:, r : r + 1]], 1)
+        corners = [jnp.pad(h[r : r + 1], ((0, 15), (0, cols - 128))) for h in (hl, hr)]
+        return jnp.concatenate([jnp.pad(field[:, r, :], ((0, CP - chan), (0, 0)))] + corners)
 
     low, high = edge(rows - 1), edge(0)
     low, high, latents = lax.optimization_barrier((low, high, latents))
@@ -287,34 +339,14 @@
         head_gain, latents, latent_gain[None, :], query_weight
     )
 
-    core = lax.axis_index("lon") & 1
-    by = (lax.axis_index("lon") >> 1) & 1
-    bx = lax.axis_index("lat") & 1
-    yx, xy = 2 * by + bx, 2 * bx + by
-    mine = 4 * core + jnp.where(core == 0, yx, xy)
-    other = 4 * (1 - core) + jnp.where(core == 0, xy, yx)
-    place = jnp.stack([mine, other]).astype(jnp.int32)
-
-    tokens = trows * half
     state = shape((HEADS // 2, HR, lat), bf16)
     tok, keep, send = call(
         encode_kernel,
         [shape((trows, half, width), bf16), state, state],
         11,
-        smem=1,
         out_spaces=[pl.ANY, VMEM, VMEM],
-        scratch=[
-            VMEM((rows + 2, CP, cols), bf16),
-            VMEM((rows + 2, 4 * CP, half), bf16),
-            VMEM((2, width, half), f32),
-            VMEM((trows, half, width), bf16),
-            VMEM((tokens, width), bf16),
-            VMEM((HEADS * HR, tokens), bf16),
-            VMEM((2, CT, lat), f32),
-            VMEM((2, width, 128), f32),
-            pltpu.SemaphoreType.DMA((trows,)),
-        ],
-    )(place, field, hl, hr, top, bot, wt, stem_bias[None, :], token_gain[None, :], wk, wvt, qz)
+        scratch=encode_scratch(rows, cols, width, lat),
+    )(field, hl, hr, top, bot, wt, stem_bias[None, :], token_gain[None, :], kv_weight, wvt, qz)
 
     def swap(x, flips0, flips1):
         pairs = []
@@ -336,20 +368,19 @@
     far += [("lon", 1 << n) for n in range(2, nlon.bit_length() - 1)]
     groups = [far[n : n + 2] for n in range(0, len(far), 2)]
 
-    one = shape((1, HR, lat), bf16)
-    own, *others = call(fold_kernel, [one] * (HEADS // 2), 2)(keep, swap(send, cores, cores))
+    four = closed_state(*merged([keep, swap(send, cores, cores)]))
+    own, *others = (four[n : n + 1] for n in range(HEADS // 2))
     states = [own] + [swap(x, *flips) for x, flips in zip(others, near)]
-    own = call(functools.partial(group_kernel, last=False), one, 4)(*states)
-    for n, bits in enumerate(groups):
-        last = n == len(groups) - 1
+    for bits in groups:
+        own = closed_state(*merged(states))
         states = [own] + [swap(own, flips, flips) for flips in subsets(bits)]
-        out = shape((1, HD, lat), bf16) if last else one
-        own = call(functools.partial(group_kernel, last=last), out, len(states))(*states)
+    sums, total, _ = merged(states)
+    own = (sums / total).astype(bf16)
     parts = [own] + [swap(own, *flips) for flips in near]
     parts += [swap(x, cores, cores) for x in parts]
     latent_out = call(
-        out_kernel, shape((lat, width), f32), HEADS + 2, smem=1, scratch=[VMEM((width, lat), f32)]
-    )(place, *parts, out_weight, out_gain[None, :])
+        out_kernel, shape((lat, width), f32), HEADS + 2, scratch=[VMEM((width, lat), f32)]
+    )(*parts, out_weight, out_gain[None, :])
     return (tok, latent_out)
 
 

time: 104 us -> 98 us (0.942)
  local copies, waits for them, and re-layouts: 12.9 us -> 6.66 us
  Pallas kernels: 50.6 us -> 48.7 us
  other arithmetic: 0.81 us -> 2.43 us
    unnamed x41 -> x28, local copies, waits for them, and re-layouts: 5.89 us -> 2.68 us
    reshape x2 -> x0, local copies, waits for them, and re-layouts: 2.89 us -> none  [the longest x1 1.46 us: shards(): wt = jnp.pad(wt, ((0, 0), (0, CP - chan), (0, 0))).reshape(16 * CP, width).T]
    pallas_call x4 -> x2, Pallas kernels: 8.47 us -> 6.27 us  [the longest x1 3.21 us: shards(): call(weights_kernel, [shape((width, 16 * CP), bf16), shape((width, width)...]
  transfers between devices with their start and end apart: 18 -> 18, of which waited for: 12 -> 11; matrix products, arithmetic and copies ran while one was open for 7% -> 3% of each run, Pallas kernels for 4% -> 7%
where the time goes in v3:
time: 98 us; the launch traced here: 97.6 us
  Pallas kernels  48.7 us (50%)
  starting transfers between devices  20.4 us (21%)
  waiting for transfers between devices  18.5 us (19%)
  local copies, waits for them, and re-layouts  6.66 us (7%)
  other arithmetic  2.43 us (2%)
    pallas_call x1, Pallas kernels, shards(): call(encode_kernel, [shape((trows, half, width), bf16), state, state], 11...  38.7 us
    ppermute x14, waiting for transfers between devices, swap(): return lax.ppermute(x, ('lat', 'lon'), pairs)  16.9 us
    ppermute x14, starting transfers between devices, swap(): return lax.ppermute(x, ('lat', 'lon'), pairs)  12.3 us
    ppermute x1, starting transfers between devices, shards(): top = lax.ppermute(low, 'lat', up)  4.17 us
    pallas_call x1, Pallas kernels, shards(): call(query_kernel, shape((HEADS, 4 * HD, lat), bf16), 3, smem=1)  3.68 us
    pallas_call x1, Pallas kernels, shards(): call(weights_kernel, [shape((width, 16 * CP), bf16), shape((width, width)...  3.21 us
    pallas_call x1, Pallas kernels, shards(): call(out_kernel, shape((lat, width), f32), HEADS + 2, scratch=[VMEM((widt...  3.06 us
    unnamed x28, local copies, waits for them, and re-layouts  2.68 us
  transfers between devices with their start and end apart: 18, of which 11 were waited for; matrix products, arithmetic and copies ran while one was open for 3% of the time, Pallas kernels for 7%

profile of v3, /device:TPU:0, one launch (start us, length us, event | category | flops | bytes accessed | tf_op | source)
XLA Modules:
  0.0 97.6 jit_solution(16604896093257592847)
XLA Ops:
  0.6 1.5 %fusion.42 = (bf16[69,32,1]{2,1,0:T(8,128)(2,1)S(1)}, bf16[69,32,1]{2,1,0:T(8,128)(2,1)S(1)}) fusion(bf16[69,32,512]{2,1,0:T(8,128)(2,1)} %x_ref.1), kind=kLoop, calls=%fused_computation.132 | loop fusion | bytes 17664 | tf_op jit(solution)/shard_map/slice | solution.py:316
  2.1 0.7 copy.23
  2.8 0.5 collective-permute-start
  3.4 0.7 copy.24
  4.1 2.0 %collective-permute-start.1 = (bf16[32,128]{1,0:T(8,128)(2,1)S(1)}, bf16[32,128]{1,0:T(8,128)(2,1)S(1)}, u32[]{:S(2)}, u32[]{:S(2)}) collective-permute-start(bf16[32,128]{1,0:T(8,128)(2,1)S(1)} %pad.28), channel_id=1, source_target_pairs={{1,0},{2,1},{3,2},{0,3},{5,4},{6,5},{7,6},{4,7},{9,8},{10,9},{11,1... | collective-permute-start | bytes 24584 | tf_op jit(solution)/shard_map/ppermute | solution.py:319
  6.1 1.5 %fusion.41 = (bf16[69,1,512]{2,1,0:T(2,128)(2,1)S(1)}, bf16[69,1,512]{2,1,0:T(2,128)(2,1)S(1)}) fusion(bf16[69,32,512]{2,1,0:T(8,128)(2,1)} %x_ref.1), kind=kLoop, calls=%fused_computation.131 | loop fusion | bytes 282624 | tf_op jit(solution)/shard_map/slice | solution.py:330
  7.6 3.2 %shard_map.122 = (bf16[512,1280]{1,0:T(8,128)(2,1)}, bf16[512,512]{1,0:T(8,128)(2,1)}) custom-call(bf16[1104,512]{1,0:T(8,128)(2,1)} %w_ref.1, bf16[512,1024]{1,0:T(8,128)(2,1)} %kv_ref.3), custom_call_target="tpu_custom_call" | custom-call | tf_op jit(solution)/shard_map/pallas_call | solution.py:320
  10.8 0.0 collective-permute-done.hl_ref
  10.8 0.0 collective-permute-done.1.hr_ref
  10.8 0.0 copy-start.11
  10.9 4.2 %collective-permute-start.2 = (bf16[112,512]{1,0:T(8,128)(2,1)S(1)}, bf16[112,512]{1,0:T(8,128)(2,1)S(1)}, u32[]{:S(2)}, u32[]{:S(2)}) collective-permute-start(bf16[112,512]{1,0:T(8,128)(2,1)S(1)} %fusion.8), channel_id=1, source_target_pairs={{0,4},{4,8},{8,12},{12,16},{16,20},{20,24},{24,28},{1,5},{5,9},{9,... | collective-permute-start | bytes 344072 | tf_op jit(solution)/shard_map/ppermute | solution.py:336
  15.0 1.5 %collective-permute-start.3 = (bf16[112,512]{1,0:T(8,128)(2,1)S(1)}, bf16[112,512]{1,0:T(8,128)(2,1)S(1)}, u32[]{:S(2)}, u32[]{:S(2)}) collective-permute-start(bf16[112,512]{1,0:T(8,128)(2,1)S(1)} %fusion.10), channel_id=1, source_target_pairs={{4,0},{8,4},{12,8},{16,12},{20,16},{24,20},{28,24},{5,1},{9,5},{13... | collective-permute-start | bytes 344072 | tf_op jit(solution)/shard_map/ppermute | solution.py:337
  16.5 3.7 %shard_map.123.qz_ref = bf16[8,256,512]{2,1,0:T(8,128)(2,1)} custom-call(f32[8]{0:T(128)} %gain_ref.1, f32[512,512]{1,0:T(8,128)} %latents_ref, f32[1,512]{1,0:T(1,128)} %bitcast.50, bf16[512,512]{1,0:T(8,128)(2,1)} %qw_ref.1), custom_call_target="tpu_custom_call" | custom-call | tf_op jit(solution)/shard_map/pallas_call | solution.py:338
  20.2 0.0 collective-permute-done.2.top_ref
  20.2 1.5 %collective-permute-done.3.bot_ref = bf16[112,512]{1,0:T(8,128)(2,1)S(1)} collective-permute-done((bf16[112,512]{1,0:T(8,128)(2,1)S(1)}, bf16[112,512]{1,0:T(8,128)(2,1)S(1)}, u32[]{:S(2)}, u32[]{:S(2)}) %collective-permute-start.3) | collective-permute-done | bytes 114720 | tf_op jit(solution)/shard_map/ppermute | solution.py:337
  21.7 0.0 copy-done.10
  21.7 0.0 copy-done.11
  21.7 0.0 copy-done.1
  21.7 0.6 copy-done.2
  22.4 38.7 %shard_map.124 = (bf16[16,256,512]{2,1,0:T(8,128)(2,1)}, bf16[4,80,512]{2,1,0:T(8,128)(2,1)}, bf16[4,80,512]{2,1,0:T(8,128)(2,1)}) custom-call(bf16[69,32,512]{2,1,0:T(8,128)(2,1)} %x_ref.1, bf16[32,128]{1,0:T(8,128)(2,1)} %copy-done.10, bf16[32,128]{1,0:T(8,128)(2,1)} %copy-done.11, bf16[112,512]{1,0:T(8,128)(2,1)} %copy-done.1, ...), custom_call_target="tpu_custom_call" | custom-call | tf_op jit(solution)/shard_map/pallas_call | solution.py:343
  61.1 0.1 collective-permute-start.4
  61.2 0.9 slice_convert_fusion.1
  62.0 1.0 collective-permute-done.4
  63.0 0.1 fusion.14
  63.1 0.1 reduce-precision_convert_fusion
  63.2 0.3 concatenate.30
  63.5 1.1 %add_convert_fusion = bf16[4,64,512]{2,1,0:T(8,128)(2,1)S(1)} fusion(bf16[4,80,512]{2,1,0:T(8,128)(2,1)S(1)} %collective-permute-done.4, f32[4,512]{1,0:T(4,128)S(1)} %bitcast.33, f32[4,512]{1,0:T(4,128)S(1)} %bitcast.34, bf16[4,80,512]{2,1,0:T(8,128)(2,1)} %get-tuple-element.24), kind=kLoop, calls=%fused_computation | loop fusion | flops 786432 | bytes 802816 | tf_op jit(solution)/shard_map/convert.8
  64.6 0.4 concatenate.31
  65.0 3.5 %collective-permute-start.7 = (bf16[1,80,512]{2,1,0:T(8,128)(2,1)S(1)}, bf16[1,80,512]{2,1,0:T(8,128)(2,1)S(1)}, u32[]{:S(2)}, u32[]{:S(2)}) collective-permute-start(bf16[1,80,512]{2,1,0:T(8,128)(2,1)S(1)} %get-tuple-element.59), channel_id=1, source_target_pairs={{0,6},{1,7},{2,4},{3,5},{4,2},{5,3},{6,0},{7,1},{8,14},{9,15},{10,... | collective-permute-start | bytes 245768 | tf_op jit(solution)/shard_map/ppermute | solution.py:359
  68.4 0.5 collective-permute-start.6
  68.9 0.2 collective-permute-start.5
  69.1 2.4 %collective-permute-done.7 = bf16[1,80,512]{2,1,0:T(8,128)(2,1)S(1)} collective-permute-done((bf16[1,80,512]{2,1,0:T(8,128)(2,1)S(1)}, bf16[1,80,512]{2,1,0:T(8,128)(2,1)S(1)}, u32[]{:S(2)}, u32[]{:S(2)}) %collective-permute-start.7) | collective-permute-done | bytes 81952 | tf_op jit(solution)/shard_map/ppermute | solution.py:359
  71.5 1.5 %collective-permute-done.6 = bf16[1,80,512]{2,1,0:T(8,128)(2,1)S(1)} collective-permute-done((bf16[1,80,512]{2,1,0:T(8,128)(2,1)S(1)}, bf16[1,80,512]{2,1,0:T(8,128)(2,1)S(1)}, u32[]{:S(2)}, u32[]{:S(2)}) %collective-permute-start.6) | collective-permute-done | bytes 81952 | tf_op jit(solution)/shard_map/ppermute | solution.py:359
  73.0 0.4 collective-permute-done.5
  73.4 0.1 reduce-precision_convert_fusion.4
  73.5 0.1 add_convert_fusion.1
  73.6 0.2 concatenate.33
  73.8 3.3 %collective-permute-start.10 = (bf16[1,80,512]{2,1,0:T(8,128)(2,1)S(1)}, bf16[1,80,512]{2,1,0:T(8,128)(2,1)S(1)}, u32[]{:S(2)}, u32[]{:S(2)}) collective-permute-start(bf16[1,80,512]{2,1,0:T(8,128)(2,1)S(1)} %concatenate.33), channel_id=1, source_target_pairs={{0,24},{1,25},{2,26},{3,27},{4,28},{5,29},{6,30},{7,31},{8,16},{9,... | collective-permute-start | bytes 245768 | tf_op jit(solution)/shard_map/ppermute | solution.py:359
  77.1 0.2 concatenate.32
  77.2 0.1 collective-permute-start.9
  77.3 1.1 %collective-permute-start.8 = (bf16[1,80,512]{2,1,0:T(8,128)(2,1)S(1)}, bf16[1,80,512]{2,1,0:T(8,128)(2,1)S(1)}, u32[]{:S(2)}, u32[]{:S(2)}) collective-permute-start(bf16[1,80,512]{2,1,0:T(8,128)(2,1)S(1)} %concatenate.33), channel_id=1, source_target_pairs={{0,8},{1,9},{2,10},{3,11},{4,12},{5,13},{6,14},{7,15},{8,0},{9,1},... | collective-permute-start | bytes 245768 | tf_op jit(solution)/shard_map/ppermute | solution.py:359
  78.5 2.4 %collective-permute-done.10 = bf16[1,80,512]{2,1,0:T(8,128)(2,1)S(1)} collective-permute-done((bf16[1,80,512]{2,1,0:T(8,128)(2,1)S(1)}, bf16[1,80,512]{2,1,0:T(8,128)(2,1)S(1)}, u32[]{:S(2)}, u32[]{:S(2)}) %collective-permute-start.10) | collective-permute-done | bytes 81952 | tf_op jit(solution)/shard_map/ppermute | solution.py:359
  80.9 3.3 %collective-permute-done.9 = bf16[1,80,512]{2,1,0:T(8,128)(2,1)S(1)} collective-permute-done((bf16[1,80,512]{2,1,0:T(8,128)(2,1)S(1)}, bf16[1,80,512]{2,1,0:T(8,128)(2,1)S(1)}, u32[]{:S(2)}, u32[]{:S(2)}) %collective-permute-start.9) | collective-permute-done | bytes 81952 | tf_op jit(solution)/shard_map/ppermute | solution.py:359
  84.2 0.0 collective-permute-done.8
  84.2 0.1 multiply_add_fusion
  84.3 0.1 divide_convert_fusion.refs_0_
  84.3 0.0 copy-start
  84.3 1.8 %collective-permute-start.11 = (bf16[1,64,512]{2,1,0:T(8,128)(2,1)S(1)}, bf16[1,64,512]{2,1,0:T(8,128)(2,1)S(1)}, u32[]{:S(2)}, u32[]{:S(2)}) collective-permute-start(bf16[1,64,512]{2,1,0:T(8,128)(2,1)S(1)} %divide_convert_fusion.refs_0_), channel_id=1, source_target_pairs={{0,4},{1,3},{2,6},{3,1},{4,0},{5,7},{6,2},{7,5},{8,12},{9,11},{10,... | collective-permute-start | bytes 196616 | tf_op jit(solution)/shard_map/ppermute | solution.py:359
  86.1 1.4 %collective-permute-start.12 = (bf16[1,64,512]{2,1,0:T(8,128)(2,1)S(1)}, bf16[1,64,512]{2,1,0:T(8,128)(2,1)S(1)}, u32[]{:S(2)}, u32[]{:S(2)}) collective-permute-start(bf16[1,64,512]{2,1,0:T(8,128)(2,1)S(1)} %divide_convert_fusion.refs_0_), channel_id=1, source_target_pairs={{0,2},{1,5},{2,0},{3,7},{4,6},{5,1},{6,4},{7,3},{8,10},{9,13},{10,... | collective-permute-start | bytes 196616 | tf_op jit(solution)/shard_map/ppermute | solution.py:359
  87.5 0.4 collective-permute-start.13
  87.9 0.0 collective-permute-start.14
  87.9 1.5 %collective-permute-done.11.refs_1_ = bf16[1,64,512]{2,1,0:T(8,128)(2,1)S(1)} collective-permute-done((bf16[1,64,512]{2,1,0:T(8,128)(2,1)S(1)}, bf16[1,64,512]{2,1,0:T(8,128)(2,1)S(1)}, u32[]{:S(2)}, u32[]{:S(2)}) %collective-permute-start.11) | collective-permute-done | bytes 65568 | tf_op jit(solution)/shard_map/ppermute | solution.py:359
  89.4 0.0 collective-permute-start.15
  89.4 1.7 %collective-permute-done.12.refs_2_ = bf16[1,64,512]{2,1,0:T(8,128)(2,1)S(1)} collective-permute-done((bf16[1,64,512]{2,1,0:T(8,128)(2,1)S(1)}, bf16[1,64,512]{2,1,0:T(8,128)(2,1)S(1)}, u32[]{:S(2)}, u32[]{:S(2)}) %collective-permute-start.12) | collective-permute-done | bytes 65568 | tf_op jit(solution)/shard_map/ppermute | solution.py:359
  91.1 0.0 collective-permute-start.16
  91.1 1.6 %collective-permute-done.13.refs_3_ = bf16[1,64,512]{2,1,0:T(8,128)(2,1)S(1)} collective-permute-done((bf16[1,64,512]{2,1,0:T(8,128)(2,1)S(1)}, bf16[1,64,512]{2,1,0:T(8,128)(2,1)S(1)}, u32[]{:S(2)}, u32[]{:S(2)}) %collective-permute-start.13) | collective-permute-done | bytes 65568 | tf_op jit(solution)/shard_map/ppermute | solution.py:359
  92.7 0.0 collective-permute-start.17
  92.7 0.0 collective-permute-done.14.refs_4_
  92.7 0.0 collective-permute-done.15.refs_5_
  92.7 0.0 copy-start.7
  92.7 0.0 collective-permute-done.16.refs_6_
  92.8 1.2 %collective-permute-done.17.refs_7_ = bf16[1,64,512]{2,1,0:T(8,128)(2,1)S(1)} collective-permute-done((bf16[1,64,512]{2,1,0:T(8,128)(2,1)S(1)}, bf16[1,64,512]{2,1,0:T(8,128)(2,1)S(1)}, u32[]{:S(2)}, u32[]{:S(2)}) %collective-permute-start.17) | collective-permute-done | bytes 65568 | tf_op jit(solution)/shard_map/ppermute | solution.py:359
  94.0 0.6 copy-done.9
  94.6 3.1 %shard_map.125 = f32[512,512]{1,0:T(8,128)} custom-call(bf16[1,64,512]{2,1,0:T(8,128)(2,1)} %copy-done, bf16[1,64,512]{2,1,0:T(8,128)(2,1)} %copy-done.3, bf16[1,64,512]{2,1,0:T(8,128)(2,1)} %copy-done.4, bf16[1,64,512]{2,1,0:T(8,128)(2,1)} %copy-done.5, bf16[1,64,512]{2,1,0:T(8,128)(2,1)} %copy-done.6, bf16[1,64,512]{2,1,0:T(8,128)(2,1)} %copy-done.7, ...), custom_call_target="tpu_custom_call" | custom-call | tf_op jit(solution)/shard_map/pallas_call | solution.py:381
  (39 shorter events, 0.2 us)
Async XLA Ops:
  2.8 8.0 %collective-permute-start = (bf16[32,128]{1,0:T(8,128)(2,1)S(1)}, bf16[32,128]{1,0:T(8,128)(2,1)S(1)}, u32[]{:S(2)}, u32[]{:S(2)}) collective-permute-start(bf16[32,128]{1,0:T(8,128)(2,1)S(1)} %pad.27), channel_id=1, source_target_pairs={{0,1},{1,2},{2,3},{3,0},{4,5},{5,6},{6,7},{7,4},{8,9},{9,10},{10,1... | collective-permute-start | bytes 24584 | tf_op jit(solution)/shard_map/ppermute | solution.py:318
  4.1 6.7 %collective-permute-start.1 = (bf16[32,128]{1,0:T(8,128)(2,1)S(1)}, bf16[32,128]{1,0:T(8,128)(2,1)S(1)}, u32[]{:S(2)}, u32[]{:S(2)}) collective-permute-start(bf16[32,128]{1,0:T(8,128)(2,1)S(1)} %pad.28), channel_id=1, source_target_pairs={{1,0},{2,1},{3,2},{0,3},{5,4},{6,5},{7,6},{4,7},{9,8},{10,9},{11,1... | collective-permute-start | bytes 24584 | tf_op jit(solution)/shard_map/ppermute | solution.py:319
  10.8 10.9 %copy-start.10 = (bf16[32,128]{1,0:T(8,128)(2,1)}, bf16[32,128]{1,0:T(8,128)(2,1)S(1)}, u32[]{:S(2)}) copy-start(bf16[32,128]{1,0:T(8,128)(2,1)S(1)} %collective-permute-done.hl_ref) | copy-start | bytes 24580
  10.8 10.9 %copy-start.11 = (bf16[32,128]{1,0:T(8,128)(2,1)}, bf16[32,128]{1,0:T(8,128)(2,1)S(1)}, u32[]{:S(2)}) copy-start(bf16[32,128]{1,0:T(8,128)(2,1)S(1)} %collective-permute-done.1.hr_ref) | copy-start | bytes 24580
  10.9 9.3 %collective-permute-start.2 = (bf16[112,512]{1,0:T(8,128)(2,1)S(1)}, bf16[112,512]{1,0:T(8,128)(2,1)S(1)}, u32[]{:S(2)}, u32[]{:S(2)}) collective-permute-start(bf16[112,512]{1,0:T(8,128)(2,1)S(1)} %fusion.8), channel_id=1, source_target_pairs={{0,4},{4,8},{8,12},{12,16},{16,20},{20,24},{24,28},{1,5},{5,9},{9,... | collective-permute-start | bytes 344072 | tf_op jit(solution)/shard_map/ppermute | solution.py:336
  15.0 6.7 %collective-permute-start.3 = (bf16[112,512]{1,0:T(8,128)(2,1)S(1)}, bf16[112,512]{1,0:T(8,128)(2,1)S(1)}, u32[]{:S(2)}, u32[]{:S(2)}) collective-permute-start(bf16[112,512]{1,0:T(8,128)(2,1)S(1)} %fusion.10), channel_id=1, source_target_pairs={{4,0},{8,4},{12,8},{16,12},{20,16},{24,20},{28,24},{5,1},{9,5},{13... | collective-permute-start | bytes 344072 | tf_op jit(solution)/shard_map/ppermute | solution.py:337
  20.2 1.5 %copy-start.1 = (bf16[112,512]{1,0:T(8,128)(2,1)}, bf16[112,512]{1,0:T(8,128)(2,1)S(1)}, u32[]{:S(2)}) copy-start(bf16[112,512]{1,0:T(8,128)(2,1)S(1)} %collective-permute-done.2.top_ref) | copy-start | bytes 344068
  21.7 0.6 copy-start.2
  61.1 1.9 %collective-permute-start.4 = (bf16[4,80,512]{2,1,0:T(8,128)(2,1)}, bf16[4,80,512]{2,1,0:T(8,128)(2,1)S(1)}, u32[]{:S(2)}, u32[]{:S(2)}) collective-permute-start(bf16[4,80,512]{2,1,0:T(8,128)(2,1)} %get-tuple-element.25), channel_id=1, source_target_pairs={{0,1},{1,0},{2,3},{3,2},{4,5},{5,4},{6,7},{7,6},{8,9},{9,8},{10,11... | collective-permute-start | bytes 983048 | tf_op jit(solution)/shard_map/ppermute | solution.py:359
  65.0 6.6 %collective-permute-start.7 = (bf16[1,80,512]{2,1,0:T(8,128)(2,1)S(1)}, bf16[1,80,512]{2,1,0:T(8,128)(2,1)S(1)}, u32[]{:S(2)}, u32[]{:S(2)}) collective-permute-start(bf16[1,80,512]{2,1,0:T(8,128)(2,1)S(1)} %get-tuple-element.59), channel_id=1, source_target_pairs={{0,6},{1,7},{2,4},{3,5},{4,2},{5,3},{6,0},{7,1},{8,14},{9,15},{10,... | collective-permute-start | bytes 245768 | tf_op jit(solution)/shard_map/ppermute | solution.py:359
  68.4 4.6 %collective-permute-start.6 = (bf16[1,80,512]{2,1,0:T(8,128)(2,1)S(1)}, bf16[1,80,512]{2,1,0:T(8,128)(2,1)S(1)}, u32[]{:S(2)}, u32[]{:S(2)}) collective-permute-start(bf16[1,80,512]{2,1,0:T(8,128)(2,1)S(1)} %get-tuple-element.60), channel_id=1, source_target_pairs={{0,2},{1,5},{2,0},{3,7},{4,6},{5,1},{6,4},{7,3},{8,10},{9,13},{10,... | collective-permute-start | bytes 245768 | tf_op jit(solution)/shard_map/ppermute | solution.py:359
  68.9 4.4 %collective-permute-start.5 = (bf16[1,80,512]{2,1,0:T(8,128)(2,1)S(1)}, bf16[1,80,512]{2,1,0:T(8,128)(2,1)S(1)}, u32[]{:S(2)}, u32[]{:S(2)}) collective-permute-start(bf16[1,80,512]{2,1,0:T(8,128)(2,1)S(1)} %get-tuple-element.58), channel_id=1, source_target_pairs={{0,4},{1,3},{2,6},{3,1},{4,0},{5,7},{6,2},{7,5},{8,12},{9,11},{10,... | collective-permute-start | bytes 245768 | tf_op jit(solution)/shard_map/ppermute | solution.py:359
  73.8 7.1 %collective-permute-start.10 = (bf16[1,80,512]{2,1,0:T(8,128)(2,1)S(1)}, bf16[1,80,512]{2,1,0:T(8,128)(2,1)S(1)}, u32[]{:S(2)}, u32[]{:S(2)}) collective-permute-start(bf16[1,80,512]{2,1,0:T(8,128)(2,1)S(1)} %concatenate.33), channel_id=1, source_target_pairs={{0,24},{1,25},{2,26},{3,27},{4,28},{5,29},{6,30},{7,31},{8,16},{9,... | collective-permute-start | bytes 245768 | tf_op jit(solution)/shard_map/ppermute | solution.py:359
  77.2 6.9 %collective-permute-start.9 = (bf16[1,80,512]{2,1,0:T(8,128)(2,1)S(1)}, bf16[1,80,512]{2,1,0:T(8,128)(2,1)S(1)}, u32[]{:S(2)}, u32[]{:S(2)}) collective-permute-start(bf16[1,80,512]{2,1,0:T(8,128)(2,1)S(1)} %concatenate.33), channel_id=1, source_target_pairs={{0,16},{1,17},{2,18},{3,19},{4,20},{5,21},{6,22},{7,23},{8,24},{9,... | collective-permute-start | bytes 245768 | tf_op jit(solution)/shard_map/ppermute | solution.py:359
  77.3 6.8 %collective-permute-start.8 = (bf16[1,80,512]{2,1,0:T(8,128)(2,1)S(1)}, bf16[1,80,512]{2,1,0:T(8,128)(2,1)S(1)}, u32[]{:S(2)}, u32[]{:S(2)}) collective-permute-start(bf16[1,80,512]{2,1,0:T(8,128)(2,1)S(1)} %concatenate.33), channel_id=1, source_target_pairs={{0,8},{1,9},{2,10},{3,11},{4,12},{5,13},{6,14},{7,15},{8,0},{9,1},... | collective-permute-start | bytes 245768 | tf_op jit(solution)/shard_map/ppermute | solution.py:359
  84.3 9.6 %copy-start = (bf16[1,64,512]{2,1,0:T(8,128)(2,1)}, bf16[1,64,512]{2,1,0:T(8,128)(2,1)S(1)}, u32[]{:S(2)}) copy-start(bf16[1,64,512]{2,1,0:T(8,128)(2,1)S(1)} %divide_convert_fusion.refs_0_) | copy-start | bytes 196612
  84.3 5.0 %collective-permute-start.11 = (bf16[1,64,512]{2,1,0:T(8,128)(2,1)S(1)}, bf16[1,64,512]{2,1,0:T(8,128)(2,1)S(1)}, u32[]{:S(2)}, u32[]{:S(2)}) collective-permute-start(bf16[1,64,512]{2,1,0:T(8,128)(2,1)S(1)} %divide_convert_fusion.refs_0_), channel_id=1, source_target_pairs={{0,4},{1,3},{2,6},{3,1},{4,0},{5,7},{6,2},{7,5},{8,12},{9,11},{10,... | collective-permute-start | bytes 196616 | tf_op jit(solution)/shard_map/ppermute | solution.py:359
  86.1 5.0 %collective-permute-start.12 = (bf16[1,64,512]{2,1,0:T(8,128)(2,1)S(1)}, bf16[1,64,512]{2,1,0:T(8,128)(2,1)S(1)}, u32[]{:S(2)}, u32[]{:S(2)}) collective-permute-start(bf16[1,64,512]{2,1,0:T(8,128)(2,1)S(1)} %divide_convert_fusion.refs_0_), channel_id=1, source_target_pairs={{0,2},{1,5},{2,0},{3,7},{4,6},{5,1},{6,4},{7,3},{8,10},{9,13},{10,... | collective-permute-start | bytes 196616 | tf_op jit(solution)/shard_map/ppermute | solution.py:359
  87.5 5.2 %collective-permute-start.13 = (bf16[1,64,512]{2,1,0:T(8,128)(2,1)S(1)}, bf16[1,64,512]{2,1,0:T(8,128)(2,1)S(1)}, u32[]{:S(2)}, u32[]{:S(2)}) collective-permute-start(bf16[1,64,512]{2,1,0:T(8,128)(2,1)S(1)} %divide_convert_fusion.refs_0_), channel_id=1, source_target_pairs={{0,6},{1,7},{2,4},{3,5},{4,2},{5,3},{6,0},{7,1},{8,14},{9,15},{10,... | collective-permute-start | bytes 196616 | tf_op jit(solution)/shard_map/ppermute | solution.py:359
  87.9 4.8 %collective-permute-start.14 = (bf16[1,64,512]{2,1,0:T(8,128)(2,1)S(1)}, bf16[1,64,512]{2,1,0:T(8,128)(2,1)S(1)}, u32[]{:S(2)}, u32[]{:S(2)}) collective-permute-start(bf16[1,64,512]{2,1,0:T(8,128)(2,1)S(1)} %divide_convert_fusion.refs_0_), channel_id=1, source_target_pairs={{0,1},{1,0},{2,3},{3,2},{4,5},{5,4},{6,7},{7,6},{8,9},{9,8},{10,11... | collective-permute-start | bytes 196616 | tf_op jit(solution)/shard_map/ppermute | solution.py:359
  89.4 4.6 %copy-start.3 = (bf16[1,64,512]{2,1,0:T(8,128)(2,1)}, bf16[1,64,512]{2,1,0:T(8,128)(2,1)S(1)}, u32[]{:S(2)}) copy-start(bf16[1,64,512]{2,1,0:T(8,128)(2,1)S(1)} %collective-permute-done.11.refs_1_) | copy-start | bytes 196612
  89.4 3.3 %collective-permute-start.15 = (bf16[1,64,512]{2,1,0:T(8,128)(2,1)S(1)}, bf16[1,64,512]{2,1,0:T(8,128)(2,1)S(1)}, u32[]{:S(2)}, u32[]{:S(2)}) collective-permute-start(bf16[1,64,512]{2,1,0:T(8,128)(2,1)S(1)} %collective-permute-done.11.refs_1_), channel_id=1, source_target_pairs={{0,1},{1,0},{2,3},{3,2},{4,5},{5,4},{6,7},{7,6},{8,9},{9,8},{10,11... | collective-permute-start | bytes 196616 | tf_op jit(solution)/shard_map/ppermute | solution.py:359
  91.1 2.9 %copy-start.4 = (bf16[1,64,512]{2,1,0:T(8,128)(2,1)}, bf16[1,64,512]{2,1,0:T(8,128)(2,1)S(1)}, u32[]{:S(2)}) copy-start(bf16[1,64,512]{2,1,0:T(8,128)(2,1)S(1)} %collective-permute-done.12.refs_2_) | copy-start | bytes 196612
  91.1 1.7 %collective-permute-start.16 = (bf16[1,64,512]{2,1,0:T(8,128)(2,1)S(1)}, bf16[1,64,512]{2,1,0:T(8,128)(2,1)S(1)}, u32[]{:S(2)}, u32[]{:S(2)}) collective-permute-start(bf16[1,64,512]{2,1,0:T(8,128)(2,1)S(1)} %collective-permute-done.12.refs_2_), channel_id=1, source_target_pairs={{0,1},{1,0},{2,3},{3,2},{4,5},{5,4},{6,7},{7,6},{8,9},{9,8},{10,11... | collective-permute-start | bytes 196616 | tf_op jit(solution)/shard_map/ppermute | solution.py:359
  92.7 1.3 %copy-start.5 = (bf16[1,64,512]{2,1,0:T(8,128)(2,1)}, bf16[1,64,512]{2,1,0:T(8,128)(2,1)S(1)}, u32[]{:S(2)}) copy-start(bf16[1,64,512]{2,1,0:T(8,128)(2,1)S(1)} %collective-permute-done.13.refs_3_) | copy-start | bytes 196612
  92.7 1.3 %collective-permute-start.17 = (bf16[1,64,512]{2,1,0:T(8,128)(2,1)S(1)}, bf16[1,64,512]{2,1,0:T(8,128)(2,1)S(1)}, u32[]{:S(2)}, u32[]{:S(2)}) collective-permute-start(bf16[1,64,512]{2,1,0:T(8,128)(2,1)S(1)} %collective-permute-done.13.refs_3_), channel_id=1, source_target_pairs={{0,1},{1,0},{2,3},{3,2},{4,5},{5,4},{6,7},{7,6},{8,9},{9,8},{10,11... | collective-permute-start | bytes 196616 | tf_op jit(solution)/shard_map/ppermute | solution.py:359
  92.7 1.3 %copy-start.6 = (bf16[1,64,512]{2,1,0:T(8,128)(2,1)}, bf16[1,64,512]{2,1,0:T(8,128)(2,1)S(1)}, u32[]{:S(2)}) copy-start(bf16[1,64,512]{2,1,0:T(8,128)(2,1)S(1)} %collective-permute-done.14.refs_4_) | copy-start | bytes 196612
  92.7 1.3 %copy-start.7 = (bf16[1,64,512]{2,1,0:T(8,128)(2,1)}, bf16[1,64,512]{2,1,0:T(8,128)(2,1)S(1)}, u32[]{:S(2)}) copy-start(bf16[1,64,512]{2,1,0:T(8,128)(2,1)S(1)} %collective-permute-done.15.refs_5_) | copy-start | bytes 196612
  92.7 1.3 %copy-start.8 = (bf16[1,64,512]{2,1,0:T(8,128)(2,1)}, bf16[1,64,512]{2,1,0:T(8,128)(2,1)S(1)}, u32[]{:S(2)}) copy-start(bf16[1,64,512]{2,1,0:T(8,128)(2,1)S(1)} %collective-permute-done.16.refs_6_) | copy-start | bytes 196612
  94.0 0.6 copy-start.9

commit v4 on v3

--- a/solution.py
+++ b/solution.py
@@ -15,22 +15,32 @@
 VMEM = pltpu.VMEM
 bf16 = jnp.bfloat16
 f32 = jnp.float32
+LIMIT = 44 << 20
 LOG2E = 1.4426950408889634
 
 
-def call(kernel, out, n_in, scratch=(), smem=0, out_spaces=None):
+def call(kernel, out, n_in, scratch=(), smem=0, out_spaces=None, aliases=None):
     outs = out if isinstance(out, (list, tuple)) else [out]
     spaces = out_spaces or [VMEM] * len(outs)
     specs = [pl.BlockSpec(memory_space=s) for s in spaces]
-    return pl.pallas_call(
+    kept = [VMEM(o.shape, o.dtype) if s is VMEM else o for o, s in zip(outs, spaces)]
+    single = not isinstance(out, (list, tuple))
+    fn = pl.pallas_call(
         kernel,
-        out_shape=out,
+        out_shape=kept[0] if single else kept,
         in_specs=[pl.BlockSpec(memory_space=pltpu.SMEM)] * smem
         + [pl.BlockSpec(memory_space=VMEM)] * n_in,
-        out_specs=specs if isinstance(out, (list, tuple)) else specs[0],
+        out_specs=specs[0] if single else specs,
         scratch_shapes=list(scratch),
-        compiler_params=pltpu.CompilerParams(vmem_limit_bytes=60 << 20),
+        input_output_aliases=aliases or {},
+        compiler_params=pltpu.CompilerParams(vmem_limit_bytes=LIMIT),
     )
+
+    def run(*args):
+        held = [pltpu.with_memory_space_constraint(x, VMEM) for x in args[smem:]]
+        return fn(*args[:smem], *held)
+
+    return run
 
 
 def shape(dims, dtype):
@@ -84,53 +94,86 @@
     return 4 * core + yx + core * (xy - yx), 4 * (1 - core) + xy + core * (yx - xy)
 
 
-def encode_kernel(
-    x_ref, hl_ref, hr_ref, top_ref, bot_ref, wt_ref, bias_ref, gain_ref, kv_ref, wvt_ref, qz_ref,
-    tok_out, keep_ref, send_ref,
-    y_ref, xs_ref, st_ref, tok_ref, k_ref, vt_ref, s_ref, col_ref, state_ref, peak_ref, side_ref, sems,
-):
+def edges_kernel(x_ref, first_ref, last_ref, low_ref, high_ref, row_ref):
     chan, rows, cols = x_ref.shape
-    half = cols // 2
-    trows = rows // 2
-    width = kv_ref.shape[0]
-    tokens = trows * half
-    lat = qz_ref.shape[2]
+    lane = lax.broadcasted_iota(jnp.int32, (rows, 128), 1)
+    first = jnp.zeros((rows, 128), f32)
+    last = jnp.zeros((rows, 128), f32)
+    row_ref[...] = jnp.zeros(row_ref.shape, f32)
+    for ch in range(chan):
+        first = jnp.where(lane == ch, x_ref[ch, :, :128].astype(f32)[:, :1], first)
+        last = jnp.where(lane == ch, x_ref[ch, :, cols - 128 :].astype(f32)[:, 127:], last)
+        row_ref[0, ch : ch + 1, :] = x_ref[ch, :16, :].astype(f32)[:1]
+        row_ref[1, ch : ch + 1, :] = x_ref[ch, rows - 16 :, :].astype(f32)[15:]
+    first_ref[...] = first.astype(bf16)
+    last_ref[...] = last.astype(bf16)
+    low_ref[...] = row_ref[0].astype(bf16)
+    high_ref[...] = row_ref[1].astype(bf16)
+
+
+def selection(cols):
+    ci = lax.broadcasted_iota(jnp.int32, (cols, cols), 0)
+    cj = lax.broadcasted_iota(jnp.int32, (cols, cols), 1)
+    want = jnp.where(cj < cols // 2, 2 * cj, 2 * (cj - cols // 2) + 1)
+    return jnp.where(ci == want, 1.0, 0.0).astype(bf16)
+
+
+def spread(pair, select, xs_ref, where, sides):
+    half = select.shape[0] // 2
+    lane = lax.broadcasted_iota(jnp.int32, (CP, half), 1)
+    sel = jnp.dot(pair, select, preferred_element_type=f32)
+    for q, (left, right) in enumerate(sides):
+        even = sel[q * CP : (q + 1) * CP, :half]
+        odd = sel[q * CP : (q + 1) * CP, half:]
+        first = jnp.where(lane == 0, left, pltpu.roll(odd, 1, 1))
+        last = jnp.where(lane == half - 1, right, pltpu.roll(even, half - 1, 1))
+        for kx, v in enumerate((first, even, odd, last)):
+            xs_ref[where[q], kx * CP : (kx + 1) * CP, :] = v.astype(bf16)
+
+
+def turned(ref, side_ref):
+    side_ref[...] = jnp.zeros(side_ref.shape, f32)
+    side_ref[: ref.shape[0]] = ref[...].astype(f32)
+    return jnp.transpose(side_ref[...])[:CP]
+
+
+def select_kernel(x_ref, hl_ref, hr_ref, xs_ref, y_ref, side_ref):
+    chan, rows, cols = x_ref.shape
 
     i = lax.broadcasted_iota(jnp.int32, (256, 256), 0)
     j = lax.broadcasted_iota(jnp.int32, (256, 256), 1)
     perm = jnp.where(((i >> 4) == (j & 15)) & ((i & 15) == (j >> 4)), 1.0, 0.0).astype(bf16)
-    for g in range(CP // 16):
-        n = min(16, chan - 16 * g)
-        for b in range(rows // 16):
+    for b in range(rows // 16):
+        for g in range(CP // 16):
+            n = min(16, chan - 16 * g)
             x = x_ref[16 * g : 16 * g + n, 16 * b : 16 * b + 16, :].reshape(n * 16, cols)
             y = jnp.dot(perm[:, : n * 16], x, preferred_element_type=f32).astype(bf16)
-            y_ref[1 + 16 * b : 17 + 16 * b, 16 * g : 16 * g + 16, :] = y.reshape(16, 16, cols)
-    y_ref[0] = top_ref[:CP]
-    y_ref[rows + 1] = bot_ref[:CP]
-
-    ci = lax.broadcasted_iota(jnp.int32, (cols, cols), 0)
-    cj = lax.broadcasted_iota(jnp.int32, (cols, cols), 1)
-    want = jnp.where(cj < half, 2 * cj, 2 * (cj - half) + 1)
-    select = jnp.where(ci == want, 1.0, 0.0).astype(bf16)
-    lane = lax.broadcasted_iota(jnp.int32, (CP, half), 1)
-    side_ref[...] = jnp.zeros(side_ref.shape, f32)
-    for n, ref in enumerate((hl_ref, hr_ref)):
-        side_ref[n, 1 : rows + 1] = ref[...].astype(f32)
-        for r, row in ((0, top_ref), (rows + 1, bot_ref)):
-            side_ref[n, r : r + 1] = row[CP + 16 * n : CP + 16 * n + 16, :128].astype(f32)[:1]
-    left_all, right_all = (jnp.transpose(side_ref[n])[:CP] for n in range(2))
-    for p in range((rows + 2) // 2):
-        pair = y_ref[2 * p : 2 * p + 2].reshape(2 * CP, cols)
-        sel = jnp.dot(pair, select, preferred_element_type=f32)
-        for q in range(2):
-            r = 2 * p + q
-            left, right = left_all[:, r : r + 1], right_all[:, r : r + 1]
-            even = sel[q * CP : (q + 1) * CP, :half]
-            odd = sel[q * CP : (q + 1) * CP, half:]
-            first = jnp.where(lane == 0, left, pltpu.roll(odd, 1, 1))
-            last = jnp.where(lane == half - 1, right, pltpu.roll(even, half - 1, 1))
-            for kx, v in enumerate((first, even, odd, last)):
-                xs_ref[r, kx * CP : (kx + 1) * CP, :] = v.astype(bf16)
+            y_ref[16 * b : 16 * b + 16, 16 * g : 16 * g + 16, :] = y.reshape(16, 16, cols)
+
+    select = selection(cols)
+    left, right = turned(hl_ref, side_ref.at[0]), turned(hr_ref, side_ref.at[1])
+    for r in range(0, rows, 2):
+        pair = y_ref[r : r + 2].reshape(2 * CP, cols)
+        sides = [(left[:, q : q + 1], right[:, q : q + 1]) for q in (r, r + 1)]
+        spread(pair, select, xs_ref, (r + 1, r + 2), sides)
+
+
+def encode_kernel(
+    xs_in, top_ref, bot_ref, wt_ref, bias_ref, gain_ref, kv_ref, wvt_ref, qz_ref,
+    tok_out, keep_ref, send_ref, xs_ref,
+    st_ref, tok_ref, k_ref, vt_ref, s_ref, col_ref, state_ref, peak_ref, side_ref, sems,
+):
+    trows, half, width = tok_ref.shape
+    rows, cols = 2 * trows, 2 * half
+    tokens = trows * half
+    lat = qz_ref.shape[2]
+
+    pair = jnp.concatenate([top_ref[:CP], bot_ref[:CP]])
+    sides = []
+    for n, ref in enumerate((top_ref, bot_ref)):
+        corners = turned(ref.at[CP:, :128], side_ref.at[n])
+        sides.append((corners[:, 0:1], corners[:, 16:17]))
+    spread(pair, selection(cols), xs_ref, (0, rows + 1), sides)
 
     for h in range(HEADS):
         vt_ref[h * HR + HD : (h + 1) * HR, :] = jnp.ones((HR - HD, tokens), bf16)
@@ -217,8 +260,6 @@
     half, trows = cols // 2, rows // 2
     tokens = trows * half
     return [
-        VMEM((rows + 2, CP, cols), bf16),
-        VMEM((rows + 2, 4 * CP, half), bf16),
         VMEM((2, width, half), f32),
         VMEM((trows, half, width), bf16),
         VMEM((tokens, width), bf16),
@@ -312,11 +353,13 @@
     ahead = [(i, (i + 1) % nlon) for i in range(nlon)]
     back = [(t, s) for s, t in ahead]
 
-    def side(c):
-        return jnp.pad(field[:, :, c].T, ((0, 0), (0, 128 - chan)))
-
-    hl = lax.ppermute(side(cols - 1), "lon", ahead)
-    hr = lax.ppermute(side(0), "lon", back)
+    edge = shape((rows, 128), bf16)
+    line = shape((CP, cols), bf16)
+    first, last, low, high = call(
+        edges_kernel, [edge, edge, line, line], 1, scratch=[VMEM((2, CP, cols), f32)]
+    )(field)
+    hl = lax.ppermute(last, "lon", ahead)
+    hr = lax.ppermute(first, "lon", back)
     wt, wvt = call(
         weights_kernel,
         [shape((width, 16 * CP), bf16), shape((width, width), bf16)],
@@ -325,28 +368,36 @@
     )(stem_weight, kv_weight)
     hl, hr, wt, wvt = lax.optimization_barrier((hl, hr, wt, wvt))
 
-    def edge(r):
+    def framed(line, r):
         corners = [jnp.pad(h[r : r + 1], ((0, 15), (0, cols - 128))) for h in (hl, hr)]
-        return jnp.concatenate([jnp.pad(field[:, r, :], ((0, CP - chan), (0, 0)))] + corners)
-
-    low, high = edge(rows - 1), edge(0)
-    low, high, latents = lax.optimization_barrier((low, high, latents))
+        return jnp.concatenate([line] + corners)
+
+    low, high = framed(low, 0), framed(high, rows - 1)
+    low, high, latents, hl = lax.optimization_barrier((low, high, latents, hl))
     up = [(i, i + 1) for i in range(nlat - 1)]
     down = [(t, s) for s, t in up]
-    top = lax.ppermute(low, "lat", up)
-    bot = lax.ppermute(high, "lat", down)
+    top = lax.ppermute(high, "lat", up)
+    bot = lax.ppermute(low, "lat", down)
     qz = call(query_kernel, shape((HEADS, 4 * HD, lat), bf16), 3, smem=1)(
         head_gain, latents, latent_gain[None, :], query_weight
     )
 
+    patches = shape((rows + 2, 4 * CP, half), bf16)
+    xs = call(
+        select_kernel,
+        patches,
+        3,
+        scratch=[VMEM((rows, CP, cols), bf16), VMEM((2, 128, 128), f32)],
+    )(field, hl, hr)
     state = shape((HEADS // 2, HR, lat), bf16)
-    tok, keep, send = call(
+    tok, keep, send, _ = call(
         encode_kernel,
-        [shape((trows, half, width), bf16), state, state],
-        11,
-        out_spaces=[pl.ANY, VMEM, VMEM],
+        [shape((trows, half, width), bf16), state, state, patches],
+        9,
+        out_spaces=[pl.ANY, VMEM, VMEM, VMEM],
+        aliases={0: 3},
         scratch=encode_scratch(rows, cols, width, lat),
-    )(field, hl, hr, top, bot, wt, stem_bias[None, :], token_gain[None, :], kv_weight, wvt, qz)
+    )(xs, top, bot, wt, stem_bias[None, :], token_gain[None, :], kv_weight, wvt, qz)
 
     def swap(x, flips0, flips1):
         pairs = []

time: 98 us -> 86.1 us (0.88)
  Pallas kernels: 48.7 us -> 38.7 us
  other arithmetic: 2.43 us -> 0.63 us
    pallas_call x4 -> x6, Pallas kernels: 48.7 us -> 38.7 us  [run(): return fn(*args[:smem], *held)]
    slice x3 -> x2, local copies, waits for them, and re-layouts: 2.93 us -> 0.01 us  [framed(): h[r:r + 1]]
    unnamed x28 -> x29, local copies, waits for them, and re-layouts: 2.68 us -> 5.15 us
  transfers between devices with their start and end apart: 18 -> 18, of which waited for: 11 -> 11; matrix products, arithmetic and copies ran while one was open for 3% -> 0% of each run, Pallas kernels for 7% -> 5%
where the time goes in v4:
time: 86.1 us; the launch traced here: 85.8 us
  Pallas kernels  38.7 us (45%)
  starting transfers between devices  20.4 us (24%)
  waiting for transfers between devices  18.9 us (22%)
  local copies, waits for them, and re-layouts  6.17 us (7%)
  between operations  1.05 us (1%)
    pallas_call x6, Pallas kernels, run(): return fn(*args[:smem], *held)  38.7 us
    ppermute x14, waiting for transfers between devices, swap(): return lax.ppermute(x, ('lat', 'lon'), pairs)  17.6 us
    ppermute x14, starting transfers between devices, swap(): return lax.ppermute(x, ('lat', 'lon'), pairs)  12.3 us
    unnamed x29, local copies, waits for them, and re-layouts  5.15 us
    ppermute x1, starting transfers between devices, shards(): top = lax.ppermute(high, 'lat', up)  4.25 us
    ppermute x1, starting transfers between devices, shards(): hr = lax.ppermute(first, 'lon', back)  2.01 us
  transfers between devices with their start and end apart: 18, of which 11 were waited for; matrix products, arithmetic and copies ran while one was open for 0% of the time, Pallas kernels for 5%

profile of v4, /device:TPU:0, one launch (start us, length us, event | category | flops | bytes accessed | tf_op | source)
XLA Modules:
  0.0 85.8 jit_solution(13103806375134561165)
XLA Ops:
  0.6 1.6 %copy-done = bf16[69,32,512]{2,1,0:T(8,128)(2,1)S(1)} copy-done((bf16[69,32,512]{2,1,0:T(8,128)(2,1)S(1)}, bf16[69,32,512]{2,1,0:T(8,128)(2,1)}, u32[]{:S(2)}) %copy-start) | copy-done | bytes 2261016
  2.3 0.7 shard_map.122
  2.9 0.5 collective-permute-start
  3.5 2.0 %collective-permute-start.1 = (bf16[32,128]{1,0:T(8,128)(2,1)S(1)}, bf16[32,128]{1,0:T(8,128)(2,1)S(1)}, u32[]{:S(2)}, u32[]{:S(2)}) collective-permute-start(bf16[32,128]{1,0:T(8,128)(2,1)S(1)} %get-tuple-element.21), channel_id=1, source_target_pairs={{1,0},{2,1},{3,2},{0,3},{5,4},{6,5},{7,6},{4,7},{9,8},{10,9},{11,1... | collective-permute-start | bytes 24584 | tf_op jit(solution)/shard_map/ppermute | solution.py:362
  5.5 1.2 %copy-done.2 = bf16[512,1024]{1,0:T(8,128)(2,1)S(1)} copy-done((bf16[512,1024]{1,0:T(8,128)(2,1)S(1)}, bf16[512,1024]{1,0:T(8,128)(2,1)}, u32[]{:S(2)}) %copy-start.2) | copy-done | bytes 1048600
  6.7 1.3 %copy-done.4 = bf16[1104,512]{1,0:T(8,128)(2,1)S(1)} copy-done((bf16[1104,512]{1,0:T(8,128)(2,1)S(1)}, bf16[1104,512]{1,0:T(8,128)(2,1)}, u32[]{:S(2)}) %copy-start.4) | copy-done | bytes 1130520
  8.0 0.5 shard_map.123
  8.5 0.0 collective-permute-done.hl_ref
  8.5 0.0 collective-permute-done.1.hr_ref
  8.6 0.0 copy-start.5
  8.6 0.0 copy-start.6
  8.6 0.0 copy-start.8
  8.6 0.0 copy-start.12
  8.7 4.3 %collective-permute-start.2 = (bf16[112,512]{1,0:T(8,128)(2,1)S(1)}, bf16[112,512]{1,0:T(8,128)(2,1)S(1)}, u32[]{:S(2)}, u32[]{:S(2)}) collective-permute-start(bf16[112,512]{1,0:T(8,128)(2,1)S(1)} %get-tuple-element.28), channel_id=1, source_target_pairs={{0,4},{4,8},{8,12},{12,16},{16,20},{20,24},{24,28},{1,5},{5,9},{9,... | collective-permute-start | bytes 344072 | tf_op jit(solution)/shard_map/ppermute | solution.py:379
  12.9 1.3 %collective-permute-start.3 = (bf16[112,512]{1,0:T(8,128)(2,1)S(1)}, bf16[112,512]{1,0:T(8,128)(2,1)S(1)}, u32[]{:S(2)}, u32[]{:S(2)}) collective-permute-start(bf16[112,512]{1,0:T(8,128)(2,1)S(1)} %get-tuple-element.29), channel_id=1, source_target_pairs={{4,0},{8,4},{12,8},{16,12},{20,16},{24,20},{28,24},{5,1},{9,5},{13... | collective-permute-start | bytes 344072 | tf_op jit(solution)/shard_map/ppermute | solution.py:380
  14.2 2.5 %shard_map.124.xs_in = bf16[34,320,256]{2,1,0:T(8,128)(2,1)S(1)} custom-call(bf16[69,32,512]{2,1,0:T(8,128)(2,1)S(1)} %copy-done.1, bf16[32,128]{1,0:T(8,128)(2,1)S(1)} %collective-permute-done.hl_ref, bf16[32,128]{1,0:T(8,128)(2,1)S(1)} %collective-permute-done.1.hr_ref), custom_call_target="tpu_custom_call" | custom-call | tf_op jit(solution)/shard_map/pallas_call | solution.py:41
  16.8 0.0 copy-start.3
  16.8 0.0 copy-start.9
  16.8 0.0 copy-start.10
  16.8 1.5 %shard_map.125.qz_ref = bf16[8,256,512]{2,1,0:T(8,128)(2,1)S(1)} custom-call(f32[8]{0:T(128)S(1)} %copy-done.12, f32[512,512]{1,0:T(8,128)S(1)} %copy-done.5, f32[1,512]{1,0:T(1,128)S(1)} %bitcast.23, bf16[512,512]{1,0:T(8,128)(2,1)S(1)} %copy-done.6), custom_call_target="tpu_custom_call" | custom-call | tf_op jit(solution)/shard_map/pallas_call | solution.py:41
  18.3 0.0 collective-permute-done.2.top_ref
  18.3 1.3 %collective-permute-done.3.bot_ref = bf16[112,512]{1,0:T(8,128)(2,1)S(1)} collective-permute-done((bf16[112,512]{1,0:T(8,128)(2,1)S(1)}, bf16[112,512]{1,0:T(8,128)(2,1)S(1)}, u32[]{:S(2)}, u32[]{:S(2)}) %collective-permute-start.3) | collective-permute-done | bytes 114720 | tf_op jit(solution)/shard_map/ppermute | solution.py:380
  19.6 32.7 %shard_map.126 = (bf16[16,256,512]{2,1,0:T(8,128)(2,1)}, bf16[4,80,512]{2,1,0:T(8,128)(2,1)S(1)}, bf16[4,80,512]{2,1,0:T(8,128)(2,1)S(1)}, bf16[34,320,256]{2,1,0:T(8,128)(2,1)S(1)}) custom-call(bf16[34,320,256]{2,1,0:T(8,128)(2,1)S(1)} %shard_map.124.xs_in, bf16[112,512]{1,0:T(8,128)(2,1)S(1)} %collective-permute-done.2.top_ref, ...), custom_call_target="tpu_custom_call", output_to_operand_aliasing={{3}: (0, {})} | custom-call | tf_op jit(solution)/shard_map/pallas_call | solution.py:41
  52.3 0.0 copy-start.7
  52.3 0.0 copy-start.11
  52.3 0.1 collective-permute-start.4
  52.4 1.6 %collective-permute-done.4 = bf16[4,80,512]{2,1,0:T(8,128)(2,1)S(1)} collective-permute-done((bf16[4,80,512]{2,1,0:T(8,128)(2,1)S(1)}, bf16[4,80,512]{2,1,0:T(8,128)(2,1)S(1)}, u32[]{:S(2)}, u32[]{:S(2)}) %collective-permute-start.4) | collective-permute-done | bytes 327712 | tf_op jit(solution)/shard_map/ppermute | solution.py:410
  54.0 0.1 fusion.12
  54.1 0.1 reduce-precision_convert_fusion
  54.2 0.3 concatenate.30
  54.5 0.1 add_convert_fusion
  54.6 0.4 concatenate.31
  55.0 3.5 %collective-permute-start.7 = (bf16[1,80,512]{2,1,0:T(8,128)(2,1)S(1)}, bf16[1,80,512]{2,1,0:T(8,128)(2,1)S(1)}, u32[]{:S(2)}, u32[]{:S(2)}) collective-permute-start(bf16[1,80,512]{2,1,0:T(8,128)(2,1)S(1)} %get-tuple-element.65), channel_id=1, source_target_pairs={{0,6},{1,7},{2,4},{3,5},{4,2},{5,3},{6,0},{7,1},{8,14},{9,15},{10,... | collective-permute-start | bytes 245768 | tf_op jit(solution)/shard_map/ppermute | solution.py:410
  58.5 0.5 collective-permute-start.6
  59.0 0.2 collective-permute-start.5
  59.2 2.4 %collective-permute-done.7 = bf16[1,80,512]{2,1,0:T(8,128)(2,1)S(1)} collective-permute-done((bf16[1,80,512]{2,1,0:T(8,128)(2,1)S(1)}, bf16[1,80,512]{2,1,0:T(8,128)(2,1)S(1)}, u32[]{:S(2)}, u32[]{:S(2)}) %collective-permute-start.7) | collective-permute-done | bytes 81952 | tf_op jit(solution)/shard_map/ppermute | solution.py:410
  61.6 1.5 %collective-permute-done.6 = bf16[1,80,512]{2,1,0:T(8,128)(2,1)S(1)} collective-permute-done((bf16[1,80,512]{2,1,0:T(8,128)(2,1)S(1)}, bf16[1,80,512]{2,1,0:T(8,128)(2,1)S(1)}, u32[]{:S(2)}, u32[]{:S(2)}) %collective-permute-start.6) | collective-permute-done | bytes 81952 | tf_op jit(solution)/shard_map/ppermute | solution.py:410
  63.1 0.4 collective-permute-done.5
  63.5 0.1 reduce-precision_convert_fusion.4
  63.6 0.1 add_convert_fusion.1
  63.7 0.2 concatenate.33
  63.8 3.5 %collective-permute-start.10 = (bf16[1,80,512]{2,1,0:T(8,128)(2,1)S(1)}, bf16[1,80,512]{2,1,0:T(8,128)(2,1)S(1)}, u32[]{:S(2)}, u32[]{:S(2)}) collective-permute-start(bf16[1,80,512]{2,1,0:T(8,128)(2,1)S(1)} %concatenate.33), channel_id=1, source_target_pairs={{0,24},{1,25},{2,26},{3,27},{4,28},{5,29},{6,30},{7,31},{8,16},{9,... | collective-permute-start | bytes 245768 | tf_op jit(solution)/shard_map/ppermute | solution.py:410
  67.4 0.2 concatenate.32
  67.6 0.1 collective-permute-start.9
  67.6 0.9 %collective-permute-start.8 = (bf16[1,80,512]{2,1,0:T(8,128)(2,1)S(1)}, bf16[1,80,512]{2,1,0:T(8,128)(2,1)S(1)}, u32[]{:S(2)}, u32[]{:S(2)}) collective-permute-start(bf16[1,80,512]{2,1,0:T(8,128)(2,1)S(1)} %concatenate.33), channel_id=1, source_target_pairs={{0,8},{1,9},{2,10},{3,11},{4,12},{5,13},{6,14},{7,15},{8,0},{9,1},... | collective-permute-start | bytes 245768 | tf_op jit(solution)/shard_map/ppermute | solution.py:410
  68.5 2.6 %collective-permute-done.10 = bf16[1,80,512]{2,1,0:T(8,128)(2,1)S(1)} collective-permute-done((bf16[1,80,512]{2,1,0:T(8,128)(2,1)S(1)}, bf16[1,80,512]{2,1,0:T(8,128)(2,1)S(1)}, u32[]{:S(2)}, u32[]{:S(2)}) %collective-permute-start.10) | collective-permute-done | bytes 81952 | tf_op jit(solution)/shard_map/ppermute | solution.py:410
  71.2 3.3 %collective-permute-done.9 = bf16[1,80,512]{2,1,0:T(8,128)(2,1)S(1)} collective-permute-done((bf16[1,80,512]{2,1,0:T(8,128)(2,1)S(1)}, bf16[1,80,512]{2,1,0:T(8,128)(2,1)S(1)}, u32[]{:S(2)}, u32[]{:S(2)}) %collective-permute-start.9) | collective-permute-done | bytes 81952 | tf_op jit(solution)/shard_map/ppermute | solution.py:410
  74.5 0.0 collective-permute-done.8
  74.5 0.1 multiply_add_fusion
  74.6 0.1 divide_convert_fusion.refs_0_
  74.6 1.5 %collective-permute-start.11 = (bf16[1,64,512]{2,1,0:T(8,128)(2,1)S(1)}, bf16[1,64,512]{2,1,0:T(8,128)(2,1)S(1)}, u32[]{:S(2)}, u32[]{:S(2)}) collective-permute-start(bf16[1,64,512]{2,1,0:T(8,128)(2,1)S(1)} %divide_convert_fusion.refs_0_), channel_id=1, source_target_pairs={{0,4},{1,3},{2,6},{3,1},{4,0},{5,7},{6,2},{7,5},{8,12},{9,11},{10,... | collective-permute-start | bytes 196616 | tf_op jit(solution)/shard_map/ppermute | solution.py:410
  76.2 1.4 %collective-permute-start.12 = (bf16[1,64,512]{2,1,0:T(8,128)(2,1)S(1)}, bf16[1,64,512]{2,1,0:T(8,128)(2,1)S(1)}, u32[]{:S(2)}, u32[]{:S(2)}) collective-permute-start(bf16[1,64,512]{2,1,0:T(8,128)(2,1)S(1)} %divide_convert_fusion.refs_0_), channel_id=1, source_target_pairs={{0,2},{1,5},{2,0},{3,7},{4,6},{5,1},{6,4},{7,3},{8,10},{9,13},{10,... | collective-permute-start | bytes 196616 | tf_op jit(solution)/shard_map/ppermute | solution.py:410
  77.6 0.6 collective-permute-start.13
  78.2 0.0 collective-permute-start.14
  78.2 1.3 %collective-permute-done.11.refs_1_ = bf16[1,64,512]{2,1,0:T(8,128)(2,1)S(1)} collective-permute-done((bf16[1,64,512]{2,1,0:T(8,128)(2,1)S(1)}, bf16[1,64,512]{2,1,0:T(8,128)(2,1)S(1)}, u32[]{:S(2)}, u32[]{:S(2)}) %collective-permute-start.11) | collective-permute-done | bytes 65568 | tf_op jit(solution)/shard_map/ppermute | solution.py:410
  79.5 0.0 collective-permute-start.15
  79.5 1.6 %collective-permute-done.12.refs_2_ = bf16[1,64,512]{2,1,0:T(8,128)(2,1)S(1)} collective-permute-done((bf16[1,64,512]{2,1,0:T(8,128)(2,1)S(1)}, bf16[1,64,512]{2,1,0:T(8,128)(2,1)S(1)}, u32[]{:S(2)}, u32[]{:S(2)}) %collective-permute-start.12) | collective-permute-done | bytes 65568 | tf_op jit(solution)/shard_map/ppermute | solution.py:410
  81.1 0.0 collective-permute-start.16
  81.1 1.6 %collective-permute-done.13.refs_3_ = bf16[1,64,512]{2,1,0:T(8,128)(2,1)S(1)} collective-permute-done((bf16[1,64,512]{2,1,0:T(8,128)(2,1)S(1)}, bf16[1,64,512]{2,1,0:T(8,128)(2,1)S(1)}, u32[]{:S(2)}, u32[]{:S(2)}) %collective-permute-start.13) | collective-permute-done | bytes 65568 | tf_op jit(solution)/shard_map/ppermute | solution.py:410
  82.8 0.0 collective-permute-start.17
  82.8 0.0 collective-permute-done.14.refs_4_
  82.8 1.2 %collective-permute-done.17.refs_7_ = bf16[1,64,512]{2,1,0:T(8,128)(2,1)S(1)} collective-permute-done((bf16[1,64,512]{2,1,0:T(8,128)(2,1)S(1)}, bf16[1,64,512]{2,1,0:T(8,128)(2,1)S(1)}, u32[]{:S(2)}, u32[]{:S(2)}) %collective-permute-start.17) | collective-permute-done | bytes 65568 | tf_op jit(solution)/shard_map/ppermute | solution.py:410
  84.0 0.8 shard_map.127
  84.8 1.0 %copy.21 = f32[512,512]{1,0:T(8,128)} copy(f32[512,512]{1,0:T(8,128)S(1)} %shard_map.127) | data formatting | bytes 2097152
  (37 shorter events, 0.2 us)
Async XLA Ops:
  0.6 1.6 %copy-start = (bf16[69,32,512]{2,1,0:T(8,128)(2,1)S(1)}, bf16[69,32,512]{2,1,0:T(8,128)(2,1)}, u32[]{:S(2)}) copy-start(bf16[69,32,512]{2,1,0:T(8,128)(2,1)} %x_ref.3) | copy-start | bytes 6782980
  2.3 11.9 %copy-start.1 = (bf16[69,32,512]{2,1,0:T(8,128)(2,1)S(1)}, bf16[69,32,512]{2,1,0:T(8,128)(2,1)}, u32[]{:S(2)}) copy-start(bf16[69,32,512]{2,1,0:T(8,128)(2,1)} %x_ref.3) | copy-start | bytes 6782980
  2.9 5.6 %collective-permute-start = (bf16[32,128]{1,0:T(8,128)(2,1)S(1)}, bf16[32,128]{1,0:T(8,128)(2,1)S(1)}, u32[]{:S(2)}, u32[]{:S(2)}) collective-permute-start(bf16[32,128]{1,0:T(8,128)(2,1)S(1)} %get-tuple-element.20), channel_id=1, source_target_pairs={{0,1},{1,2},{2,3},{3,0},{4,5},{5,6},{6,7},{7,4},{8,9},{9,10},{10,1... | collective-permute-start | bytes 24584 | tf_op jit(solution)/shard_map/ppermute | solution.py:361
  3.5 5.1 %collective-permute-start.1 = (bf16[32,128]{1,0:T(8,128)(2,1)S(1)}, bf16[32,128]{1,0:T(8,128)(2,1)S(1)}, u32[]{:S(2)}, u32[]{:S(2)}) collective-permute-start(bf16[32,128]{1,0:T(8,128)(2,1)S(1)} %get-tuple-element.21), channel_id=1, source_target_pairs={{1,0},{2,1},{3,2},{0,3},{5,4},{6,5},{7,6},{4,7},{9,8},{10,9},{11,1... | collective-permute-start | bytes 24584 | tf_op jit(solution)/shard_map/ppermute | solution.py:362
  5.5 1.2 %copy-start.2 = (bf16[512,1024]{1,0:T(8,128)(2,1)S(1)}, bf16[512,1024]{1,0:T(8,128)(2,1)}, u32[]{:S(2)}) copy-start(bf16[512,1024]{1,0:T(8,128)(2,1)} %kv_ref.3) | copy-start | bytes 3145732
  6.7 1.3 %copy-start.4 = (bf16[1104,512]{1,0:T(8,128)(2,1)S(1)}, bf16[1104,512]{1,0:T(8,128)(2,1)}, u32[]{:S(2)}) copy-start(bf16[1104,512]{1,0:T(8,128)(2,1)} %w_ref.1) | copy-start | bytes 3391492
  8.6 8.2 %copy-start.5 = (f32[512,512]{1,0:T(8,128)S(1)}, f32[512,512]{1,0:T(8,128)}, u32[]{:S(2)}) copy-start(f32[512,512]{1,0:T(8,128)} %latents_ref) | copy-start | bytes 3145732
  8.6 8.2 %copy-start.6 = (bf16[512,512]{1,0:T(8,128)(2,1)S(1)}, bf16[512,512]{1,0:T(8,128)(2,1)}, u32[]{:S(2)}) copy-start(bf16[512,512]{1,0:T(8,128)(2,1)} %qw_ref.1) | copy-start | bytes 1572868
  8.6 8.2 %copy-start.8 = (f32[512]{0:T(512)S(1)}, f32[512]{0:T(512)}, u32[]{:S(2)}) copy-start(f32[512]{0:T(512)} %param.17) | copy-start | bytes 6148
  8.6 8.2 %copy-start.12 = (f32[8]{0:T(128)S(1)}, f32[8]{0:T(128)}, u32[]{:S(2)}) copy-start(f32[8]{0:T(128)} %gain_ref.1) | copy-start | bytes 100
  8.7 9.7 %collective-permute-start.2 = (bf16[112,512]{1,0:T(8,128)(2,1)S(1)}, bf16[112,512]{1,0:T(8,128)(2,1)S(1)}, u32[]{:S(2)}, u32[]{:S(2)}) collective-permute-start(bf16[112,512]{1,0:T(8,128)(2,1)S(1)} %get-tuple-element.28), channel_id=1, source_target_pairs={{0,4},{4,8},{8,12},{12,16},{16,20},{20,24},{24,28},{1,5},{5,9},{9,... | collective-permute-start | bytes 344072 | tf_op jit(solution)/shard_map/ppermute | solution.py:379
  12.9 6.7 %collective-permute-start.3 = (bf16[112,512]{1,0:T(8,128)(2,1)S(1)}, bf16[112,512]{1,0:T(8,128)(2,1)S(1)}, u32[]{:S(2)}, u32[]{:S(2)}) collective-permute-start(bf16[112,512]{1,0:T(8,128)(2,1)S(1)} %get-tuple-element.29), channel_id=1, source_target_pairs={{4,0},{8,4},{12,8},{16,12},{20,16},{24,20},{28,24},{5,1},{9,5},{13... | collective-permute-start | bytes 344072 | tf_op jit(solution)/shard_map/ppermute | solution.py:380
  16.8 2.9 %copy-start.3 = (bf16[512,1024]{1,0:T(8,128)(2,1)S(1)}, bf16[512,1024]{1,0:T(8,128)(2,1)}, u32[]{:S(2)}) copy-start(bf16[512,1024]{1,0:T(8,128)(2,1)} %kv_ref.3) | copy-start | bytes 3145732
  16.8 2.8 %copy-start.9 = (f32[512]{0:T(512)S(1)}, f32[512]{0:T(512)}, u32[]{:S(2)}) copy-start(f32[512]{0:T(512)} %param.13) | copy-start | bytes 6148
  16.8 2.8 %copy-start.10 = (f32[512]{0:T(512)S(1)}, f32[512]{0:T(512)}, u32[]{:S(2)}) copy-start(f32[512]{0:T(512)} %param.14) | copy-start | bytes 6148
  52.3 31.7 %copy-start.7 = (bf16[512,512]{1,0:T(8,128)(2,1)S(1)}, bf16[512,512]{1,0:T(8,128)(2,1)}, u32[]{:S(2)}) copy-start(bf16[512,512]{1,0:T(8,128)(2,1)} %refs_8_.1) | copy-start | bytes 1572868
  52.3 31.7 %copy-start.11 = (f32[512]{0:T(512)S(1)}, f32[512]{0:T(512)}, u32[]{:S(2)}) copy-start(f32[512]{0:T(512)} %param.21) | copy-start | bytes 6148
  52.3 1.7 %collective-permute-start.4 = (bf16[4,80,512]{2,1,0:T(8,128)(2,1)S(1)}, bf16[4,80,512]{2,1,0:T(8,128)(2,1)S(1)}, u32[]{:S(2)}, u32[]{:S(2)}) collective-permute-start(bf16[4,80,512]{2,1,0:T(8,128)(2,1)S(1)} %get-tuple-element.35), channel_id=1, source_target_pairs={{0,1},{1,0},{2,3},{3,2},{4,5},{5,4},{6,7},{7,6},{8,9},{9,8},{10,11... | collective-permute-start | bytes 983048 | tf_op jit(solution)/shard_map/ppermute | solution.py:410
  55.0 6.6 %collective-permute-start.7 = (bf16[1,80,512]{2,1,0:T(8,128)(2,1)S(1)}, bf16[1,80,512]{2,1,0:T(8,128)(2,1)S(1)}, u32[]{:S(2)}, u32[]{:S(2)}) collective-permute-start(bf16[1,80,512]{2,1,0:T(8,128)(2,1)S(1)} %get-tuple-element.65), channel_id=1, source_target_pairs={{0,6},{1,7},{2,4},{3,5},{4,2},{5,3},{6,0},{7,1},{8,14},{9,15},{10,... | collective-permute-start | bytes 245768 | tf_op jit(solution)/shard_map/ppermute | solution.py:410
  58.5 4.6 %collective-permute-start.6 = (bf16[1,80,512]{2,1,0:T(8,128)(2,1)S(1)}, bf16[1,80,512]{2,1,0:T(8,128)(2,1)S(1)}, u32[]{:S(2)}, u32[]{:S(2)}) collective-permute-start(bf16[1,80,512]{2,1,0:T(8,128)(2,1)S(1)} %get-tuple-element.66), channel_id=1, source_target_pairs={{0,2},{1,5},{2,0},{3,7},{4,6},{5,1},{6,4},{7,3},{8,10},{9,13},{10,... | collective-permute-start | bytes 245768 | tf_op jit(solution)/shard_map/ppermute | solution.py:410
  59.0 4.4 %collective-permute-start.5 = (bf16[1,80,512]{2,1,0:T(8,128)(2,1)S(1)}, bf16[1,80,512]{2,1,0:T(8,128)(2,1)S(1)}, u32[]{:S(2)}, u32[]{:S(2)}) collective-permute-start(bf16[1,80,512]{2,1,0:T(8,128)(2,1)S(1)} %get-tuple-element.64), channel_id=1, source_target_pairs={{0,4},{1,3},{2,6},{3,1},{4,0},{5,7},{6,2},{7,5},{8,12},{9,11},{10,... | collective-permute-start | bytes 245768 | tf_op jit(solution)/shard_map/ppermute | solution.py:410
  63.8 7.3 %collective-permute-start.10 = (bf16[1,80,512]{2,1,0:T(8,128)(2,1)S(1)}, bf16[1,80,512]{2,1,0:T(8,128)(2,1)S(1)}, u32[]{:S(2)}, u32[]{:S(2)}) collective-permute-start(bf16[1,80,512]{2,1,0:T(8,128)(2,1)S(1)} %concatenate.33), channel_id=1, source_target_pairs={{0,24},{1,25},{2,26},{3,27},{4,28},{5,29},{6,30},{7,31},{8,16},{9,... | collective-permute-start | bytes 245768 | tf_op jit(solution)/shard_map/ppermute | solution.py:410
  67.6 6.9 %collective-permute-start.9 = (bf16[1,80,512]{2,1,0:T(8,128)(2,1)S(1)}, bf16[1,80,512]{2,1,0:T(8,128)(2,1)S(1)}, u32[]{:S(2)}, u32[]{:S(2)}) collective-permute-start(bf16[1,80,512]{2,1,0:T(8,128)(2,1)S(1)} %concatenate.33), channel_id=1, source_target_pairs={{0,16},{1,17},{2,18},{3,19},{4,20},{5,21},{6,22},{7,23},{8,24},{9,... | collective-permute-start | bytes 245768 | tf_op jit(solution)/shard_map/ppermute | solution.py:410
  67.6 6.8 %collective-permute-start.8 = (bf16[1,80,512]{2,1,0:T(8,128)(2,1)S(1)}, bf16[1,80,512]{2,1,0:T(8,128)(2,1)S(1)}, u32[]{:S(2)}, u32[]{:S(2)}) collective-permute-start(bf16[1,80,512]{2,1,0:T(8,128)(2,1)S(1)} %concatenate.33), channel_id=1, source_target_pairs={{0,8},{1,9},{2,10},{3,11},{4,12},{5,13},{6,14},{7,15},{8,0},{9,1},... | collective-permute-start | bytes 245768 | tf_op jit(solution)/shard_map/ppermute | solution.py:410
  74.6 4.9 %collective-permute-start.11 = (bf16[1,64,512]{2,1,0:T(8,128)(2,1)S(1)}, bf16[1,64,512]{2,1,0:T(8,128)(2,1)S(1)}, u32[]{:S(2)}, u32[]{:S(2)}) collective-permute-start(bf16[1,64,512]{2,1,0:T(8,128)(2,1)S(1)} %divide_convert_fusion.refs_0_), channel_id=1, source_target_pairs={{0,4},{1,3},{2,6},{3,1},{4,0},{5,7},{6,2},{7,5},{8,12},{9,11},{10,... | collective-permute-start | bytes 196616 | tf_op jit(solution)/shard_map/ppermute | solution.py:410
  76.2 5.0 %collective-permute-start.12 = (bf16[1,64,512]{2,1,0:T(8,128)(2,1)S(1)}, bf16[1,64,512]{2,1,0:T(8,128)(2,1)S(1)}, u32[]{:S(2)}, u32[]{:S(2)}) collective-permute-start(bf16[1,64,512]{2,1,0:T(8,128)(2,1)S(1)} %divide_convert_fusion.refs_0_), channel_id=1, source_target_pairs={{0,2},{1,5},{2,0},{3,7},{4,6},{5,1},{6,4},{7,3},{8,10},{9,13},{10,... | collective-permute-start | bytes 196616 | tf_op jit(solution)/shard_map/ppermute | solution.py:410
  77.6 5.2 %collective-permute-start.13 = (bf16[1,64,512]{2,1,0:T(8,128)(2,1)S(1)}, bf16[1,64,512]{2,1,0:T(8,128)(2,1)S(1)}, u32[]{:S(2)}, u32[]{:S(2)}) collective-permute-start(bf16[1,64,512]{2,1,0:T(8,128)(2,1)S(1)} %divide_convert_fusion.refs_0_), channel_id=1, source_target_pairs={{0,6},{1,7},{2,4},{3,5},{4,2},{5,3},{6,0},{7,1},{8,14},{9,15},{10,... | collective-permute-start | bytes 196616 | tf_op jit(solution)/shard_map/ppermute | solution.py:410
  78.2 4.6 %collective-permute-start.14 = (bf16[1,64,512]{2,1,0:T(8,128)(2,1)S(1)}, bf16[1,64,512]{2,1,0:T(8,128)(2,1)S(1)}, u32[]{:S(2)}, u32[]{:S(2)}) collective-permute-start(bf16[1,64,512]{2,1,0:T(8,128)(2,1)S(1)} %divide_convert_fusion.refs_0_), channel_id=1, source_target_pairs={{0,1},{1,0},{2,3},{3,2},{4,5},{5,4},{6,7},{7,6},{8,9},{9,8},{10,11... | collective-permute-start | bytes 196616 | tf_op jit(solution)/shard_map/ppermute | solution.py:410
  79.5 3.3 %collective-permute-start.15 = (bf16[1,64,512]{2,1,0:T(8,128)(2,1)S(1)}, bf16[1,64,512]{2,1,0:T(8,128)(2,1)S(1)}, u32[]{:S(2)}, u32[]{:S(2)}) collective-permute-start(bf16[1,64,512]{2,1,0:T(8,128)(2,1)S(1)} %collective-permute-done.11.refs_1_), channel_id=1, source_target_pairs={{0,1},{1,0},{2,3},{3,2},{4,5},{5,4},{6,7},{7,6},{8,9},{9,8},{10,11... | collective-permute-start | bytes 196616 | tf_op jit(solution)/shard_map/ppermute | solution.py:410
  81.1 1.7 %collective-permute-start.16 = (bf16[1,64,512]{2,1,0:T(8,128)(2,1)S(1)}, bf16[1,64,512]{2,1,0:T(8,128)(2,1)S(1)}, u32[]{:S(2)}, u32[]{:S(2)}) collective-permute-start(bf16[1,64,512]{2,1,0:T(8,128)(2,1)S(1)} %collective-permute-done.12.refs_2_), channel_id=1, source_target_pairs={{0,1},{1,0},{2,3},{3,2},{4,5},{5,4},{6,7},{7,6},{8,9},{9,8},{10,11... | collective-permute-start | bytes 196616 | tf_op jit(solution)/shard_map/ppermute | solution.py:410
  82.8 1.3 %collective-permute-start.17 = (bf16[1,64,512]{2,1,0:T(8,128)(2,1)S(1)}, bf16[1,64,512]{2,1,0:T(8,128)(2,1)S(1)}, u32[]{:S(2)}, u32[]{:S(2)}) collective-permute-start(bf16[1,64,512]{2,1,0:T(8,128)(2,1)S(1)} %collective-permute-done.13.refs_3_), channel_id=1, source_target_pairs={{0,1},{1,0},{2,3},{3,2},{4,5},{5,4},{6,7},{7,6},{8,9},{9,8},{10,11... | collective-permute-start | bytes 196616 | tf_op jit(solution)/shard_map/ppermute | solution.py:410

commit v5 on v4

--- a/solution.py
+++ b/solution.py
@@ -16,6 +16,7 @@
 bf16 = jnp.bfloat16
 f32 = jnp.float32
 LIMIT = 44 << 20
+CORNER = CP - 8
 LOG2E = 1.4426950408889634
 
 
@@ -168,11 +169,12 @@
     tokens = trows * half
     lat = qz_ref.shape[2]
 
-    pair = jnp.concatenate([top_ref[:CP], bot_ref[:CP]])
+    pair = jnp.concatenate([top_ref[...], bot_ref[...]])
     sides = []
     for n, ref in enumerate((top_ref, bot_ref)):
-        corners = turned(ref.at[CP:, :128], side_ref.at[n])
-        sides.append((corners[:, 0:1], corners[:, 16:17]))
+        corners = turned(ref.at[CP - 16 :, :128], side_ref.at[n])
+        at = CORNER - (CP - 16)
+        sides.append((corners[:, at : at + 1], corners[:, at + 1 : at + 2]))
     spread(pair, selection(cols), xs_ref, (0, rows + 1), sides)
 
     for h in range(HEADS):
@@ -327,15 +329,24 @@
 
 
 def out_kernel(*refs):
-    parts, (wo_ref, gain_ref, out_ref, all_ref) = refs[:HEADS], refs[HEADS:]
+    parts, (wo_ref, gain_ref, out_ref, all_ref, done_ref, sems) = refs[:HEADS], refs[HEADS:]
     half, place = HEADS // 2, places()
     for t in range(HEADS):
         value = parts[t][0]
         h = (t % half) ^ place[t // half]
         all_ref[pl.ds(pl.multiple_of(h * HD, HD), HD), :] = value.astype(f32)
     attended = jnp.transpose(all_ref[...]).astype(bf16)
-    mixed = jnp.dot(attended, wo_ref[...], preferred_element_type=f32)
-    out_ref[...] = rows_norm(mixed, 1) * gain_ref[...]
+    lat = attended.shape[0]
+    step = lat // 4
+    copies = []
+    for n in range(4):
+        at = slice(n * step, (n + 1) * step)
+        mixed = jnp.dot(attended[at], wo_ref[...], preferred_element_type=f32)
+        done_ref[at] = rows_norm(mixed, 1) * gain_ref[...]
+        copies.append(pltpu.make_async_copy(done_ref.at[at], out_ref.at[at], sems.at[n]))
+        copies[-1].start()
+    for copy in copies:
+        copy.wait()
 
 
 def shards(
@@ -360,20 +371,14 @@
     )(field)
     hl = lax.ppermute(last, "lon", ahead)
     hr = lax.ppermute(first, "lon", back)
-    wt, wvt = call(
-        weights_kernel,
-        [shape((width, 16 * CP), bf16), shape((width, width), bf16)],
-        2,
-        scratch=[VMEM((16 * CP, width), f32)],
-    )(stem_weight, kv_weight)
-    hl, hr, wt, wvt = lax.optimization_barrier((hl, hr, wt, wvt))
-
     def framed(line, r):
-        corners = [jnp.pad(h[r : r + 1], ((0, 15), (0, cols - 128))) for h in (hl, hr)]
-        return jnp.concatenate([line] + corners)
+        corners = [jnp.pad(h[r : r + 1], ((0, 0), (0, cols - 128))) for h in (hl, hr)]
+        return jnp.concatenate([line[:CORNER]] + corners + [line[CORNER + 2 :]])
 
     low, high = framed(low, 0), framed(high, rows - 1)
-    low, high, latents, hl = lax.optimization_barrier((low, high, latents, hl))
+    low, high, latents, hl, stem_weight, kv_weight = lax.optimization_barrier(
+        (low, high, latents, hl, stem_weight, kv_weight)
+    )
     up = [(i, i + 1) for i in range(nlat - 1)]
     down = [(t, s) for s, t in up]
     top = lax.ppermute(high, "lat", up)
@@ -382,6 +387,12 @@
         head_gain, latents, latent_gain[None, :], query_weight
     )
 
+    wt, wvt = call(
+        weights_kernel,
+        [shape((width, 16 * CP), bf16), shape((width, width), bf16)],
+        2,
+        scratch=[VMEM((16 * CP, width), f32)],
+    )(stem_weight, kv_weight)
     patches = shape((rows + 2, 4 * CP, half), bf16)
     xs = call(
         select_kernel,
@@ -430,7 +441,11 @@
     parts = [own] + [swap(own, *flips) for flips in near]
     parts += [swap(x, cores, cores) for x in parts]
     latent_out = call(
-        out_kernel, shape((lat, width), f32), HEADS + 2, scratch=[VMEM((width, lat), f32)]
+        out_kernel,
+        shape((lat, width), f32),
+        HEADS + 2,
+        out_spaces=[pl.ANY],
+        scratch=[VMEM((width, lat), f32), VMEM((lat, width), f32), pltpu.SemaphoreType.DMA((4,))],
     )(*parts, out_weight, out_gain[None, :])
     return (tok, latent_out)
 

time: 86.1 us -> 83.9 us (0.974)
  local copies, waits for them, and re-layouts: 6.17 us -> 2.86 us
  Pallas kernels: 38.7 us -> 39.7 us
    unnamed x29 -> x26, local copies, waits for them, and re-layouts: 5.15 us -> 1.82 us
    ppermute x14, waiting for transfers between devices: 17.6 us -> 16.2 us  [swap(): return lax.ppermute(x, ('lat', 'lon'), pairs)]
    ppermute x1, waiting for transfers between devices: 0.01 us -> 1.23 us  [shards(): hl = lax.ppermute(last, 'lon', ahead)]
    pallas_call x6, Pallas kernels: 38.7 us -> 39.7 us  [run(): return fn(*args[:smem], *held)]
    ppermute x14, starting transfers between devices: 12.3 us -> 13.2 us  [swap(): return lax.ppermute(x, ('lat', 'lon'), pairs)]
  transfers between devices with their start and end apart: 18 -> 18, of which waited for: 11 -> 14; matrix products, arithmetic and copies ran while one was open for 0% -> 0% of each run, Pallas kernels for 5% -> 5%
where the time goes in v5:
time: 83.9 us; the launch traced here: 83.7 us
  Pallas kernels  39.7 us (47%)
  starting transfers between devices  21.2 us (25%)
  waiting for transfers between devices  18.3 us (22%)
  local copies, waits for them, and re-layouts  2.86 us (3%)
  between operations  0.98 us (1%)
    pallas_call x6, Pallas kernels, run(): return fn(*args[:smem], *held)  39.7 us
    ppermute x14, waiting for transfers between devices, swap(): return lax.ppermute(x, ('lat', 'lon'), pairs)  16.2 us
    ppermute x14, starting transfers between devices, swap(): return lax.ppermute(x, ('lat', 'lon'), pairs)  13.2 us
    ppermute x1, starting transfers between devices, shards(): top = lax.ppermute(high, 'lat', up)  4.12 us
    ppermute x1, starting transfers between devices, shards(): hr = lax.ppermute(first, 'lon', back)  2.01 us
    unnamed x26, local copies, waits for them, and re-layouts  1.82 us
  transfers between devices with their start and end apart: 18, of which 14 were waited for; matrix products, arithmetic and copies ran while one was open for 0% of the time, Pallas kernels for 5%

profile of v5, /device:TPU:0, one launch (start us, length us, event | category | flops | bytes accessed | tf_op | source)
XLA Modules:
  0.0 83.7 jit_solution(14627153933028056033)
XLA Ops:
  0.6 0.0 copy-start
  0.6 1.6 %copy-done = bf16[69,32,512]{2,1,0:T(8,128)(2,1)S(1)} copy-done((bf16[69,32,512]{2,1,0:T(8,128)(2,1)S(1)}, bf16[69,32,512]{2,1,0:T(8,128)(2,1)}, u32[]{:S(2)}) %copy-start) | copy-done | bytes 2261016
  2.3 0.0 copy-start.7
  2.3 0.0 copy-start.11
  2.3 0.7 shard_map.122
  3.0 0.5 collective-permute-start
  3.5 2.0 %collective-permute-start.1 = (bf16[32,128]{1,0:T(8,128)(2,1)S(1)}, bf16[32,128]{1,0:T(8,128)(2,1)S(1)}, u32[]{:S(2)}, u32[]{:S(2)}) collective-permute-start(bf16[32,128]{1,0:T(8,128)(2,1)S(1)} %get-tuple-element.19), channel_id=1, source_target_pairs={{1,0},{2,1},{3,2},{0,3},{5,4},{6,5},{7,6},{4,7},{9,8},{10,9},{11,1... | collective-permute-start | bytes 24584 | tf_op jit(solution)/shard_map/ppermute | solution.py:373
  5.6 1.2 %collective-permute-done.hl_ref = bf16[32,128]{1,0:T(8,128)(2,1)S(1)} collective-permute-done((bf16[32,128]{1,0:T(8,128)(2,1)S(1)}, bf16[32,128]{1,0:T(8,128)(2,1)S(1)}, u32[]{:S(2)}, u32[]{:S(2)}) %collective-permute-start) | collective-permute-done | bytes 8224 | tf_op jit(solution)/shard_map/ppermute | solution.py:372
  6.8 0.1 collective-permute-done.1.hr_ref
  6.9 4.1 %collective-permute-start.2 = (bf16[80,512]{1,0:T(8,128)(2,1)S(1)}, bf16[80,512]{1,0:T(8,128)(2,1)S(1)}, u32[]{:S(2)}, u32[]{:S(2)}) collective-permute-start(bf16[80,512]{1,0:T(8,128)(2,1)S(1)} %get-tuple-element.22), channel_id=1, source_target_pairs={{0,4},{4,8},{8,12},{12,16},{16,20},{20,24},{24,28},{1,5},{5,9},{9,... | collective-permute-start | bytes 245768 | tf_op jit(solution)/shard_map/ppermute | solution.py:384
  11.1 1.3 %collective-permute-start.3 = (bf16[80,512]{1,0:T(8,128)(2,1)S(1)}, bf16[80,512]{1,0:T(8,128)(2,1)S(1)}, u32[]{:S(2)}, u32[]{:S(2)}) collective-permute-start(bf16[80,512]{1,0:T(8,128)(2,1)S(1)} %get-tuple-element.23), channel_id=1, source_target_pairs={{4,0},{8,4},{12,8},{16,12},{20,16},{24,20},{28,24},{5,1},{9,5},{13... | collective-permute-start | bytes 245768 | tf_op jit(solution)/shard_map/ppermute | solution.py:385
  12.4 0.0 copy-done.2
  12.4 0.0 copy-done.3
  12.4 0.5 shard_map.124
  12.9 0.0 copy-start.1
  13.0 1.5 %shard_map.125.qz_ref = bf16[8,256,512]{2,1,0:T(8,128)(2,1)S(1)} custom-call(f32[8]{0:T(128)S(1)} %copy-done.11, f32[512,512]{1,0:T(8,128)S(1)} %copy-done.4, f32[1,512]{1,0:T(1,128)S(1)} %bitcast.23, bf16[512,512]{1,0:T(8,128)(2,1)S(1)} %copy-done.5), custom_call_target="tpu_custom_call" | custom-call | tf_op jit(solution)/shard_map/pallas_call | solution.py:42
  14.4 0.1 copy-done.1
  14.6 2.5 %shard_map.123.xs_in = bf16[34,320,256]{2,1,0:T(8,128)(2,1)S(1)} custom-call(bf16[69,32,512]{2,1,0:T(8,128)(2,1)S(1)} %copy-done.1, bf16[32,128]{1,0:T(8,128)(2,1)S(1)} %collective-permute-done.hl_ref, bf16[32,128]{1,0:T(8,128)(2,1)S(1)} %collective-permute-done.1.hr_ref), custom_call_target="tpu_custom_call" | custom-call | tf_op jit(solution)/shard_map/pallas_call | solution.py:42
  17.1 0.0 collective-permute-done.2.top_ref
  17.1 0.8 collective-permute-done.3.bot_ref
  17.9 0.0 copy-done.8
  17.9 32.9 %shard_map.126 = (bf16[16,256,512]{2,1,0:T(8,128)(2,1)}, bf16[4,80,512]{2,1,0:T(8,128)(2,1)S(1)}, bf16[4,80,512]{2,1,0:T(8,128)(2,1)S(1)}, bf16[34,320,256]{2,1,0:T(8,128)(2,1)S(1)}) custom-call(bf16[34,320,256]{2,1,0:T(8,128)(2,1)S(1)} %shard_map.123.xs_in, bf16[80,512]{1,0:T(8,128)(2,1)S(1)} %collective-permute-done.2.top_ref, ...), custom_call_target="tpu_custom_call", output_to_operand_aliasing={{3}: (0, {})} | custom-call | tf_op jit(solution)/shard_map/pallas_call | solution.py:42
  50.8 0.0 copy-start.6
  50.9 0.0 copy-start.10
  50.9 0.6 collective-permute-start.4
  51.5 1.2 %collective-permute-done.4 = bf16[4,80,512]{2,1,0:T(8,128)(2,1)S(1)} collective-permute-done((bf16[4,80,512]{2,1,0:T(8,128)(2,1)S(1)}, bf16[4,80,512]{2,1,0:T(8,128)(2,1)S(1)}, u32[]{:S(2)}, u32[]{:S(2)}) %collective-permute-start.4) | collective-permute-done | bytes 327712 | tf_op jit(solution)/shard_map/ppermute | solution.py:421
  52.7 0.1 fusion.15
  52.8 0.1 reduce-precision_convert_fusion
  52.9 0.3 concatenate.30
  53.2 0.1 add_convert_fusion
  53.3 0.4 concatenate.31
  53.7 3.0 %collective-permute-start.7 = (bf16[1,80,512]{2,1,0:T(8,128)(2,1)S(1)}, bf16[1,80,512]{2,1,0:T(8,128)(2,1)S(1)}, u32[]{:S(2)}, u32[]{:S(2)}) collective-permute-start(bf16[1,80,512]{2,1,0:T(8,128)(2,1)S(1)} %get-tuple-element.61), channel_id=1, source_target_pairs={{0,6},{1,7},{2,4},{3,5},{4,2},{5,3},{6,0},{7,1},{8,14},{9,15},{10,... | collective-permute-start | bytes 245768 | tf_op jit(solution)/shard_map/ppermute | solution.py:421
  56.7 0.9 %collective-permute-start.6 = (bf16[1,80,512]{2,1,0:T(8,128)(2,1)S(1)}, bf16[1,80,512]{2,1,0:T(8,128)(2,1)S(1)}, u32[]{:S(2)}, u32[]{:S(2)}) collective-permute-start(bf16[1,80,512]{2,1,0:T(8,128)(2,1)S(1)} %get-tuple-element.62), channel_id=1, source_target_pairs={{0,2},{1,5},{2,0},{3,7},{4,6},{5,1},{6,4},{7,3},{8,10},{9,13},{10,... | collective-permute-start | bytes 245768 | tf_op jit(solution)/shard_map/ppermute | solution.py:421
  57.6 0.0 collective-permute-start.5
  57.6 1.9 %collective-permute-done.7 = bf16[1,80,512]{2,1,0:T(8,128)(2,1)S(1)} collective-permute-done((bf16[1,80,512]{2,1,0:T(8,128)(2,1)S(1)}, bf16[1,80,512]{2,1,0:T(8,128)(2,1)S(1)}, u32[]{:S(2)}, u32[]{:S(2)}) %collective-permute-start.7) | collective-permute-done | bytes 81952 | tf_op jit(solution)/shard_map/ppermute | solution.py:421
  59.6 1.7 %collective-permute-done.6 = bf16[1,80,512]{2,1,0:T(8,128)(2,1)S(1)} collective-permute-done((bf16[1,80,512]{2,1,0:T(8,128)(2,1)S(1)}, bf16[1,80,512]{2,1,0:T(8,128)(2,1)S(1)}, u32[]{:S(2)}, u32[]{:S(2)}) %collective-permute-start.6) | collective-permute-done | bytes 81952 | tf_op jit(solution)/shard_map/ppermute | solution.py:421
  61.2 0.9 %collective-permute-done.5 = bf16[1,80,512]{2,1,0:T(8,128)(2,1)S(1)} collective-permute-done((bf16[1,80,512]{2,1,0:T(8,128)(2,1)S(1)}, bf16[1,80,512]{2,1,0:T(8,128)(2,1)S(1)}, u32[]{:S(2)}, u32[]{:S(2)}) %collective-permute-start.5) | collective-permute-done | bytes 81952 | tf_op jit(solution)/shard_map/ppermute | solution.py:421
  62.1 0.1 reduce-precision_convert_fusion.4
  62.2 0.1 add_convert_fusion.1
  62.3 0.2 concatenate.33
  62.5 4.6 %collective-permute-start.10 = (bf16[1,80,512]{2,1,0:T(8,128)(2,1)S(1)}, bf16[1,80,512]{2,1,0:T(8,128)(2,1)S(1)}, u32[]{:S(2)}, u32[]{:S(2)}) collective-permute-start(bf16[1,80,512]{2,1,0:T(8,128)(2,1)S(1)} %concatenate.33), channel_id=1, source_target_pairs={{0,24},{1,25},{2,26},{3,27},{4,28},{5,29},{6,30},{7,31},{8,16},{9,... | collective-permute-start | bytes 245768 | tf_op jit(solution)/shard_map/ppermute | solution.py:421
  67.0 0.2 concatenate.32
  67.2 0.1 collective-permute-start.9
  67.3 0.6 collective-permute-start.8
  67.8 2.2 %collective-permute-done.10 = bf16[1,80,512]{2,1,0:T(8,128)(2,1)S(1)} collective-permute-done((bf16[1,80,512]{2,1,0:T(8,128)(2,1)S(1)}, bf16[1,80,512]{2,1,0:T(8,128)(2,1)S(1)}, u32[]{:S(2)}, u32[]{:S(2)}) %collective-permute-start.10) | collective-permute-done | bytes 81952 | tf_op jit(solution)/shard_map/ppermute | solution.py:421
  70.0 4.1 %collective-permute-done.9 = bf16[1,80,512]{2,1,0:T(8,128)(2,1)S(1)} collective-permute-done((bf16[1,80,512]{2,1,0:T(8,128)(2,1)S(1)}, bf16[1,80,512]{2,1,0:T(8,128)(2,1)S(1)}, u32[]{:S(2)}, u32[]{:S(2)}) %collective-permute-start.9) | collective-permute-done | bytes 81952 | tf_op jit(solution)/shard_map/ppermute | solution.py:421
  74.1 0.0 collective-permute-done.8
  74.1 0.1 multiply_add_fusion
  74.2 0.1 divide_convert_fusion.refs_0_
  74.3 0.6 collective-permute-start.11
  74.8 0.9 %collective-permute-start.12 = (bf16[1,64,512]{2,1,0:T(8,128)(2,1)S(1)}, bf16[1,64,512]{2,1,0:T(8,128)(2,1)S(1)}, u32[]{:S(2)}, u32[]{:S(2)}) collective-permute-start(bf16[1,64,512]{2,1,0:T(8,128)(2,1)S(1)} %divide_convert_fusion.refs_0_), channel_id=1, source_target_pairs={{0,2},{1,5},{2,0},{3,7},{4,6},{5,1},{6,4},{7,3},{8,10},{9,13},{10,... | collective-permute-start | bytes 196616 | tf_op jit(solution)/shard_map/ppermute | solution.py:421
  75.7 2.1 %collective-permute-start.13 = (bf16[1,64,512]{2,1,0:T(8,128)(2,1)S(1)}, bf16[1,64,512]{2,1,0:T(8,128)(2,1)S(1)}, u32[]{:S(2)}, u32[]{:S(2)}) collective-permute-start(bf16[1,64,512]{2,1,0:T(8,128)(2,1)S(1)} %divide_convert_fusion.refs_0_), channel_id=1, source_target_pairs={{0,6},{1,7},{2,4},{3,5},{4,2},{5,3},{6,0},{7,1},{8,14},{9,15},{10,... | collective-permute-start | bytes 196616 | tf_op jit(solution)/shard_map/ppermute | solution.py:421
  77.8 0.0 collective-permute-start.14
  77.8 1.2 %collective-permute-done.11.refs_1_ = bf16[1,64,512]{2,1,0:T(8,128)(2,1)S(1)} collective-permute-done((bf16[1,64,512]{2,1,0:T(8,128)(2,1)S(1)}, bf16[1,64,512]{2,1,0:T(8,128)(2,1)S(1)}, u32[]{:S(2)}, u32[]{:S(2)}) %collective-permute-start.11) | collective-permute-done | bytes 65568 | tf_op jit(solution)/shard_map/ppermute | solution.py:421
  79.0 0.0 collective-permute-start.15
  79.0 0.7 collective-permute-done.12.refs_2_
  79.8 0.0 collective-permute-start.16
  79.8 1.1 %collective-permute-done.13.refs_3_ = bf16[1,64,512]{2,1,0:T(8,128)(2,1)S(1)} collective-permute-done((bf16[1,64,512]{2,1,0:T(8,128)(2,1)S(1)}, bf16[1,64,512]{2,1,0:T(8,128)(2,1)S(1)}, u32[]{:S(2)}, u32[]{:S(2)}) %collective-permute-start.13) | collective-permute-done | bytes 65568 | tf_op jit(solution)/shard_map/ppermute | solution.py:421
  80.8 0.0 collective-permute-start.17
  80.8 0.0 collective-permute-done.14.refs_4_
  80.8 0.0 collective-permute-done.15.refs_5_
  80.9 0.2 collective-permute-done.16.refs_6_
  81.0 1.1 %collective-permute-done.17.refs_7_ = bf16[1,64,512]{2,1,0:T(8,128)(2,1)S(1)} collective-permute-done((bf16[1,64,512]{2,1,0:T(8,128)(2,1)S(1)}, bf16[1,64,512]{2,1,0:T(8,128)(2,1)S(1)}, u32[]{:S(2)}, u32[]{:S(2)}) %collective-permute-start.17) | collective-permute-done | bytes 65568 | tf_op jit(solution)/shard_map/ppermute | solution.py:421
  82.1 1.6 %shard_map.127 = f32[512,512]{1,0:T(8,128)} custom-call(bf16[1,64,512]{2,1,0:T(8,128)(2,1)S(1)} %divide_convert_fusion.refs_0_, bf16[1,64,512]{2,1,0:T(8,128)(2,1)S(1)} %collective-permute-done.11.refs_1_, bf16[1,64,512]{2,1,0:T(8,128)(2,1)S(1)} %collective-permute-done.12.refs_2_, bf16[1,64,512]{2,1,0:T(8,128)(2,1)S(1)} %collective-permute-done.13.refs_3_, ...), custom_call_target="tpu_custom_call" | custom-call | tf_op jit(solution)/shard_map/pallas_call | solution.py:42
  (38 shorter events, 0.2 us)
Async XLA Ops:
  0.6 1.6 %copy-start = (bf16[69,32,512]{2,1,0:T(8,128)(2,1)S(1)}, bf16[69,32,512]{2,1,0:T(8,128)(2,1)}, u32[]{:S(2)}) copy-start(bf16[69,32,512]{2,1,0:T(8,128)(2,1)} %x_ref.3) | copy-start | bytes 6782980
  2.3 10.1 %copy-start.2 = (bf16[512,1024]{1,0:T(8,128)(2,1)S(1)}, bf16[512,1024]{1,0:T(8,128)(2,1)}, u32[]{:S(2)}) copy-start(bf16[512,1024]{1,0:T(8,128)(2,1)} %kv_ref.1) | copy-start | bytes 3145732
  2.3 10.1 %copy-start.3 = (bf16[1104,512]{1,0:T(8,128)(2,1)S(1)}, bf16[1104,512]{1,0:T(8,128)(2,1)}, u32[]{:S(2)}) copy-start(bf16[1104,512]{1,0:T(8,128)(2,1)} %w_ref) | copy-start | bytes 3391492
  2.3 10.7 %copy-start.4 = (f32[512,512]{1,0:T(8,128)S(1)}, f32[512,512]{1,0:T(8,128)}, u32[]{:S(2)}) copy-start(f32[512,512]{1,0:T(8,128)} %latents_ref) | copy-start | bytes 3145732
  2.3 10.7 %copy-start.5 = (bf16[512,512]{1,0:T(8,128)(2,1)S(1)}, bf16[512,512]{1,0:T(8,128)(2,1)}, u32[]{:S(2)}) copy-start(bf16[512,512]{1,0:T(8,128)(2,1)} %qw_ref.1) | copy-start | bytes 1572868
  2.3 10.7 %copy-start.7 = (f32[512]{0:T(512)S(1)}, f32[512]{0:T(512)}, u32[]{:S(2)}) copy-start(f32[512]{0:T(512)} %param.17) | copy-start | bytes 6148
  2.3 10.7 %copy-start.11 = (f32[8]{0:T(128)S(1)}, f32[8]{0:T(128)}, u32[]{:S(2)}) copy-start(f32[8]{0:T(128)} %gain_ref.1) | copy-start | bytes 100
  3.0 3.8 %collective-permute-start = (bf16[32,128]{1,0:T(8,128)(2,1)S(1)}, bf16[32,128]{1,0:T(8,128)(2,1)S(1)}, u32[]{:S(2)}, u32[]{:S(2)}) collective-permute-start(bf16[32,128]{1,0:T(8,128)(2,1)S(1)} %get-tuple-element.18), channel_id=1, source_target_pairs={{0,1},{1,2},{2,3},{3,0},{4,5},{5,6},{6,7},{7,4},{8,9},{9,10},{10,1... | collective-permute-start | bytes 24584 | tf_op jit(solution)/shard_map/ppermute | solution.py:372
  3.5 3.4 %collective-permute-start.1 = (bf16[32,128]{1,0:T(8,128)(2,1)S(1)}, bf16[32,128]{1,0:T(8,128)(2,1)S(1)}, u32[]{:S(2)}, u32[]{:S(2)}) collective-permute-start(bf16[32,128]{1,0:T(8,128)(2,1)S(1)} %get-tuple-element.19), channel_id=1, source_target_pairs={{1,0},{2,1},{3,2},{0,3},{5,4},{6,5},{7,6},{4,7},{9,8},{10,9},{11,1... | collective-permute-start | bytes 24584 | tf_op jit(solution)/shard_map/ppermute | solution.py:373
  6.9 10.2 %collective-permute-start.2 = (bf16[80,512]{1,0:T(8,128)(2,1)S(1)}, bf16[80,512]{1,0:T(8,128)(2,1)S(1)}, u32[]{:S(2)}, u32[]{:S(2)}) collective-permute-start(bf16[80,512]{1,0:T(8,128)(2,1)S(1)} %get-tuple-element.22), channel_id=1, source_target_pairs={{0,4},{4,8},{8,12},{12,16},{16,20},{20,24},{24,28},{1,5},{5,9},{9,... | collective-permute-start | bytes 245768 | tf_op jit(solution)/shard_map/ppermute | solution.py:384
  11.1 6.9 %collective-permute-start.3 = (bf16[80,512]{1,0:T(8,128)(2,1)S(1)}, bf16[80,512]{1,0:T(8,128)(2,1)S(1)}, u32[]{:S(2)}, u32[]{:S(2)}) collective-permute-start(bf16[80,512]{1,0:T(8,128)(2,1)S(1)} %get-tuple-element.23), channel_id=1, source_target_pairs={{4,0},{8,4},{12,8},{16,12},{20,16},{24,20},{28,24},{5,1},{9,5},{13... | collective-permute-start | bytes 245768 | tf_op jit(solution)/shard_map/ppermute | solution.py:385
  12.9 1.6 %copy-start.1 = (bf16[69,32,512]{2,1,0:T(8,128)(2,1)S(1)}, bf16[69,32,512]{2,1,0:T(8,128)(2,1)}, u32[]{:S(2)}) copy-start(bf16[69,32,512]{2,1,0:T(8,128)(2,1)} %x_ref.3) | copy-start | bytes 6782980
  14.6 3.3 %copy-start.8 = (f32[512]{0:T(512)S(1)}, f32[512]{0:T(512)}, u32[]{:S(2)}) copy-start(f32[512]{0:T(512)} %param.13) | copy-start | bytes 6148
  14.6 3.3 %copy-start.9 = (f32[512]{0:T(512)S(1)}, f32[512]{0:T(512)}, u32[]{:S(2)}) copy-start(f32[512]{0:T(512)} %param.14) | copy-start | bytes 6148
  50.8 31.3 %copy-start.6 = (bf16[512,512]{1,0:T(8,128)(2,1)S(1)}, bf16[512,512]{1,0:T(8,128)(2,1)}, u32[]{:S(2)}) copy-start(bf16[512,512]{1,0:T(8,128)(2,1)} %refs_8_.1) | copy-start | bytes 1572868
  50.9 31.2 %copy-start.10 = (f32[512]{0:T(512)S(1)}, f32[512]{0:T(512)}, u32[]{:S(2)}) copy-start(f32[512]{0:T(512)} %param.21) | copy-start | bytes 6148
  50.9 1.8 %collective-permute-start.4 = (bf16[4,80,512]{2,1,0:T(8,128)(2,1)S(1)}, bf16[4,80,512]{2,1,0:T(8,128)(2,1)S(1)}, u32[]{:S(2)}, u32[]{:S(2)}) collective-permute-start(bf16[4,80,512]{2,1,0:T(8,128)(2,1)S(1)} %get-tuple-element.31), channel_id=1, source_target_pairs={{0,1},{1,0},{2,3},{3,2},{4,5},{5,4},{6,7},{7,6},{8,9},{9,8},{10,11... | collective-permute-start | bytes 983048 | tf_op jit(solution)/shard_map/ppermute | solution.py:421
  53.7 5.8 %collective-permute-start.7 = (bf16[1,80,512]{2,1,0:T(8,128)(2,1)S(1)}, bf16[1,80,512]{2,1,0:T(8,128)(2,1)S(1)}, u32[]{:S(2)}, u32[]{:S(2)}) collective-permute-start(bf16[1,80,512]{2,1,0:T(8,128)(2,1)S(1)} %get-tuple-element.61), channel_id=1, source_target_pairs={{0,6},{1,7},{2,4},{3,5},{4,2},{5,3},{6,0},{7,1},{8,14},{9,15},{10,... | collective-permute-start | bytes 245768 | tf_op jit(solution)/shard_map/ppermute | solution.py:421
  56.7 4.5 %collective-permute-start.6 = (bf16[1,80,512]{2,1,0:T(8,128)(2,1)S(1)}, bf16[1,80,512]{2,1,0:T(8,128)(2,1)S(1)}, u32[]{:S(2)}, u32[]{:S(2)}) collective-permute-start(bf16[1,80,512]{2,1,0:T(8,128)(2,1)S(1)} %get-tuple-element.62), channel_id=1, source_target_pairs={{0,2},{1,5},{2,0},{3,7},{4,6},{5,1},{6,4},{7,3},{8,10},{9,13},{10,... | collective-permute-start | bytes 245768 | tf_op jit(solution)/shard_map/ppermute | solution.py:421
  57.6 4.4 %collective-permute-start.5 = (bf16[1,80,512]{2,1,0:T(8,128)(2,1)S(1)}, bf16[1,80,512]{2,1,0:T(8,128)(2,1)S(1)}, u32[]{:S(2)}, u32[]{:S(2)}) collective-permute-start(bf16[1,80,512]{2,1,0:T(8,128)(2,1)S(1)} %get-tuple-element.60), channel_id=1, source_target_pairs={{0,4},{1,3},{2,6},{3,1},{4,0},{5,7},{6,2},{7,5},{8,12},{9,11},{10,... | collective-permute-start | bytes 245768 | tf_op jit(solution)/shard_map/ppermute | solution.py:421
  62.5 7.5 %collective-permute-start.10 = (bf16[1,80,512]{2,1,0:T(8,128)(2,1)S(1)}, bf16[1,80,512]{2,1,0:T(8,128)(2,1)S(1)}, u32[]{:S(2)}, u32[]{:S(2)}) collective-permute-start(bf16[1,80,512]{2,1,0:T(8,128)(2,1)S(1)} %concatenate.33), channel_id=1, source_target_pairs={{0,24},{1,25},{2,26},{3,27},{4,28},{5,29},{6,30},{7,31},{8,16},{9,... | collective-permute-start | bytes 245768 | tf_op jit(solution)/shard_map/ppermute | solution.py:421
  67.2 6.9 %collective-permute-start.9 = (bf16[1,80,512]{2,1,0:T(8,128)(2,1)S(1)}, bf16[1,80,512]{2,1,0:T(8,128)(2,1)S(1)}, u32[]{:S(2)}, u32[]{:S(2)}) collective-permute-start(bf16[1,80,512]{2,1,0:T(8,128)(2,1)S(1)} %concatenate.33), channel_id=1, source_target_pairs={{0,16},{1,17},{2,18},{3,19},{4,20},{5,21},{6,22},{7,23},{8,24},{9,... | collective-permute-start | bytes 245768 | tf_op jit(solution)/shard_map/ppermute | solution.py:421
  67.3 6.8 %collective-permute-start.8 = (bf16[1,80,512]{2,1,0:T(8,128)(2,1)S(1)}, bf16[1,80,512]{2,1,0:T(8,128)(2,1)S(1)}, u32[]{:S(2)}, u32[]{:S(2)}) collective-permute-start(bf16[1,80,512]{2,1,0:T(8,128)(2,1)S(1)} %concatenate.33), channel_id=1, source_target_pairs={{0,8},{1,9},{2,10},{3,11},{4,12},{5,13},{6,14},{7,15},{8,0},{9,1},... | collective-permute-start | bytes 245768 | tf_op jit(solution)/shard_map/ppermute | solution.py:421
  74.3 4.8 %collective-permute-start.11 = (bf16[1,64,512]{2,1,0:T(8,128)(2,1)S(1)}, bf16[1,64,512]{2,1,0:T(8,128)(2,1)S(1)}, u32[]{:S(2)}, u32[]{:S(2)}) collective-permute-start(bf16[1,64,512]{2,1,0:T(8,128)(2,1)S(1)} %divide_convert_fusion.refs_0_), channel_id=1, source_target_pairs={{0,4},{1,3},{2,6},{3,1},{4,0},{5,7},{6,2},{7,5},{8,12},{9,11},{10,... | collective-permute-start | bytes 196616 | tf_op jit(solution)/shard_map/ppermute | solution.py:421
  74.8 4.9 %collective-permute-start.12 = (bf16[1,64,512]{2,1,0:T(8,128)(2,1)S(1)}, bf16[1,64,512]{2,1,0:T(8,128)(2,1)S(1)}, u32[]{:S(2)}, u32[]{:S(2)}) collective-permute-start(bf16[1,64,512]{2,1,0:T(8,128)(2,1)S(1)} %divide_convert_fusion.refs_0_), channel_id=1, source_target_pairs={{0,2},{1,5},{2,0},{3,7},{4,6},{5,1},{6,4},{7,3},{8,10},{9,13},{10,... | collective-permute-start | bytes 196616 | tf_op jit(solution)/shard_map/ppermute | solution.py:421
  75.7 5.2 %collective-permute-start.13 = (bf16[1,64,512]{2,1,0:T(8,128)(2,1)S(1)}, bf16[1,64,512]{2,1,0:T(8,128)(2,1)S(1)}, u32[]{:S(2)}, u32[]{:S(2)}) collective-permute-start(bf16[1,64,512]{2,1,0:T(8,128)(2,1)S(1)} %divide_convert_fusion.refs_0_), channel_id=1, source_target_pairs={{0,6},{1,7},{2,4},{3,5},{4,2},{5,3},{6,0},{7,1},{8,14},{9,15},{10,... | collective-permute-start | bytes 196616 | tf_op jit(solution)/shard_map/ppermute | solution.py:421
  77.8 3.0 %collective-permute-start.14 = (bf16[1,64,512]{2,1,0:T(8,128)(2,1)S(1)}, bf16[1,64,512]{2,1,0:T(8,128)(2,1)S(1)}, u32[]{:S(2)}, u32[]{:S(2)}) collective-permute-start(bf16[1,64,512]{2,1,0:T(8,128)(2,1)S(1)} %divide_convert_fusion.refs_0_), channel_id=1, source_target_pairs={{0,1},{1,0},{2,3},{3,2},{4,5},{5,4},{6,7},{7,6},{8,9},{9,8},{10,11... | collective-permute-start | bytes 196616 | tf_op jit(solution)/shard_map/ppermute | solution.py:421
  79.0 1.8 %collective-permute-start.15 = (bf16[1,64,512]{2,1,0:T(8,128)(2,1)S(1)}, bf16[1,64,512]{2,1,0:T(8,128)(2,1)S(1)}, u32[]{:S(2)}, u32[]{:S(2)}) collective-permute-start(bf16[1,64,512]{2,1,0:T(8,128)(2,1)S(1)} %collective-permute-done.11.refs_1_), channel_id=1, source_target_pairs={{0,1},{1,0},{2,3},{3,2},{4,5},{5,4},{6,7},{7,6},{8,9},{9,8},{10,11... | collective-permute-start | bytes 196616 | tf_op jit(solution)/shard_map/ppermute | solution.py:421
  79.8 1.3 %collective-permute-start.16 = (bf16[1,64,512]{2,1,0:T(8,128)(2,1)S(1)}, bf16[1,64,512]{2,1,0:T(8,128)(2,1)S(1)}, u32[]{:S(2)}, u32[]{:S(2)}) collective-permute-start(bf16[1,64,512]{2,1,0:T(8,128)(2,1)S(1)} %collective-permute-done.12.refs_2_), channel_id=1, source_target_pairs={{0,1},{1,0},{2,3},{3,2},{4,5},{5,4},{6,7},{7,6},{8,9},{9,8},{10,11... | collective-permute-start | bytes 196616 | tf_op jit(solution)/shard_map/ppermute | solution.py:421
  80.8 1.3 %collective-permute-start.17 = (bf16[1,64,512]{2,1,0:T(8,128)(2,1)S(1)}, bf16[1,64,512]{2,1,0:T(8,128)(2,1)S(1)}, u32[]{:S(2)}, u32[]{:S(2)}) collective-permute-start(bf16[1,64,512]{2,1,0:T(8,128)(2,1)S(1)} %collective-permute-done.13.refs_3_), channel_id=1, source_target_pairs={{0,1},{1,0},{2,3},{3,2},{4,5},{5,4},{6,7},{7,6},{8,9},{9,8},{10,11... | collective-permute-start | bytes 196616 | tf_op jit(solution)/shard_map/ppermute | solution.py:421

commit v6 on v5

--- a/solution.py
+++ b/solution.py
@@ -20,7 +20,7 @@
 LOG2E = 1.4426950408889634
 
 
-def call(kernel, out, n_in, scratch=(), smem=0, out_spaces=None, aliases=None):
+def call(kernel, out, n_in, scratch=(), smem=0, out_spaces=None, aliases=None, space=VMEM):
     outs = out if isinstance(out, (list, tuple)) else [out]
     spaces = out_spaces or [VMEM] * len(outs)
     specs = [pl.BlockSpec(memory_space=s) for s in spaces]
@@ -30,7 +30,7 @@
         kernel,
         out_shape=kept[0] if single else kept,
         in_specs=[pl.BlockSpec(memory_space=pltpu.SMEM)] * smem
-        + [pl.BlockSpec(memory_space=VMEM)] * n_in,
+        + [pl.BlockSpec(memory_space=space)] * n_in,
         out_specs=specs[0] if single else specs,
         scratch_shapes=list(scratch),
         input_output_aliases=aliases or {},
@@ -38,7 +38,7 @@
     )
 
     def run(*args):
-        held = [pltpu.with_memory_space_constraint(x, VMEM) for x in args[smem:]]
+        held = [pltpu.with_memory_space_constraint(x, space) for x in args[smem:]]
         return fn(*args[:smem], *held)
 
     return run
@@ -95,19 +95,30 @@
     return 4 * core + yx + core * (xy - yx), 4 * (1 - core) + xy + core * (yx - xy)
 
 
-def edges_kernel(x_ref, first_ref, last_ref, low_ref, high_ref, row_ref):
+def columns_kernel(x_ref, first_ref, last_ref, tile_ref, sems):
     chan, rows, cols = x_ref.shape
     lane = lax.broadcasted_iota(jnp.int32, (rows, 128), 1)
-    first = jnp.zeros((rows, 128), f32)
-    last = jnp.zeros((rows, 128), f32)
+    ends = ((last_ref, cols - 128, 127), (first_ref, 0, 0))
+    copies = [
+        pltpu.make_async_copy(x_ref.at[:, :, at : at + 128], tile_ref.at[n], sems.at[n])
+        for n, (_, at, _) in enumerate(ends)
+    ]
+    for copy in copies:
+        copy.start()
+    for n, (out_ref, _, c) in enumerate(ends):
+        copies[n].wait()
+        side = jnp.zeros((rows, 128), f32)
+        for ch in range(chan):
+            side = jnp.where(lane == ch, tile_ref[n, ch].astype(f32)[:, c : c + 1], side)
+        out_ref[...] = side.astype(bf16)
+
+
+def lines_kernel(x_ref, low_ref, high_ref, row_ref):
+    chan, rows, cols = x_ref.shape
     row_ref[...] = jnp.zeros(row_ref.shape, f32)
     for ch in range(chan):
-        first = jnp.where(lane == ch, x_ref[ch, :, :128].astype(f32)[:, :1], first)
-        last = jnp.where(lane == ch, x_ref[ch, :, cols - 128 :].astype(f32)[:, 127:], last)
         row_ref[0, ch : ch + 1, :] = x_ref[ch, :16, :].astype(f32)[:1]
         row_ref[1, ch : ch + 1, :] = x_ref[ch, rows - 16 :, :].astype(f32)[15:]
-    first_ref[...] = first.astype(bf16)
-    last_ref[...] = last.astype(bf16)
     low_ref[...] = row_ref[0].astype(bf16)
     high_ref[...] = row_ref[1].astype(bf16)
 
@@ -160,7 +171,7 @@
 
 
 def encode_kernel(
-    xs_in, top_ref, bot_ref, wt_ref, bias_ref, gain_ref, kv_ref, wvt_ref, qz_ref,
+    xs_in, near_ref, far_ref, wt_ref, bias_ref, gain_ref, kv_ref, wvt_ref, qz_ref,
     tok_out, keep_ref, send_ref, xs_ref,
     st_ref, tok_ref, k_ref, vt_ref, s_ref, col_ref, state_ref, peak_ref, side_ref, sems,
 ):
@@ -169,10 +180,13 @@
     tokens = trows * half
     lat = qz_ref.shape[2]
 
-    pair = jnp.concatenate([top_ref[...], bot_ref[...]])
+    odd = lax.axis_index("lat") & 1
+    near, far = near_ref[...].astype(f32), far_ref[...].astype(f32)
+    ends = (jnp.where(odd == 1, near, far), jnp.where(odd == 1, far, near))
+    pair = jnp.concatenate(ends).astype(bf16)
     sides = []
-    for n, ref in enumerate((top_ref, bot_ref)):
-        corners = turned(ref.at[CP - 16 :, :128], side_ref.at[n])
+    for n, end in enumerate(ends):
+        corners = turned(end[CP - 16 :, :128], side_ref.at[n])
         at = CORNER - (CP - 16)
         sides.append((corners[:, at : at + 1], corners[:, at + 1 : at + 2]))
     spread(pair, selection(cols), xs_ref, (0, rows + 1), sides)
@@ -366,9 +380,14 @@
 
     edge = shape((rows, 128), bf16)
     line = shape((CP, cols), bf16)
-    first, last, low, high = call(
-        edges_kernel, [edge, edge, line, line], 1, scratch=[VMEM((2, CP, cols), f32)]
+    first, last = call(
+        columns_kernel,
+        [edge, edge],
+        1,
+        space=pltpu.HBM,
+        scratch=[VMEM((2, chan, rows, 128), bf16), pltpu.SemaphoreType.DMA((2,))],
     )(field)
+    low, high = call(lines_kernel, [line, line], 1, scratch=[VMEM((2, CP, cols), f32)])(field)
     hl = lax.ppermute(last, "lon", ahead)
     hr = lax.ppermute(first, "lon", back)
     def framed(line, r):
@@ -379,14 +398,15 @@
     low, high, latents, hl, stem_weight, kv_weight = lax.optimization_barrier(
         (low, high, latents, hl, stem_weight, kv_weight)
     )
-    up = [(i, i + 1) for i in range(nlat - 1)]
-    down = [(t, s) for s, t in up]
-    top = lax.ppermute(high, "lat", up)
-    bot = lax.ppermute(low, "lat", down)
+    odd = (lax.axis_index("lat") & 1) == 1
+    twos = [(i, i ^ 1) for i in range(nlat) if i ^ 1 < nlat]
+    others = [(i, ((i + 1) ^ 1) - 1) for i in range(nlat)]
+    others = [(i, j) for i, j in others if 0 <= j < nlat]
+    near_row = lax.ppermute(jnp.where(odd, low, high), "lat", twos)
+    far_row = lax.ppermute(jnp.where(odd, high, low), "lat", others)
     qz = call(query_kernel, shape((HEADS, 4 * HD, lat), bf16), 3, smem=1)(
         head_gain, latents, latent_gain[None, :], query_weight
     )
-
     wt, wvt = call(
         weights_kernel,
         [shape((width, 16 * CP), bf16), shape((width, width), bf16)],
@@ -408,7 +428,7 @@
         out_spaces=[pl.ANY, VMEM, VMEM, VMEM],
         aliases={0: 3},
         scratch=encode_scratch(rows, cols, width, lat),
-    )(xs, top, bot, wt, stem_bias[None, :], token_gain[None, :], kv_weight, wvt, qz)
+    )(xs, near_row, far_row, wt, stem_bias[None, :], token_gain[None, :], kv_weight, wvt, qz)
 
     def swap(x, flips0, flips1):
         pairs = []

time: 83.9 us -> 83.8 us (level)
  Pallas kernels: 39.7 us -> 40.7 us
    ppermute x2, starting transfers between devices: 5.41 us -> 2.91 us  [the longest x1 2.26 us: shards(): near_row = lax.ppermute(jnp.where(odd, low, high), 'lat', twos)]
    ppermute x14, starting transfers between devices: 13.2 us -> 15.2 us  [swap(): return lax.ppermute(x, ('lat', 'lon'), pairs)]
    pallas_call x6 -> x7, Pallas kernels: 39.7 us -> 40.7 us  [run(): return fn(*args[:smem], *held)]
    unnamed x26 -> x24, local copies, waits for them, and re-layouts: 1.82 us -> 1.94 us
  transfers between devices with their start and end apart: 18 -> 18, of which waited for: 14 -> 12; matrix products, arithmetic and copies ran while one was open for 0% -> 0% of each run, Pallas kernels for 5% -> 6%
where the time goes in v6:
time: 83.8 us; the launch traced here: 83.6 us
  Pallas kernels  40.7 us (49%)
  starting transfers between devices  20.7 us (25%)
  waiting for transfers between devices  17.6 us (21%)
  local copies, waits for them, and re-layouts  2.99 us (4%)
  between operations  1.02 us (1%)
    pallas_call x7, Pallas kernels, run(): return fn(*args[:smem], *held)  40.7 us
    ppermute x14, waiting for transfers between devices, swap(): return lax.ppermute(x, ('lat', 'lon'), pairs)  16.5 us
    ppermute x14, starting transfers between devices, swap(): return lax.ppermute(x, ('lat', 'lon'), pairs)  15.2 us
    ppermute x1, starting transfers between devices, shards(): near_row = lax.ppermute(jnp.where(odd, low, high), 'lat', twos)  2.26 us
    ppermute x1, starting transfers between devices, shards(): hr = lax.ppermute(first, 'lon', back)  2.03 us
    unnamed x24, local copies, waits for them, and re-layouts  1.94 us
  transfers between devices with their start and end apart: 18, of which 12 were waited for; matrix products, arithmetic and copies ran while one was open for 0% of the time, Pallas kernels for 6%

profile of v6, /device:TPU:0, one launch (start us, length us, event | category | flops | bytes accessed | tf_op | source)
XLA Modules:
  0.0 83.6 jit_solution(12197467607724141978)
XLA Ops:
  0.6 0.0 copy-start
  0.6 0.0 copy-start.1
  0.6 1.7 %shard_map.123 = (bf16[32,128]{1,0:T(8,128)(2,1)S(1)}, bf16[32,128]{1,0:T(8,128)(2,1)S(1)}) custom-call(bf16[69,32,512]{2,1,0:T(8,128)(2,1)} %x_ref.5), custom_call_target="tpu_custom_call" | custom-call | tf_op jit(solution)/shard_map/pallas_call | solution.py:42
  2.3 0.5 collective-permute-start
  2.9 2.0 %collective-permute-start.1 = (bf16[32,128]{1,0:T(8,128)(2,1)S(1)}, bf16[32,128]{1,0:T(8,128)(2,1)S(1)}, u32[]{:S(2)}, u32[]{:S(2)}) collective-permute-start(bf16[32,128]{1,0:T(8,128)(2,1)S(1)} %get-tuple-element.19), channel_id=1, source_target_pairs={{1,0},{2,1},{3,2},{0,3},{5,4},{6,5},{7,6},{4,7},{9,8},{10,9},{11,1... | collective-permute-start | bytes 24584 | tf_op jit(solution)/shard_map/ppermute | solution.py:392
  4.9 0.2 shard_map.122
  5.2 0.0 copy-start.4
  5.2 1.0 %collective-permute-done.hl_ref = bf16[32,128]{1,0:T(8,128)(2,1)S(1)} collective-permute-done((bf16[32,128]{1,0:T(8,128)(2,1)S(1)}, bf16[32,128]{1,0:T(8,128)(2,1)S(1)}, u32[]{:S(2)}, u32[]{:S(2)}) %collective-permute-start) | collective-permute-done | bytes 8224 | tf_op jit(solution)/shard_map/ppermute | solution.py:391
  6.2 0.1 collective-permute-done.1.hr_ref
  6.3 2.3 %collective-permute-start.2 = (bf16[80,512]{1,0:T(8,128)(2,1)S(1)}, bf16[80,512]{1,0:T(8,128)(2,1)S(1)}, u32[]{:S(2)}, u32[]{:S(2)}) collective-permute-start(bf16[80,512]{1,0:T(8,128)(2,1)S(1)} %get-tuple-element.64), channel_id=1, source_target_pairs={{0,4},{4,0},{8,12},{12,8},{16,20},{20,16},{24,28},{28,24},{1,5},{5... | collective-permute-start | bytes 245768 | tf_op jit(solution)/shard_map/ppermute | solution.py:405
  8.6 0.7 collective-permute-start.3
  9.3 0.0 copy-start.2
  9.3 1.2 %copy-done.2 = bf16[1104,512]{1,0:T(8,128)(2,1)S(1)} copy-done((bf16[1104,512]{1,0:T(8,128)(2,1)S(1)}, bf16[1104,512]{1,0:T(8,128)(2,1)}, u32[]{:S(2)}) %copy-start.2) | copy-done | bytes 1130520
  10.5 0.5 shard_map.125
  11.1 0.6 copy-done.3
  11.7 1.5 %shard_map.126.qz_ref = bf16[8,256,512]{2,1,0:T(8,128)(2,1)S(1)} custom-call(f32[8]{0:T(128)S(1)} %copy-done.10, f32[512,512]{1,0:T(8,128)S(1)} %copy-done.3, f32[1,512]{1,0:T(1,128)S(1)} %bitcast.23, bf16[512,512]{1,0:T(8,128)(2,1)S(1)} %copy-done.4), custom_call_target="tpu_custom_call" | custom-call | tf_op jit(solution)/shard_map/pallas_call | solution.py:42
  13.2 0.0 copy-start.7
  13.2 0.0 copy-start.8
  13.2 2.5 %shard_map.124.xs_in = bf16[34,320,256]{2,1,0:T(8,128)(2,1)S(1)} custom-call(bf16[69,32,512]{2,1,0:T(8,128)(2,1)S(1)} %copy-done, bf16[32,128]{1,0:T(8,128)(2,1)S(1)} %collective-permute-done.hl_ref, bf16[32,128]{1,0:T(8,128)(2,1)S(1)} %collective-permute-done.1.hr_ref), custom_call_target="tpu_custom_call" | custom-call | tf_op jit(solution)/shard_map/pallas_call | solution.py:42
  15.8 0.0 collective-permute-done.2.near_ref
  15.8 0.0 collective-permute-done.3.far_ref
  15.8 32.7 %shard_map.127 = (bf16[16,256,512]{2,1,0:T(8,128)(2,1)}, bf16[4,80,512]{2,1,0:T(8,128)(2,1)S(1)}, bf16[4,80,512]{2,1,0:T(8,128)(2,1)S(1)}, bf16[34,320,256]{2,1,0:T(8,128)(2,1)S(1)}) custom-call(bf16[34,320,256]{2,1,0:T(8,128)(2,1)S(1)} %shard_map.124.xs_in, bf16[80,512]{1,0:T(8,128)(2,1)S(1)} %collective-permute-done.2.near_ref, ...), custom_call_target="tpu_custom_call", output_to_operand_aliasing={{3}: (0, {})} | custom-call | tf_op jit(solution)/shard_map/pallas_call | solution.py:42
  48.5 0.0 copy-start.5
  48.5 0.0 copy-start.9
  48.5 1.4 %collective-permute-start.4 = (bf16[4,80,512]{2,1,0:T(8,128)(2,1)S(1)}, bf16[4,80,512]{2,1,0:T(8,128)(2,1)S(1)}, u32[]{:S(2)}, u32[]{:S(2)}) collective-permute-start(bf16[4,80,512]{2,1,0:T(8,128)(2,1)S(1)} %get-tuple-element.31), channel_id=1, source_target_pairs={{0,1},{1,0},{2,3},{3,2},{4,5},{5,4},{6,7},{7,6},{8,9},{9,8},{10,11... | collective-permute-start | bytes 983048 | tf_op jit(solution)/shard_map/ppermute | solution.py:441
  49.9 1.2 %collective-permute-done.4 = bf16[4,80,512]{2,1,0:T(8,128)(2,1)S(1)} collective-permute-done((bf16[4,80,512]{2,1,0:T(8,128)(2,1)S(1)}, bf16[4,80,512]{2,1,0:T(8,128)(2,1)S(1)}, u32[]{:S(2)}, u32[]{:S(2)}) %collective-permute-start.4) | collective-permute-done | bytes 327712 | tf_op jit(solution)/shard_map/ppermute | solution.py:441
  51.1 0.1 fusion.15
  51.2 0.1 reduce-precision_convert_fusion
  51.3 0.3 concatenate.30
  51.6 0.1 add_convert_fusion
  51.7 0.4 concatenate.31
  52.1 4.4 %collective-permute-start.7 = (bf16[1,80,512]{2,1,0:T(8,128)(2,1)S(1)}, bf16[1,80,512]{2,1,0:T(8,128)(2,1)S(1)}, u32[]{:S(2)}, u32[]{:S(2)}) collective-permute-start(bf16[1,80,512]{2,1,0:T(8,128)(2,1)S(1)} %get-tuple-element.61), channel_id=1, source_target_pairs={{0,6},{1,7},{2,4},{3,5},{4,2},{5,3},{6,0},{7,1},{8,14},{9,15},{10,... | collective-permute-start | bytes 245768 | tf_op jit(solution)/shard_map/ppermute | solution.py:441
  56.5 1.2 %collective-permute-start.6 = (bf16[1,80,512]{2,1,0:T(8,128)(2,1)S(1)}, bf16[1,80,512]{2,1,0:T(8,128)(2,1)S(1)}, u32[]{:S(2)}, u32[]{:S(2)}) collective-permute-start(bf16[1,80,512]{2,1,0:T(8,128)(2,1)S(1)} %get-tuple-element.62), channel_id=1, source_target_pairs={{0,2},{1,5},{2,0},{3,7},{4,6},{5,1},{6,4},{7,3},{8,10},{9,13},{10,... | collective-permute-start | bytes 245768 | tf_op jit(solution)/shard_map/ppermute | solution.py:441
  57.7 0.0 collective-permute-start.5
  57.7 1.7 %collective-permute-done.7 = bf16[1,80,512]{2,1,0:T(8,128)(2,1)S(1)} collective-permute-done((bf16[1,80,512]{2,1,0:T(8,128)(2,1)S(1)}, bf16[1,80,512]{2,1,0:T(8,128)(2,1)S(1)}, u32[]{:S(2)}, u32[]{:S(2)}) %collective-permute-start.7) | collective-permute-done | bytes 81952 | tf_op jit(solution)/shard_map/ppermute | solution.py:441
  59.3 1.7 %collective-permute-done.6 = bf16[1,80,512]{2,1,0:T(8,128)(2,1)S(1)} collective-permute-done((bf16[1,80,512]{2,1,0:T(8,128)(2,1)S(1)}, bf16[1,80,512]{2,1,0:T(8,128)(2,1)S(1)}, u32[]{:S(2)}, u32[]{:S(2)}) %collective-permute-start.6) | collective-permute-done | bytes 81952 | tf_op jit(solution)/shard_map/ppermute | solution.py:441
  61.0 1.1 %collective-permute-done.5 = bf16[1,80,512]{2,1,0:T(8,128)(2,1)S(1)} collective-permute-done((bf16[1,80,512]{2,1,0:T(8,128)(2,1)S(1)}, bf16[1,80,512]{2,1,0:T(8,128)(2,1)S(1)}, u32[]{:S(2)}, u32[]{:S(2)}) %collective-permute-start.5) | collective-permute-done | bytes 81952 | tf_op jit(solution)/shard_map/ppermute | solution.py:441
  62.1 0.1 reduce-precision_convert_fusion.4
  62.2 0.1 add_convert_fusion.1
  62.3 0.2 concatenate.33
  62.5 2.0 %collective-permute-start.10 = (bf16[1,80,512]{2,1,0:T(8,128)(2,1)S(1)}, bf16[1,80,512]{2,1,0:T(8,128)(2,1)S(1)}, u32[]{:S(2)}, u32[]{:S(2)}) collective-permute-start(bf16[1,80,512]{2,1,0:T(8,128)(2,1)S(1)} %concatenate.33), channel_id=1, source_target_pairs={{0,24},{1,25},{2,26},{3,27},{4,28},{5,29},{6,30},{7,31},{8,16},{9,... | collective-permute-start | bytes 245768 | tf_op jit(solution)/shard_map/ppermute | solution.py:441
  64.5 0.2 concatenate.32
  64.7 1.1 %collective-permute-start.9 = (bf16[1,80,512]{2,1,0:T(8,128)(2,1)S(1)}, bf16[1,80,512]{2,1,0:T(8,128)(2,1)S(1)}, u32[]{:S(2)}, u32[]{:S(2)}) collective-permute-start(bf16[1,80,512]{2,1,0:T(8,128)(2,1)S(1)} %concatenate.33), channel_id=1, source_target_pairs={{0,16},{1,17},{2,18},{3,19},{4,20},{5,21},{6,22},{7,23},{8,24},{9,... | collective-permute-start | bytes 245768 | tf_op jit(solution)/shard_map/ppermute | solution.py:441
  65.8 1.3 %collective-permute-start.8 = (bf16[1,80,512]{2,1,0:T(8,128)(2,1)S(1)}, bf16[1,80,512]{2,1,0:T(8,128)(2,1)S(1)}, u32[]{:S(2)}, u32[]{:S(2)}) collective-permute-start(bf16[1,80,512]{2,1,0:T(8,128)(2,1)S(1)} %concatenate.33), channel_id=1, source_target_pairs={{0,8},{1,9},{2,10},{3,11},{4,12},{5,13},{6,14},{7,15},{8,0},{9,1},... | collective-permute-start | bytes 245768 | tf_op jit(solution)/shard_map/ppermute | solution.py:441
  67.2 1.7 %collective-permute-done.10 = bf16[1,80,512]{2,1,0:T(8,128)(2,1)S(1)} collective-permute-done((bf16[1,80,512]{2,1,0:T(8,128)(2,1)S(1)}, bf16[1,80,512]{2,1,0:T(8,128)(2,1)S(1)}, u32[]{:S(2)}, u32[]{:S(2)}) %collective-permute-start.10) | collective-permute-done | bytes 81952 | tf_op jit(solution)/shard_map/ppermute | solution.py:441
  68.9 3.1 %collective-permute-done.9 = bf16[1,80,512]{2,1,0:T(8,128)(2,1)S(1)} collective-permute-done((bf16[1,80,512]{2,1,0:T(8,128)(2,1)S(1)}, bf16[1,80,512]{2,1,0:T(8,128)(2,1)S(1)}, u32[]{:S(2)}, u32[]{:S(2)}) %collective-permute-start.9) | collective-permute-done | bytes 81952 | tf_op jit(solution)/shard_map/ppermute | solution.py:441
  72.0 0.0 collective-permute-done.8
  72.1 0.1 multiply_add_fusion
  72.1 0.1 divide_convert_fusion.refs_0_
  72.2 2.3 %collective-permute-start.11 = (bf16[1,64,512]{2,1,0:T(8,128)(2,1)S(1)}, bf16[1,64,512]{2,1,0:T(8,128)(2,1)S(1)}, u32[]{:S(2)}, u32[]{:S(2)}) collective-permute-start(bf16[1,64,512]{2,1,0:T(8,128)(2,1)S(1)} %divide_convert_fusion.refs_0_), channel_id=1, source_target_pairs={{0,4},{1,3},{2,6},{3,1},{4,0},{5,7},{6,2},{7,5},{8,12},{9,11},{10,... | collective-permute-start | bytes 196616 | tf_op jit(solution)/shard_map/ppermute | solution.py:441
  74.5 1.1 %collective-permute-start.12 = (bf16[1,64,512]{2,1,0:T(8,128)(2,1)S(1)}, bf16[1,64,512]{2,1,0:T(8,128)(2,1)S(1)}, u32[]{:S(2)}, u32[]{:S(2)}) collective-permute-start(bf16[1,64,512]{2,1,0:T(8,128)(2,1)S(1)} %divide_convert_fusion.refs_0_), channel_id=1, source_target_pairs={{0,2},{1,5},{2,0},{3,7},{4,6},{5,1},{6,4},{7,3},{8,10},{9,13},{10,... | collective-permute-start | bytes 196616 | tf_op jit(solution)/shard_map/ppermute | solution.py:441
  75.6 0.4 collective-permute-start.13
  76.0 0.0 collective-permute-start.14
  76.0 0.9 %collective-permute-done.11.refs_1_ = bf16[1,64,512]{2,1,0:T(8,128)(2,1)S(1)} collective-permute-done((bf16[1,64,512]{2,1,0:T(8,128)(2,1)S(1)}, bf16[1,64,512]{2,1,0:T(8,128)(2,1)S(1)}, u32[]{:S(2)}, u32[]{:S(2)}) %collective-permute-start.11) | collective-permute-done | bytes 65568 | tf_op jit(solution)/shard_map/ppermute | solution.py:441
  77.0 0.0 collective-permute-start.15
  77.0 2.2 %collective-permute-done.12.refs_2_ = bf16[1,64,512]{2,1,0:T(8,128)(2,1)S(1)} collective-permute-done((bf16[1,64,512]{2,1,0:T(8,128)(2,1)S(1)}, bf16[1,64,512]{2,1,0:T(8,128)(2,1)S(1)}, u32[]{:S(2)}, u32[]{:S(2)}) %collective-permute-start.12) | collective-permute-done | bytes 65568 | tf_op jit(solution)/shard_map/ppermute | solution.py:441
  79.2 0.0 collective-permute-start.16
  79.2 1.6 %collective-permute-done.13.refs_3_ = bf16[1,64,512]{2,1,0:T(8,128)(2,1)S(1)} collective-permute-done((bf16[1,64,512]{2,1,0:T(8,128)(2,1)S(1)}, bf16[1,64,512]{2,1,0:T(8,128)(2,1)S(1)}, u32[]{:S(2)}, u32[]{:S(2)}) %collective-permute-start.13) | collective-permute-done | bytes 65568 | tf_op jit(solution)/shard_map/ppermute | solution.py:441
  80.8 0.0 collective-permute-start.17
  80.8 0.0 collective-permute-done.14.refs_4_
  80.8 0.0 collective-permute-done.15.refs_5_
  80.8 0.0 collective-permute-done.16.refs_6_
  80.8 1.2 %collective-permute-done.17.refs_7_ = bf16[1,64,512]{2,1,0:T(8,128)(2,1)S(1)} collective-permute-done((bf16[1,64,512]{2,1,0:T(8,128)(2,1)S(1)}, bf16[1,64,512]{2,1,0:T(8,128)(2,1)S(1)}, u32[]{:S(2)}, u32[]{:S(2)}) %collective-permute-start.17) | collective-permute-done | bytes 65568 | tf_op jit(solution)/shard_map/ppermute | solution.py:441
  82.0 1.6 %shard_map.128 = f32[512,512]{1,0:T(8,128)} custom-call(bf16[1,64,512]{2,1,0:T(8,128)(2,1)S(1)} %divide_convert_fusion.refs_0_, bf16[1,64,512]{2,1,0:T(8,128)(2,1)S(1)} %collective-permute-done.11.refs_1_, bf16[1,64,512]{2,1,0:T(8,128)(2,1)S(1)} %collective-permute-done.12.refs_2_, bf16[1,64,512]{2,1,0:T(8,128)(2,1)S(1)} %collective-permute-done.13.refs_3_, ...), custom_call_target="tpu_custom_call" | custom-call | tf_op jit(solution)/shard_map/pallas_call | solution.py:42
  (38 shorter events, 0.2 us)
Async XLA Ops:
  0.6 4.3 %copy-start = (bf16[69,32,512]{2,1,0:T(8,128)(2,1)S(1)}, bf16[69,32,512]{2,1,0:T(8,128)(2,1)}, u32[]{:S(2)}) copy-start(bf16[69,32,512]{2,1,0:T(8,128)(2,1)} %x_ref.5) | copy-start | bytes 6782980
  0.6 8.6 %copy-start.1 = (bf16[512,1024]{1,0:T(8,128)(2,1)S(1)}, bf16[512,1024]{1,0:T(8,128)(2,1)}, u32[]{:S(2)}) copy-start(bf16[512,1024]{1,0:T(8,128)(2,1)} %kv_ref.1) | copy-start | bytes 3145732
  2.3 3.8 %collective-permute-start = (bf16[32,128]{1,0:T(8,128)(2,1)S(1)}, bf16[32,128]{1,0:T(8,128)(2,1)S(1)}, u32[]{:S(2)}, u32[]{:S(2)}) collective-permute-start(bf16[32,128]{1,0:T(8,128)(2,1)S(1)} %get-tuple-element.18), channel_id=1, source_target_pairs={{0,1},{1,2},{2,3},{3,0},{4,5},{5,6},{6,7},{7,4},{8,9},{9,10},{10,1... | collective-permute-start | bytes 24584 | tf_op jit(solution)/shard_map/ppermute | solution.py:391
  2.9 8.2 %copy-start.6 = (f32[512]{0:T(512)S(1)}, f32[512]{0:T(512)}, u32[]{:S(2)}) copy-start(f32[512]{0:T(512)} %param.17) | copy-start | bytes 6148
  2.9 8.2 %copy-start.10 = (f32[8]{0:T(128)S(1)}, f32[8]{0:T(128)}, u32[]{:S(2)}) copy-start(f32[8]{0:T(128)} %gain_ref.1) | copy-start | bytes 100
  2.9 3.4 %collective-permute-start.1 = (bf16[32,128]{1,0:T(8,128)(2,1)S(1)}, bf16[32,128]{1,0:T(8,128)(2,1)S(1)}, u32[]{:S(2)}, u32[]{:S(2)}) collective-permute-start(bf16[32,128]{1,0:T(8,128)(2,1)S(1)} %get-tuple-element.19), channel_id=1, source_target_pairs={{1,0},{2,1},{3,2},{0,3},{5,4},{6,5},{7,6},{4,7},{9,8},{10,9},{11,1... | collective-permute-start | bytes 24584 | tf_op jit(solution)/shard_map/ppermute | solution.py:392
  5.2 5.9 %copy-start.4 = (bf16[512,512]{1,0:T(8,128)(2,1)S(1)}, bf16[512,512]{1,0:T(8,128)(2,1)}, u32[]{:S(2)}) copy-start(bf16[512,512]{1,0:T(8,128)(2,1)} %qw_ref.1) | copy-start | bytes 1572868
  6.3 9.4 %collective-permute-start.2 = (bf16[80,512]{1,0:T(8,128)(2,1)S(1)}, bf16[80,512]{1,0:T(8,128)(2,1)S(1)}, u32[]{:S(2)}, u32[]{:S(2)}) collective-permute-start(bf16[80,512]{1,0:T(8,128)(2,1)S(1)} %get-tuple-element.64), channel_id=1, source_target_pairs={{0,4},{4,0},{8,12},{12,8},{16,20},{20,16},{24,28},{28,24},{1,5},{5... | collective-permute-start | bytes 245768 | tf_op jit(solution)/shard_map/ppermute | solution.py:405
  8.6 7.2 %collective-permute-start.3 = (bf16[80,512]{1,0:T(8,128)(2,1)S(1)}, bf16[80,512]{1,0:T(8,128)(2,1)S(1)}, u32[]{:S(2)}, u32[]{:S(2)}) collective-permute-start(bf16[80,512]{1,0:T(8,128)(2,1)S(1)} %get-tuple-element.63), channel_id=1, source_target_pairs={{4,8},{8,4},{12,16},{16,12},{20,24},{24,20},{5,9},{9,5},{13,17},{1... | collective-permute-start | bytes 245768 | tf_op jit(solution)/shard_map/ppermute | solution.py:406
  9.3 1.3 %copy-start.2 = (bf16[1104,512]{1,0:T(8,128)(2,1)S(1)}, bf16[1104,512]{1,0:T(8,128)(2,1)}, u32[]{:S(2)}) copy-start(bf16[1104,512]{1,0:T(8,128)(2,1)} %w_ref) | copy-start | bytes 3391492
  10.5 1.2 %copy-start.3 = (f32[512,512]{1,0:T(8,128)S(1)}, f32[512,512]{1,0:T(8,128)}, u32[]{:S(2)}) copy-start(f32[512,512]{1,0:T(8,128)} %latents_ref) | copy-start | bytes 3145732
  13.2 2.6 %copy-start.7 = (f32[512]{0:T(512)S(1)}, f32[512]{0:T(512)}, u32[]{:S(2)}) copy-start(f32[512]{0:T(512)} %param.13) | copy-start | bytes 6148
  13.2 2.6 %copy-start.8 = (f32[512]{0:T(512)S(1)}, f32[512]{0:T(512)}, u32[]{:S(2)}) copy-start(f32[512]{0:T(512)} %param.14) | copy-start | bytes 6148
  48.5 33.6 %copy-start.5 = (bf16[512,512]{1,0:T(8,128)(2,1)S(1)}, bf16[512,512]{1,0:T(8,128)(2,1)}, u32[]{:S(2)}) copy-start(bf16[512,512]{1,0:T(8,128)(2,1)} %refs_8_.1) | copy-start | bytes 1572868
  48.5 33.5 %copy-start.9 = (f32[512]{0:T(512)S(1)}, f32[512]{0:T(512)}, u32[]{:S(2)}) copy-start(f32[512]{0:T(512)} %param.21) | copy-start | bytes 6148
  48.5 2.6 %collective-permute-start.4 = (bf16[4,80,512]{2,1,0:T(8,128)(2,1)S(1)}, bf16[4,80,512]{2,1,0:T(8,128)(2,1)S(1)}, u32[]{:S(2)}, u32[]{:S(2)}) collective-permute-start(bf16[4,80,512]{2,1,0:T(8,128)(2,1)S(1)} %get-tuple-element.31), channel_id=1, source_target_pairs={{0,1},{1,0},{2,3},{3,2},{4,5},{5,4},{6,7},{7,6},{8,9},{9,8},{10,11... | collective-permute-start | bytes 983048 | tf_op jit(solution)/shard_map/ppermute | solution.py:441
  52.1 7.2 %collective-permute-start.7 = (bf16[1,80,512]{2,1,0:T(8,128)(2,1)S(1)}, bf16[1,80,512]{2,1,0:T(8,128)(2,1)S(1)}, u32[]{:S(2)}, u32[]{:S(2)}) collective-permute-start(bf16[1,80,512]{2,1,0:T(8,128)(2,1)S(1)} %get-tuple-element.61), channel_id=1, source_target_pairs={{0,6},{1,7},{2,4},{3,5},{4,2},{5,3},{6,0},{7,1},{8,14},{9,15},{10,... | collective-permute-start | bytes 245768 | tf_op jit(solution)/shard_map/ppermute | solution.py:441
  56.5 4.5 %collective-permute-start.6 = (bf16[1,80,512]{2,1,0:T(8,128)(2,1)S(1)}, bf16[1,80,512]{2,1,0:T(8,128)(2,1)S(1)}, u32[]{:S(2)}, u32[]{:S(2)}) collective-permute-start(bf16[1,80,512]{2,1,0:T(8,128)(2,1)S(1)} %get-tuple-element.62), channel_id=1, source_target_pairs={{0,2},{1,5},{2,0},{3,7},{4,6},{5,1},{6,4},{7,3},{8,10},{9,13},{10,... | collective-permute-start | bytes 245768 | tf_op jit(solution)/shard_map/ppermute | solution.py:441
  57.7 4.4 %collective-permute-start.5 = (bf16[1,80,512]{2,1,0:T(8,128)(2,1)S(1)}, bf16[1,80,512]{2,1,0:T(8,128)(2,1)S(1)}, u32[]{:S(2)}, u32[]{:S(2)}) collective-permute-start(bf16[1,80,512]{2,1,0:T(8,128)(2,1)S(1)} %get-tuple-element.60), channel_id=1, source_target_pairs={{0,4},{1,3},{2,6},{3,1},{4,0},{5,7},{6,2},{7,5},{8,12},{9,11},{10,... | collective-permute-start | bytes 245768 | tf_op jit(solution)/shard_map/ppermute | solution.py:441
  62.5 6.4 %collective-permute-start.10 = (bf16[1,80,512]{2,1,0:T(8,128)(2,1)S(1)}, bf16[1,80,512]{2,1,0:T(8,128)(2,1)S(1)}, u32[]{:S(2)}, u32[]{:S(2)}) collective-permute-start(bf16[1,80,512]{2,1,0:T(8,128)(2,1)S(1)} %concatenate.33), channel_id=1, source_target_pairs={{0,24},{1,25},{2,26},{3,27},{4,28},{5,29},{6,30},{7,31},{8,16},{9,... | collective-permute-start | bytes 245768 | tf_op jit(solution)/shard_map/ppermute | solution.py:441
  64.7 7.4 %collective-permute-start.9 = (bf16[1,80,512]{2,1,0:T(8,128)(2,1)S(1)}, bf16[1,80,512]{2,1,0:T(8,128)(2,1)S(1)}, u32[]{:S(2)}, u32[]{:S(2)}) collective-permute-start(bf16[1,80,512]{2,1,0:T(8,128)(2,1)S(1)} %concatenate.33), channel_id=1, source_target_pairs={{0,16},{1,17},{2,18},{3,19},{4,20},{5,21},{6,22},{7,23},{8,24},{9,... | collective-permute-start | bytes 245768 | tf_op jit(solution)/shard_map/ppermute | solution.py:441
  65.8 6.2 %collective-permute-start.8 = (bf16[1,80,512]{2,1,0:T(8,128)(2,1)S(1)}, bf16[1,80,512]{2,1,0:T(8,128)(2,1)S(1)}, u32[]{:S(2)}, u32[]{:S(2)}) collective-permute-start(bf16[1,80,512]{2,1,0:T(8,128)(2,1)S(1)} %concatenate.33), channel_id=1, source_target_pairs={{0,8},{1,9},{2,10},{3,11},{4,12},{5,13},{6,14},{7,15},{8,0},{9,1},... | collective-permute-start | bytes 245768 | tf_op jit(solution)/shard_map/ppermute | solution.py:441
  72.2 4.8 %collective-permute-start.11 = (bf16[1,64,512]{2,1,0:T(8,128)(2,1)S(1)}, bf16[1,64,512]{2,1,0:T(8,128)(2,1)S(1)}, u32[]{:S(2)}, u32[]{:S(2)}) collective-permute-start(bf16[1,64,512]{2,1,0:T(8,128)(2,1)S(1)} %divide_convert_fusion.refs_0_), channel_id=1, source_target_pairs={{0,4},{1,3},{2,6},{3,1},{4,0},{5,7},{6,2},{7,5},{8,12},{9,11},{10,... | collective-permute-start | bytes 196616 | tf_op jit(solution)/shard_map/ppermute | solution.py:441
  74.5 4.7 %collective-permute-start.12 = (bf16[1,64,512]{2,1,0:T(8,128)(2,1)S(1)}, bf16[1,64,512]{2,1,0:T(8,128)(2,1)S(1)}, u32[]{:S(2)}, u32[]{:S(2)}) collective-permute-start(bf16[1,64,512]{2,1,0:T(8,128)(2,1)S(1)} %divide_convert_fusion.refs_0_), channel_id=1, source_target_pairs={{0,2},{1,5},{2,0},{3,7},{4,6},{5,1},{6,4},{7,3},{8,10},{9,13},{10,... | collective-permute-start | bytes 196616 | tf_op jit(solution)/shard_map/ppermute | solution.py:441
  75.6 5.2 %collective-permute-start.13 = (bf16[1,64,512]{2,1,0:T(8,128)(2,1)S(1)}, bf16[1,64,512]{2,1,0:T(8,128)(2,1)S(1)}, u32[]{:S(2)}, u32[]{:S(2)}) collective-permute-start(bf16[1,64,512]{2,1,0:T(8,128)(2,1)S(1)} %divide_convert_fusion.refs_0_), channel_id=1, source_target_pairs={{0,6},{1,7},{2,4},{3,5},{4,2},{5,3},{6,0},{7,1},{8,14},{9,15},{10,... | collective-permute-start | bytes 196616 | tf_op jit(solution)/shard_map/ppermute | solution.py:441
  76.0 4.7 %collective-permute-start.14 = (bf16[1,64,512]{2,1,0:T(8,128)(2,1)S(1)}, bf16[1,64,512]{2,1,0:T(8,128)(2,1)S(1)}, u32[]{:S(2)}, u32[]{:S(2)}) collective-permute-start(bf16[1,64,512]{2,1,0:T(8,128)(2,1)S(1)} %divide_convert_fusion.refs_0_), channel_id=1, source_target_pairs={{0,1},{1,0},{2,3},{3,2},{4,5},{5,4},{6,7},{7,6},{8,9},{9,8},{10,11... | collective-permute-start | bytes 196616 | tf_op jit(solution)/shard_map/ppermute | solution.py:441
  77.0 3.8 %collective-permute-start.15 = (bf16[1,64,512]{2,1,0:T(8,128)(2,1)S(1)}, bf16[1,64,512]{2,1,0:T(8,128)(2,1)S(1)}, u32[]{:S(2)}, u32[]{:S(2)}) collective-permute-start(bf16[1,64,512]{2,1,0:T(8,128)(2,1)S(1)} %collective-permute-done.11.refs_1_), channel_id=1, source_target_pairs={{0,1},{1,0},{2,3},{3,2},{4,5},{5,4},{6,7},{7,6},{8,9},{9,8},{10,11... | collective-permute-start | bytes 196616 | tf_op jit(solution)/shard_map/ppermute | solution.py:441
  79.2 1.6 %collective-permute-start.16 = (bf16[1,64,512]{2,1,0:T(8,128)(2,1)S(1)}, bf16[1,64,512]{2,1,0:T(8,128)(2,1)S(1)}, u32[]{:S(2)}, u32[]{:S(2)}) collective-permute-start(bf16[1,64,512]{2,1,0:T(8,128)(2,1)S(1)} %collective-permute-done.12.refs_2_), channel_id=1, source_target_pairs={{0,1},{1,0},{2,3},{3,2},{4,5},{5,4},{6,7},{7,6},{8,9},{9,8},{10,11... | collective-permute-start | bytes 196616 | tf_op jit(solution)/shard_map/ppermute | solution.py:441
  80.8 1.3 %collective-permute-start.17 = (bf16[1,64,512]{2,1,0:T(8,128)(2,1)S(1)}, bf16[1,64,512]{2,1,0:T(8,128)(2,1)S(1)}, u32[]{:S(2)}, u32[]{:S(2)}) collective-permute-start(bf16[1,64,512]{2,1,0:T(8,128)(2,1)S(1)} %collective-permute-done.13.refs_3_), channel_id=1, source_target_pairs={{0,1},{1,0},{2,3},{3,2},{4,5},{5,4},{6,7},{7,6},{8,9},{9,8},{10,11... | collective-permute-start | bytes 196616 | tf_op jit(solution)/shard_map/ppermute | solution.py:441

commit v7 on v6

--- a/solution.py
+++ b/solution.py
@@ -226,7 +226,7 @@
         finish(r + 1, 1)
         return carry
 
-    lax.fori_loop(0, trows // 2, band, 0)
+    lax.fori_loop(0, trows // 2, band, 0, unroll=2)
 
     def produce(h, c, slot):
         pair = pl.ds(pl.multiple_of((h >> 1) * (2 * HD), 2 * HD), 2 * HD)

time: 83.8 us -> 83.7 us (level)
  no operation moved by 1% of the time
where the time goes in v7:
time: 83.7 us; the launch traced here: 83.5 us
  Pallas kernels  40.3 us (48%)
  starting transfers between devices  20.8 us (25%)
  waiting for transfers between devices  17.6 us (21%)
  local copies, waits for them, and re-layouts  2.99 us (4%)
  between operations  1.18 us (1%)
    pallas_call x7, Pallas kernels, run(): return fn(*args[:smem], *held)  40.3 us
    ppermute x14, waiting for transfers between devices, swap(): return lax.ppermute(x, ('lat', 'lon'), pairs)  16.5 us
    ppermute x14, starting transfers between devices, swap(): return lax.ppermute(x, ('lat', 'lon'), pairs)  15.3 us
    ppermute x1, starting transfers between devices, shards(): near_row = lax.ppermute(jnp.where(odd, low, high), 'lat', twos)  2.26 us
    ppermute x1, starting transfers between devices, shards(): hr = lax.ppermute(first, 'lon', back)  2.03 us
    unnamed x24, local copies, waits for them, and re-layouts  1.94 us
  transfers between devices with their start and end apart: 18, of which 12 were waited for; matrix products, arithmetic and copies ran while one was open for 0% of the time, Pallas kernels for 6%

profile of v7, /device:TPU:0, one launch (start us, length us, event | category | flops | bytes accessed | tf_op | source)
XLA Modules:
  0.0 83.5 jit_solution(5238352620575790475)
XLA Ops:
  0.6 1.7 %shard_map.123 = (bf16[32,128]{1,0:T(8,128)(2,1)S(1)}, bf16[32,128]{1,0:T(8,128)(2,1)S(1)}) custom-call(bf16[69,32,512]{2,1,0:T(8,128)(2,1)} %x_ref.5), custom_call_target="tpu_custom_call" | custom-call | tf_op jit(solution)/shard_map/pallas_call | solution.py:42
  2.3 0.5 collective-permute-start
  2.9 2.0 %collective-permute-start.1 = (bf16[32,128]{1,0:T(8,128)(2,1)S(1)}, bf16[32,128]{1,0:T(8,128)(2,1)S(1)}, u32[]{:S(2)}, u32[]{:S(2)}) collective-permute-start(bf16[32,128]{1,0:T(8,128)(2,1)S(1)} %get-tuple-element.19), channel_id=1, source_target_pairs={{1,0},{2,1},{3,2},{0,3},{5,4},{6,5},{7,6},{4,7},{9,8},{10,9},{11,1... | collective-permute-start | bytes 24584 | tf_op jit(solution)/shard_map/ppermute | solution.py:392
  4.9 0.2 shard_map.122
  5.2 0.0 copy-start.4
  5.2 1.0 %collective-permute-done.hl_ref = bf16[32,128]{1,0:T(8,128)(2,1)S(1)} collective-permute-done((bf16[32,128]{1,0:T(8,128)(2,1)S(1)}, bf16[32,128]{1,0:T(8,128)(2,1)S(1)}, u32[]{:S(2)}, u32[]{:S(2)}) %collective-permute-start) | collective-permute-done | bytes 8224 | tf_op jit(solution)/shard_map/ppermute | solution.py:391
  6.2 0.1 collective-permute-done.1.hr_ref
  6.3 2.3 %collective-permute-start.2 = (bf16[80,512]{1,0:T(8,128)(2,1)S(1)}, bf16[80,512]{1,0:T(8,128)(2,1)S(1)}, u32[]{:S(2)}, u32[]{:S(2)}) collective-permute-start(bf16[80,512]{1,0:T(8,128)(2,1)S(1)} %get-tuple-element.64), channel_id=1, source_target_pairs={{0,4},{4,0},{8,12},{12,8},{16,20},{20,16},{24,28},{28,24},{1,5},{5... | collective-permute-start | bytes 245768 | tf_op jit(solution)/shard_map/ppermute | solution.py:405
  8.6 0.7 collective-permute-start.3
  9.2 0.0 copy-done.1
  9.3 0.0 copy-start.2
  9.3 1.2 %copy-done.2 = bf16[1104,512]{1,0:T(8,128)(2,1)S(1)} copy-done((bf16[1104,512]{1,0:T(8,128)(2,1)S(1)}, bf16[1104,512]{1,0:T(8,128)(2,1)}, u32[]{:S(2)}) %copy-start.2) | copy-done | bytes 1130520
  10.5 0.5 shard_map.125
  11.1 0.6 copy-done.3
  11.7 1.5 %shard_map.126.qz_ref = bf16[8,256,512]{2,1,0:T(8,128)(2,1)S(1)} custom-call(f32[8]{0:T(128)S(1)} %copy-done.10, f32[512,512]{1,0:T(8,128)S(1)} %copy-done.3, f32[1,512]{1,0:T(1,128)S(1)} %bitcast.23, bf16[512,512]{1,0:T(8,128)(2,1)S(1)} %copy-done.4), custom_call_target="tpu_custom_call" | custom-call | tf_op jit(solution)/shard_map/pallas_call | solution.py:42
  13.2 0.0 copy-start.7
  13.2 0.0 copy-start.8
  13.2 2.5 %shard_map.124.xs_in = bf16[34,320,256]{2,1,0:T(8,128)(2,1)S(1)} custom-call(bf16[69,32,512]{2,1,0:T(8,128)(2,1)S(1)} %copy-done, bf16[32,128]{1,0:T(8,128)(2,1)S(1)} %collective-permute-done.hl_ref, bf16[32,128]{1,0:T(8,128)(2,1)S(1)} %collective-permute-done.1.hr_ref), custom_call_target="tpu_custom_call" | custom-call | tf_op jit(solution)/shard_map/pallas_call | solution.py:42
  15.8 0.0 collective-permute-done.2.near_ref
  15.8 0.0 collective-permute-done.3.far_ref
  15.8 32.3 %shard_map.127 = (bf16[16,256,512]{2,1,0:T(8,128)(2,1)}, bf16[4,80,512]{2,1,0:T(8,128)(2,1)S(1)}, bf16[4,80,512]{2,1,0:T(8,128)(2,1)S(1)}, bf16[34,320,256]{2,1,0:T(8,128)(2,1)S(1)}) custom-call(bf16[34,320,256]{2,1,0:T(8,128)(2,1)S(1)} %shard_map.124.xs_in, bf16[80,512]{1,0:T(8,128)(2,1)S(1)} %collective-permute-done.2.near_ref, ...), custom_call_target="tpu_custom_call", output_to_operand_aliasing={{3}: (0, {})} | custom-call | tf_op jit(solution)/shard_map/pallas_call | solution.py:42
  48.1 0.0 copy-start.5
  48.1 0.0 copy-start.9
  48.1 1.4 %collective-permute-start.4 = (bf16[4,80,512]{2,1,0:T(8,128)(2,1)S(1)}, bf16[4,80,512]{2,1,0:T(8,128)(2,1)S(1)}, u32[]{:S(2)}, u32[]{:S(2)}) collective-permute-start(bf16[4,80,512]{2,1,0:T(8,128)(2,1)S(1)} %get-tuple-element.31), channel_id=1, source_target_pairs={{0,1},{1,0},{2,3},{3,2},{4,5},{5,4},{6,7},{7,6},{8,9},{9,8},{10,11... | collective-permute-start | bytes 983048 | tf_op jit(solution)/shard_map/ppermute | solution.py:441
  49.5 1.2 %collective-permute-done.4 = bf16[4,80,512]{2,1,0:T(8,128)(2,1)S(1)} collective-permute-done((bf16[4,80,512]{2,1,0:T(8,128)(2,1)S(1)}, bf16[4,80,512]{2,1,0:T(8,128)(2,1)S(1)}, u32[]{:S(2)}, u32[]{:S(2)}) %collective-permute-start.4) | collective-permute-done | bytes 327712 | tf_op jit(solution)/shard_map/ppermute | solution.py:441
  50.8 0.1 fusion.15
  50.9 0.1 reduce-precision_convert_fusion
  51.0 0.3 concatenate.30
  51.3 0.1 add_convert_fusion
  51.4 0.4 concatenate.31
  51.8 4.4 %collective-permute-start.7 = (bf16[1,80,512]{2,1,0:T(8,128)(2,1)S(1)}, bf16[1,80,512]{2,1,0:T(8,128)(2,1)S(1)}, u32[]{:S(2)}, u32[]{:S(2)}) collective-permute-start(bf16[1,80,512]{2,1,0:T(8,128)(2,1)S(1)} %get-tuple-element.61), channel_id=1, source_target_pairs={{0,6},{1,7},{2,4},{3,5},{4,2},{5,3},{6,0},{7,1},{8,14},{9,15},{10,... | collective-permute-start | bytes 245768 | tf_op jit(solution)/shard_map/ppermute | solution.py:441
  56.2 1.2 %collective-permute-start.6 = (bf16[1,80,512]{2,1,0:T(8,128)(2,1)S(1)}, bf16[1,80,512]{2,1,0:T(8,128)(2,1)S(1)}, u32[]{:S(2)}, u32[]{:S(2)}) collective-permute-start(bf16[1,80,512]{2,1,0:T(8,128)(2,1)S(1)} %get-tuple-element.62), channel_id=1, source_target_pairs={{0,2},{1,5},{2,0},{3,7},{4,6},{5,1},{6,4},{7,3},{8,10},{9,13},{10,... | collective-permute-start | bytes 245768 | tf_op jit(solution)/shard_map/ppermute | solution.py:441
  57.3 0.0 collective-permute-start.5
  57.3 1.7 %collective-permute-done.7 = bf16[1,80,512]{2,1,0:T(8,128)(2,1)S(1)} collective-permute-done((bf16[1,80,512]{2,1,0:T(8,128)(2,1)S(1)}, bf16[1,80,512]{2,1,0:T(8,128)(2,1)S(1)}, u32[]{:S(2)}, u32[]{:S(2)}) %collective-permute-start.7) | collective-permute-done | bytes 81952 | tf_op jit(solution)/shard_map/ppermute | solution.py:441
  59.0 1.7 %collective-permute-done.6 = bf16[1,80,512]{2,1,0:T(8,128)(2,1)S(1)} collective-permute-done((bf16[1,80,512]{2,1,0:T(8,128)(2,1)S(1)}, bf16[1,80,512]{2,1,0:T(8,128)(2,1)S(1)}, u32[]{:S(2)}, u32[]{:S(2)}) %collective-permute-start.6) | collective-permute-done | bytes 81952 | tf_op jit(solution)/shard_map/ppermute | solution.py:441
  60.7 1.1 %collective-permute-done.5 = bf16[1,80,512]{2,1,0:T(8,128)(2,1)S(1)} collective-permute-done((bf16[1,80,512]{2,1,0:T(8,128)(2,1)S(1)}, bf16[1,80,512]{2,1,0:T(8,128)(2,1)S(1)}, u32[]{:S(2)}, u32[]{:S(2)}) %collective-permute-start.5) | collective-permute-done | bytes 81952 | tf_op jit(solution)/shard_map/ppermute | solution.py:441
  61.8 0.1 reduce-precision_convert_fusion.4
  61.9 0.1 add_convert_fusion.1
  62.0 0.2 concatenate.33
  62.2 2.0 %collective-permute-start.10 = (bf16[1,80,512]{2,1,0:T(8,128)(2,1)S(1)}, bf16[1,80,512]{2,1,0:T(8,128)(2,1)S(1)}, u32[]{:S(2)}, u32[]{:S(2)}) collective-permute-start(bf16[1,80,512]{2,1,0:T(8,128)(2,1)S(1)} %concatenate.33), channel_id=1, source_target_pairs={{0,24},{1,25},{2,26},{3,27},{4,28},{5,29},{6,30},{7,31},{8,16},{9,... | collective-permute-start | bytes 245768 | tf_op jit(solution)/shard_map/ppermute | solution.py:441
  64.2 0.2 concatenate.32
  64.3 1.2 %collective-permute-start.9 = (bf16[1,80,512]{2,1,0:T(8,128)(2,1)S(1)}, bf16[1,80,512]{2,1,0:T(8,128)(2,1)S(1)}, u32[]{:S(2)}, u32[]{:S(2)}) collective-permute-start(bf16[1,80,512]{2,1,0:T(8,128)(2,1)S(1)} %concatenate.33), channel_id=1, source_target_pairs={{0,16},{1,17},{2,18},{3,19},{4,20},{5,21},{6,22},{7,23},{8,24},{9,... | collective-permute-start | bytes 245768 | tf_op jit(solution)/shard_map/ppermute | solution.py:441
  65.5 1.3 %collective-permute-start.8 = (bf16[1,80,512]{2,1,0:T(8,128)(2,1)S(1)}, bf16[1,80,512]{2,1,0:T(8,128)(2,1)S(1)}, u32[]{:S(2)}, u32[]{:S(2)}) collective-permute-start(bf16[1,80,512]{2,1,0:T(8,128)(2,1)S(1)} %concatenate.33), channel_id=1, source_target_pairs={{0,8},{1,9},{2,10},{3,11},{4,12},{5,13},{6,14},{7,15},{8,0},{9,1},... | collective-permute-start | bytes 245768 | tf_op jit(solution)/shard_map/ppermute | solution.py:441
  66.8 1.7 %collective-permute-done.10 = bf16[1,80,512]{2,1,0:T(8,128)(2,1)S(1)} collective-permute-done((bf16[1,80,512]{2,1,0:T(8,128)(2,1)S(1)}, bf16[1,80,512]{2,1,0:T(8,128)(2,1)S(1)}, u32[]{:S(2)}, u32[]{:S(2)}) %collective-permute-start.10) | collective-permute-done | bytes 81952 | tf_op jit(solution)/shard_map/ppermute | solution.py:441
  68.6 3.1 %collective-permute-done.9 = bf16[1,80,512]{2,1,0:T(8,128)(2,1)S(1)} collective-permute-done((bf16[1,80,512]{2,1,0:T(8,128)(2,1)S(1)}, bf16[1,80,512]{2,1,0:T(8,128)(2,1)S(1)}, u32[]{:S(2)}, u32[]{:S(2)}) %collective-permute-start.9) | collective-permute-done | bytes 81952 | tf_op jit(solution)/shard_map/ppermute | solution.py:441
  71.7 0.0 collective-permute-done.8
  71.7 0.1 multiply_add_fusion
  71.8 0.1 divide_convert_fusion.refs_0_
  71.9 2.3 %collective-permute-start.11 = (bf16[1,64,512]{2,1,0:T(8,128)(2,1)S(1)}, bf16[1,64,512]{2,1,0:T(8,128)(2,1)S(1)}, u32[]{:S(2)}, u32[]{:S(2)}) collective-permute-start(bf16[1,64,512]{2,1,0:T(8,128)(2,1)S(1)} %divide_convert_fusion.refs_0_), channel_id=1, source_target_pairs={{0,4},{1,3},{2,6},{3,1},{4,0},{5,7},{6,2},{7,5},{8,12},{9,11},{10,... | collective-permute-start | bytes 196616 | tf_op jit(solution)/shard_map/ppermute | solution.py:441
  74.2 1.1 %collective-permute-start.12 = (bf16[1,64,512]{2,1,0:T(8,128)(2,1)S(1)}, bf16[1,64,512]{2,1,0:T(8,128)(2,1)S(1)}, u32[]{:S(2)}, u32[]{:S(2)}) collective-permute-start(bf16[1,64,512]{2,1,0:T(8,128)(2,1)S(1)} %divide_convert_fusion.refs_0_), channel_id=1, source_target_pairs={{0,2},{1,5},{2,0},{3,7},{4,6},{5,1},{6,4},{7,3},{8,10},{9,13},{10,... | collective-permute-start | bytes 196616 | tf_op jit(solution)/shard_map/ppermute | solution.py:441
  75.3 0.4 collective-permute-start.13
  75.7 0.0 collective-permute-start.14
  75.7 0.9 %collective-permute-done.11.refs_1_ = bf16[1,64,512]{2,1,0:T(8,128)(2,1)S(1)} collective-permute-done((bf16[1,64,512]{2,1,0:T(8,128)(2,1)S(1)}, bf16[1,64,512]{2,1,0:T(8,128)(2,1)S(1)}, u32[]{:S(2)}, u32[]{:S(2)}) %collective-permute-start.11) | collective-permute-done | bytes 65568 | tf_op jit(solution)/shard_map/ppermute | solution.py:441
  76.6 0.0 collective-permute-start.15
  76.6 2.3 %collective-permute-done.12.refs_2_ = bf16[1,64,512]{2,1,0:T(8,128)(2,1)S(1)} collective-permute-done((bf16[1,64,512]{2,1,0:T(8,128)(2,1)S(1)}, bf16[1,64,512]{2,1,0:T(8,128)(2,1)S(1)}, u32[]{:S(2)}, u32[]{:S(2)}) %collective-permute-start.12) | collective-permute-done | bytes 65568 | tf_op jit(solution)/shard_map/ppermute | solution.py:441
  78.9 0.0 collective-permute-start.16
  78.9 1.6 %collective-permute-done.13.refs_3_ = bf16[1,64,512]{2,1,0:T(8,128)(2,1)S(1)} collective-permute-done((bf16[1,64,512]{2,1,0:T(8,128)(2,1)S(1)}, bf16[1,64,512]{2,1,0:T(8,128)(2,1)S(1)}, u32[]{:S(2)}, u32[]{:S(2)}) %collective-permute-start.13) | collective-permute-done | bytes 65568 | tf_op jit(solution)/shard_map/ppermute | solution.py:441
  80.4 0.0 collective-permute-start.17
  80.4 0.0 collective-permute-done.14.refs_4_
  80.5 0.0 collective-permute-done.15.refs_5_
  80.5 0.0 collective-permute-done.16.refs_6_
  80.5 1.2 %collective-permute-done.17.refs_7_ = bf16[1,64,512]{2,1,0:T(8,128)(2,1)S(1)} collective-permute-done((bf16[1,64,512]{2,1,0:T(8,128)(2,1)S(1)}, bf16[1,64,512]{2,1,0:T(8,128)(2,1)S(1)}, u32[]{:S(2)}, u32[]{:S(2)}) %collective-permute-start.17) | collective-permute-done | bytes 65568 | tf_op jit(solution)/shard_map/ppermute | solution.py:441
  81.7 0.0 copy-done.9
  81.7 1.6 %shard_map.128 = f32[512,512]{1,0:T(8,128)} custom-call(bf16[1,64,512]{2,1,0:T(8,128)(2,1)S(1)} %divide_convert_fusion.refs_0_, bf16[1,64,512]{2,1,0:T(8,128)(2,1)S(1)} %collective-permute-done.11.refs_1_, bf16[1,64,512]{2,1,0:T(8,128)(2,1)S(1)} %collective-permute-done.12.refs_2_, bf16[1,64,512]{2,1,0:T(8,128)(2,1)S(1)} %collective-permute-done.13.refs_3_, ...), custom_call_target="tpu_custom_call" | custom-call | tf_op jit(solution)/shard_map/pallas_call | solution.py:42
  (38 shorter events, 0.2 us)
Async XLA Ops:
  0.6 4.3 %copy-start = (bf16[69,32,512]{2,1,0:T(8,128)(2,1)S(1)}, bf16[69,32,512]{2,1,0:T(8,128)(2,1)}, u32[]{:S(2)}) copy-start(bf16[69,32,512]{2,1,0:T(8,128)(2,1)} %x_ref.5) | copy-start | bytes 6782980
  0.6 8.6 %copy-start.1 = (bf16[512,1024]{1,0:T(8,128)(2,1)S(1)}, bf16[512,1024]{1,0:T(8,128)(2,1)}, u32[]{:S(2)}) copy-start(bf16[512,1024]{1,0:T(8,128)(2,1)} %kv_ref.1) | copy-start | bytes 3145732
  2.3 3.8 %collective-permute-start = (bf16[32,128]{1,0:T(8,128)(2,1)S(1)}, bf16[32,128]{1,0:T(8,128)(2,1)S(1)}, u32[]{:S(2)}, u32[]{:S(2)}) collective-permute-start(bf16[32,128]{1,0:T(8,128)(2,1)S(1)} %get-tuple-element.18), channel_id=1, source_target_pairs={{0,1},{1,2},{2,3},{3,0},{4,5},{5,6},{6,7},{7,4},{8,9},{9,10},{10,1... | collective-permute-start | bytes 24584 | tf_op jit(solution)/shard_map/ppermute | solution.py:391
  2.9 8.2 %copy-start.6 = (f32[512]{0:T(512)S(1)}, f32[512]{0:T(512)}, u32[]{:S(2)}) copy-start(f32[512]{0:T(512)} %param.17) | copy-start | bytes 6148
  2.9 8.2 %copy-start.10 = (f32[8]{0:T(128)S(1)}, f32[8]{0:T(128)}, u32[]{:S(2)}) copy-start(f32[8]{0:T(128)} %gain_ref.1) | copy-start | bytes 100
  2.9 3.4 %collective-permute-start.1 = (bf16[32,128]{1,0:T(8,128)(2,1)S(1)}, bf16[32,128]{1,0:T(8,128)(2,1)S(1)}, u32[]{:S(2)}, u32[]{:S(2)}) collective-permute-start(bf16[32,128]{1,0:T(8,128)(2,1)S(1)} %get-tuple-element.19), channel_id=1, source_target_pairs={{1,0},{2,1},{3,2},{0,3},{5,4},{6,5},{7,6},{4,7},{9,8},{10,9},{11,1... | collective-permute-start | bytes 24584 | tf_op jit(solution)/shard_map/ppermute | solution.py:392
  5.2 5.9 %copy-start.4 = (bf16[512,512]{1,0:T(8,128)(2,1)S(1)}, bf16[512,512]{1,0:T(8,128)(2,1)}, u32[]{:S(2)}) copy-start(bf16[512,512]{1,0:T(8,128)(2,1)} %qw_ref.1) | copy-start | bytes 1572868
  6.3 9.4 %collective-permute-start.2 = (bf16[80,512]{1,0:T(8,128)(2,1)S(1)}, bf16[80,512]{1,0:T(8,128)(2,1)S(1)}, u32[]{:S(2)}, u32[]{:S(2)}) collective-permute-start(bf16[80,512]{1,0:T(8,128)(2,1)S(1)} %get-tuple-element.64), channel_id=1, source_target_pairs={{0,4},{4,0},{8,12},{12,8},{16,20},{20,16},{24,28},{28,24},{1,5},{5... | collective-permute-start | bytes 245768 | tf_op jit(solution)/shard_map/ppermute | solution.py:405
  8.6 7.2 %collective-permute-start.3 = (bf16[80,512]{1,0:T(8,128)(2,1)S(1)}, bf16[80,512]{1,0:T(8,128)(2,1)S(1)}, u32[]{:S(2)}, u32[]{:S(2)}) collective-permute-start(bf16[80,512]{1,0:T(8,128)(2,1)S(1)} %get-tuple-element.63), channel_id=1, source_target_pairs={{4,8},{8,4},{12,16},{16,12},{20,24},{24,20},{5,9},{9,5},{13,17},{1... | collective-permute-start | bytes 245768 | tf_op jit(solution)/shard_map/ppermute | solution.py:406
  9.3 1.3 %copy-start.2 = (bf16[1104,512]{1,0:T(8,128)(2,1)S(1)}, bf16[1104,512]{1,0:T(8,128)(2,1)}, u32[]{:S(2)}) copy-start(bf16[1104,512]{1,0:T(8,128)(2,1)} %w_ref) | copy-start | bytes 3391492
  10.5 1.2 %copy-start.3 = (f32[512,512]{1,0:T(8,128)S(1)}, f32[512,512]{1,0:T(8,128)}, u32[]{:S(2)}) copy-start(f32[512,512]{1,0:T(8,128)} %latents_ref) | copy-start | bytes 3145732
  13.2 2.6 %copy-start.7 = (f32[512]{0:T(512)S(1)}, f32[512]{0:T(512)}, u32[]{:S(2)}) copy-start(f32[512]{0:T(512)} %param.13) | copy-start | bytes 6148
  13.2 2.6 %copy-start.8 = (f32[512]{0:T(512)S(1)}, f32[512]{0:T(512)}, u32[]{:S(2)}) copy-start(f32[512]{0:T(512)} %param.14) | copy-start | bytes 6148
  48.1 33.6 %copy-start.5 = (bf16[512,512]{1,0:T(8,128)(2,1)S(1)}, bf16[512,512]{1,0:T(8,128)(2,1)}, u32[]{:S(2)}) copy-start(bf16[512,512]{1,0:T(8,128)(2,1)} %refs_8_.1) | copy-start | bytes 1572868
  48.1 33.6 %copy-start.9 = (f32[512]{0:T(512)S(1)}, f32[512]{0:T(512)}, u32[]{:S(2)}) copy-start(f32[512]{0:T(512)} %param.21) | copy-start | bytes 6148
  48.1 2.6 %collective-permute-start.4 = (bf16[4,80,512]{2,1,0:T(8,128)(2,1)S(1)}, bf16[4,80,512]{2,1,0:T(8,128)(2,1)S(1)}, u32[]{:S(2)}, u32[]{:S(2)}) collective-permute-start(bf16[4,80,512]{2,1,0:T(8,128)(2,1)S(1)} %get-tuple-element.31), channel_id=1, source_target_pairs={{0,1},{1,0},{2,3},{3,2},{4,5},{5,4},{6,7},{7,6},{8,9},{9,8},{10,11... | collective-permute-start | bytes 983048 | tf_op jit(solution)/shard_map/ppermute | solution.py:441
  51.8 7.2 %collective-permute-start.7 = (bf16[1,80,512]{2,1,0:T(8,128)(2,1)S(1)}, bf16[1,80,512]{2,1,0:T(8,128)(2,1)S(1)}, u32[]{:S(2)}, u32[]{:S(2)}) collective-permute-start(bf16[1,80,512]{2,1,0:T(8,128)(2,1)S(1)} %get-tuple-element.61), channel_id=1, source_target_pairs={{0,6},{1,7},{2,4},{3,5},{4,2},{5,3},{6,0},{7,1},{8,14},{9,15},{10,... | collective-permute-start | bytes 245768 | tf_op jit(solution)/shard_map/ppermute | solution.py:441
  56.2 4.5 %collective-permute-start.6 = (bf16[1,80,512]{2,1,0:T(8,128)(2,1)S(1)}, bf16[1,80,512]{2,1,0:T(8,128)(2,1)S(1)}, u32[]{:S(2)}, u32[]{:S(2)}) collective-permute-start(bf16[1,80,512]{2,1,0:T(8,128)(2,1)S(1)} %get-tuple-element.62), channel_id=1, source_target_pairs={{0,2},{1,5},{2,0},{3,7},{4,6},{5,1},{6,4},{7,3},{8,10},{9,13},{10,... | collective-permute-start | bytes 245768 | tf_op jit(solution)/shard_map/ppermute | solution.py:441
  57.3 4.4 %collective-permute-start.5 = (bf16[1,80,512]{2,1,0:T(8,128)(2,1)S(1)}, bf16[1,80,512]{2,1,0:T(8,128)(2,1)S(1)}, u32[]{:S(2)}, u32[]{:S(2)}) collective-permute-start(bf16[1,80,512]{2,1,0:T(8,128)(2,1)S(1)} %get-tuple-element.60), channel_id=1, source_target_pairs={{0,4},{1,3},{2,6},{3,1},{4,0},{5,7},{6,2},{7,5},{8,12},{9,11},{10,... | collective-permute-start | bytes 245768 | tf_op jit(solution)/shard_map/ppermute | solution.py:441
  62.2 6.4 %collective-permute-start.10 = (bf16[1,80,512]{2,1,0:T(8,128)(2,1)S(1)}, bf16[1,80,512]{2,1,0:T(8,128)(2,1)S(1)}, u32[]{:S(2)}, u32[]{:S(2)}) collective-permute-start(bf16[1,80,512]{2,1,0:T(8,128)(2,1)S(1)} %concatenate.33), channel_id=1, source_target_pairs={{0,24},{1,25},{2,26},{3,27},{4,28},{5,29},{6,30},{7,31},{8,16},{9,... | collective-permute-start | bytes 245768 | tf_op jit(solution)/shard_map/ppermute | solution.py:441
  64.3 7.4 %collective-permute-start.9 = (bf16[1,80,512]{2,1,0:T(8,128)(2,1)S(1)}, bf16[1,80,512]{2,1,0:T(8,128)(2,1)S(1)}, u32[]{:S(2)}, u32[]{:S(2)}) collective-permute-start(bf16[1,80,512]{2,1,0:T(8,128)(2,1)S(1)} %concatenate.33), channel_id=1, source_target_pairs={{0,16},{1,17},{2,18},{3,19},{4,20},{5,21},{6,22},{7,23},{8,24},{9,... | collective-permute-start | bytes 245768 | tf_op jit(solution)/shard_map/ppermute | solution.py:441
  65.5 6.2 %collective-permute-start.8 = (bf16[1,80,512]{2,1,0:T(8,128)(2,1)S(1)}, bf16[1,80,512]{2,1,0:T(8,128)(2,1)S(1)}, u32[]{:S(2)}, u32[]{:S(2)}) collective-permute-start(bf16[1,80,512]{2,1,0:T(8,128)(2,1)S(1)} %concatenate.33), channel_id=1, source_target_pairs={{0,8},{1,9},{2,10},{3,11},{4,12},{5,13},{6,14},{7,15},{8,0},{9,1},... | collective-permute-start | bytes 245768 | tf_op jit(solution)/shard_map/ppermute | solution.py:441
  71.9 4.8 %collective-permute-start.11 = (bf16[1,64,512]{2,1,0:T(8,128)(2,1)S(1)}, bf16[1,64,512]{2,1,0:T(8,128)(2,1)S(1)}, u32[]{:S(2)}, u32[]{:S(2)}) collective-permute-start(bf16[1,64,512]{2,1,0:T(8,128)(2,1)S(1)} %divide_convert_fusion.refs_0_), channel_id=1, source_target_pairs={{0,4},{1,3},{2,6},{3,1},{4,0},{5,7},{6,2},{7,5},{8,12},{9,11},{10,... | collective-permute-start | bytes 196616 | tf_op jit(solution)/shard_map/ppermute | solution.py:441
  74.2 4.7 %collective-permute-start.12 = (bf16[1,64,512]{2,1,0:T(8,128)(2,1)S(1)}, bf16[1,64,512]{2,1,0:T(8,128)(2,1)S(1)}, u32[]{:S(2)}, u32[]{:S(2)}) collective-permute-start(bf16[1,64,512]{2,1,0:T(8,128)(2,1)S(1)} %divide_convert_fusion.refs_0_), channel_id=1, source_target_pairs={{0,2},{1,5},{2,0},{3,7},{4,6},{5,1},{6,4},{7,3},{8,10},{9,13},{10,... | collective-permute-start | bytes 196616 | tf_op jit(solution)/shard_map/ppermute | solution.py:441
  75.3 5.2 %collective-permute-start.13 = (bf16[1,64,512]{2,1,0:T(8,128)(2,1)S(1)}, bf16[1,64,512]{2,1,0:T(8,128)(2,1)S(1)}, u32[]{:S(2)}, u32[]{:S(2)}) collective-permute-start(bf16[1,64,512]{2,1,0:T(8,128)(2,1)S(1)} %divide_convert_fusion.refs_0_), channel_id=1, source_target_pairs={{0,6},{1,7},{2,4},{3,5},{4,2},{5,3},{6,0},{7,1},{8,14},{9,15},{10,... | collective-permute-start | bytes 196616 | tf_op jit(solution)/shard_map/ppermute | solution.py:441
  75.7 4.7 %collective-permute-start.14 = (bf16[1,64,512]{2,1,0:T(8,128)(2,1)S(1)}, bf16[1,64,512]{2,1,0:T(8,128)(2,1)S(1)}, u32[]{:S(2)}, u32[]{:S(2)}) collective-permute-start(bf16[1,64,512]{2,1,0:T(8,128)(2,1)S(1)} %divide_convert_fusion.refs_0_), channel_id=1, source_target_pairs={{0,1},{1,0},{2,3},{3,2},{4,5},{5,4},{6,7},{7,6},{8,9},{9,8},{10,11... | collective-permute-start | bytes 196616 | tf_op jit(solution)/shard_map/ppermute | solution.py:441
  76.6 3.8 %collective-permute-start.15 = (bf16[1,64,512]{2,1,0:T(8,128)(2,1)S(1)}, bf16[1,64,512]{2,1,0:T(8,128)(2,1)S(1)}, u32[]{:S(2)}, u32[]{:S(2)}) collective-permute-start(bf16[1,64,512]{2,1,0:T(8,128)(2,1)S(1)} %collective-permute-done.11.refs_1_), channel_id=1, source_target_pairs={{0,1},{1,0},{2,3},{3,2},{4,5},{5,4},{6,7},{7,6},{8,9},{9,8},{10,11... | collective-permute-start | bytes 196616 | tf_op jit(solution)/shard_map/ppermute | solution.py:441
  78.9 1.6 %collective-permute-start.16 = (bf16[1,64,512]{2,1,0:T(8,128)(2,1)S(1)}, bf16[1,64,512]{2,1,0:T(8,128)(2,1)S(1)}, u32[]{:S(2)}, u32[]{:S(2)}) collective-permute-start(bf16[1,64,512]{2,1,0:T(8,128)(2,1)S(1)} %collective-permute-done.12.refs_2_), channel_id=1, source_target_pairs={{0,1},{1,0},{2,3},{3,2},{4,5},{5,4},{6,7},{7,6},{8,9},{9,8},{10,11... | collective-permute-start | bytes 196616 | tf_op jit(solution)/shard_map/ppermute | solution.py:441
  80.4 1.3 %collective-permute-start.17 = (bf16[1,64,512]{2,1,0:T(8,128)(2,1)S(1)}, bf16[1,64,512]{2,1,0:T(8,128)(2,1)S(1)}, u32[]{:S(2)}, u32[]{:S(2)}) collective-permute-start(bf16[1,64,512]{2,1,0:T(8,128)(2,1)S(1)} %collective-permute-done.13.refs_3_), channel_id=1, source_target_pairs={{0,1},{1,0},{2,3},{3,2},{4,5},{5,4},{6,7},{7,6},{8,9},{9,8},{10,11... | collective-permute-start | bytes 196616 | tf_op jit(solution)/shard_map/ppermute | solution.py:441
